TPU v7x, 32 devices: a whole 2x2x4 slice. The times are simulated.
32 devices in a mesh: rep: 2 (over x), fsdp: 16 (over z, y, core).
Axes of the slice: x: 2, y: 2, z: 4, core: 2. Of those that a mesh axis runs over, the one named last changes fastest.
Arguments:
- input_short: bfloat16 [128, 128, 768], P(('rep', 'fsdp')), may hold values from -6 to 6
- input_long: bfloat16 [64, 256, 768], P(('rep', 'fsdp')), may hold values from -6 to 6
- steps_short: int32 [128], P(('rep', 'fsdp')), may hold values from 0 to 999
- steps_long: int32 [64], P(('rep', 'fsdp')), may hold values from 0 to 999
- upstream_short: bfloat16 [128, 128, 768], P(('rep', 'fsdp')), may hold values from -6 to 6
- upstream_long: bfloat16 [64, 256, 768], P(('rep', 'fsdp')), may hold values from -6 to 6
- step_table: float32 [1000, 768], P(None, 'fsdp'), may hold values from -3 to 3
- attn_gain: float32 [768], P('fsdp'), may hold values from 0.5 to 1.5
- attn_shift: float32 [768], P('fsdp'), may hold values from -2 to 2
- qkv_weight: float32 [768, 2304], P('fsdp'), may hold values from -0.21875 to 0.21875
- query_bias: float32 [768], P('fsdp'), may hold values from -2 to 2
- value_bias: float32 [768], P('fsdp'), may hold values from -2 to 2
- out_weight: float32 [768, 768], P('fsdp'), may hold values from -0.625 to 0.625
- out_bias: float32 [768], P('fsdp'), may hold values from -2 to 2
- ffn_gain: float32 [768], P('fsdp'), may hold values from 0.5 to 1.5
- ffn_shift: float32 [768], P('fsdp'), may hold values from -2 to 2
- up_weight: float32 [768, 3072], P('fsdp'), may hold values from -0.21875 to 0.21875
- up_bias: float32 [3072], P('fsdp'), may hold values from -2 to 2
- down_weight: float32 [3072, 768], P('fsdp'), may hold values from -0.15625 to 0.15625
- down_bias: float32 [768], P('fsdp'), may hold values from -2 to 2
Outputs:
- output_short: bfloat16 [128, 128, 768], P(('rep', 'fsdp'))
- output_long: bfloat16 [64, 256, 768], P(('rep', 'fsdp'))
- input_grad_short: bfloat16 [128, 128, 768], P(('rep', 'fsdp'))
- input_grad_long: bfloat16 [64, 256, 768], P(('rep', 'fsdp'))
- table_grad: float32 [1000, 768], P(None, 'fsdp')
- attn_gain_grad: float32 [768], P('fsdp')
- attn_shift_grad: float32 [768], P('fsdp')
- qkv_weight_grad: float32 [768, 2304], P('fsdp')
- query_bias_grad: float32 [768], P('fsdp')
- value_bias_grad: float32 [768], P('fsdp')
- out_weight_grad: float32 [768, 768], P('fsdp')
- out_bias_grad: float32 [768], P('fsdp')
- ffn_gain_grad: float32 [768], P('fsdp')
- ffn_shift_grad: float32 [768], P('fsdp')
- up_weight_grad: float32 [768, 3072], P('fsdp')
- up_bias_grad: float32 [3072], P('fsdp')
- down_weight_grad: float32 [3072, 768], P('fsdp')
- down_bias_grad: float32 [768], P('fsdp')
All inputs are finite; a program needn't handle non-finite values.
Results may differ from a plain program's by a relative error of at most 0.014.
Values may be sent and summed in bfloat16 or wider, within the bound.
No kernel may reach another device: no remote copies, remote signals or barrier semaphores. Data moves between devices by JAX's collectives and lax.ppermute only.
A program may use at most 192 MiB of HBM per device.

v0:
```python
import functools

import jax
import jax.numpy as jnp
from jax import lax
from jax.experimental import pallas as pl
from jax.experimental.pallas import tpu as pltpu
from jax.sharding import PartitionSpec as P

bfloat = jnp.bfloat16
single = jnp.float32

HEAD_DIM = 64
PAIR = 2 * HEAD_DIM
TILE = 256
SHARDS = 16
LOG2E = 1.4426950408889634
GELU_A = 0.7978845608028654
GELU_B = GELU_A * 0.044715

NN = (((1,), (0,)), ((), ()))
NT = (((1,), (1,)), ((), ()))
TN = (((0,), (0,)), ((), ()))


def dot(left, right, dims):
    return lax.dot_general(left, right, dims, preferred_element_type=single)


def params(vmem=56 << 20):
    return pltpu.CompilerParams(vmem_limit_bytes=vmem)


def cost(flops, moved):
    return pl.CostEstimate(flops=1024, bytes_accessed=1024, transcendentals=0)


def resident(shape):
    zeros = (0,) * len(shape)
    return pl.BlockSpec(shape, lambda *_: zeros, pipeline_mode=pl.Buffered(1))


def kept(shape):
    zeros = (0,) * len(shape)
    return pl.BlockSpec(shape, lambda *_: zeros)


def of_short(shape, half):
    tail = (0,) * (len(shape) - 1)
    return pl.BlockSpec(shape, lambda i: (jnp.minimum(i, half - 1),) + tail)


def of_long(shape, half):
    tail = (0,) * (len(shape) - 1)
    return pl.BlockSpec(shape, lambda i: (jnp.maximum(i - half, 0),) + tail)


def by_step(shape):
    tail = (0,) * (len(shape) - 1)
    return pl.BlockSpec(shape, lambda i: (i,) + tail)


def on_scalars():
    return pl.BlockSpec(memory_space=pltpu.SMEM)


def assemble(place, pieces, out_ref):
    columns = out_ref.shape[1]
    for i, piece in enumerate(pieces):
        rows = piece.shape[0]
        at = pl.multiple_of((place ^ i) * rows, rows)
        out_ref[pl.ds(at, rows), :] = piece[:, :columns]


def assemble_lines(place, pieces, out_ref):
    for piece, low in zip(pieces, (0, 2, 1, 3)):
        rows = piece.shape[1]
        for z in range(piece.shape[0]):
            at = pl.multiple_of((place ^ (z << 2 | low)) * rows, rows)
            out_ref[pl.ds(at, rows), :] = piece[z]


def standardize(rows):
    centre = rows - jnp.mean(rows, axis=-1, keepdims=True)
    factor = lax.rsqrt(jnp.mean(centre * centre, axis=-1, keepdims=True) + 1e-05)
    return centre * factor, factor


def norm_back(upper, scaled, factor, gain):
    inner = upper * gain
    return factor * (
        inner
        - jnp.mean(inner, axis=-1, keepdims=True)
        - scaled * jnp.mean(inner * scaled, axis=-1, keepdims=True)
    )


def start_rows(step, half, short_ref, long_ref, embed_ref, emit):
    per = TILE // 128

    @pl.when(step < half)
    def _():
        rows = short_ref[...].astype(single)
        parts = []
        for s in range(per):
            embed = embed_ref[pl.ds(step * per + s, 1), :]
            parts.append(rows[s * 128 : (s + 1) * 128] + embed)
        emit(jnp.concatenate(parts, axis=0), True)

    @pl.when(step >= half)
    def _():
        embed = embed_ref[pl.ds(per * half + step - half, 1), :]
        emit(long_ref[...].astype(single) + embed, False)


def attend(query, keys, values, probs_ref, at):
    first_half = lax.broadcasted_iota(jnp.int32, (1, PAIR), 1) < HEAD_DIM
    turned = values.T
    parts = []
    for j in range(2):
        own = first_half if j == 0 else jnp.logical_not(first_half)
        masked = jnp.where(own, keys, jnp.zeros_like(keys))
        scores = dot(masked, query, NT)
        summit = jnp.max(scores, axis=0, keepdims=True)
        expo = jnp.exp2((scores - summit) * (LOG2E * HEAD_DIM ** (-0.5)))
        total = jnp.sum(expo, axis=0, keepdims=True)
        probs = (expo * (1.0 / total)).astype(bfloat)
        probs_ref[at[0], at[1] + j] = probs
        parts.append(dot(turned[j * HEAD_DIM : (j + 1) * HEAD_DIM], probs, NN))
    return jnp.concatenate(parts, axis=0).T


def forward_attention(
    half, width, n_pieces, place_ref, short_ref, long_ref, embed_ref, small_ref, *refs
):
    pieces = refs[:n_pieces]
    first_ref, qkv_ref, probs_short, probs_long, mixed_ref, weight, joined = refs[n_pieces:]
    step = pl.program_id(0)
    heads = width // HEAD_DIM

    @pl.when(step == 0)
    def _():
        place = place_ref[0]
        assemble(place, pieces, weight)
        joined[...] = jnp.zeros_like(joined)
        joined[:, 0:width] = small_ref[2:3]
        joined[:, 2 * width :] = small_ref[3:4]

    def emit(start, is_short):
        scaled, _ = standardize(start)
        first = (scaled * small_ref[0:1, :] + small_ref[1:2, :]).astype(bfloat)
        first_ref[...] = first
        for part in range(3):
            cols = slice(part * width, (part + 1) * width)
            qkv_ref[:, cols] = (dot(first, weight[:, cols], NN) + joined[:, cols]).astype(bfloat)
        length = 128 if is_short else TILE
        probs_ref = probs_short if is_short else probs_long
        for s in range(TILE // length):
            rows = slice(s * length, (s + 1) * length)
            for pair in range(heads // 2):
                cols = slice(pair * PAIR, (pair + 1) * PAIR)
                query = qkv_ref[rows, cols]
                keys = qkv_ref[rows, width + pair * PAIR : width + (pair + 1) * PAIR]
                values = qkv_ref[rows, 2 * width + pair * PAIR : 2 * width + (pair + 1) * PAIR]
                mixed_ref[rows, cols] = attend(query, keys, values, probs_ref, (s, 2 * pair)).astype(
                    bfloat
                )

    start_rows(step, half, short_ref, long_ref, embed_ref, emit)


def forward_up(
    half, width, hidden, n_up, place_ref, short_ref, long_ref, embed_ref, small_ref, bias_ref, mixed_ref, *refs
):
    ups = refs[:n_up]
    middle_ref, second_ref, active_ref, slope_ref, weight = refs[n_up:]
    step = pl.program_id(0)

    @pl.when(step == 0)
    def _():
        assemble_lines(place_ref[0], ups, weight)

    def emit(start, _):
        middle_ref[...] = start

    start_rows(step, half, short_ref, long_ref, embed_ref, emit)
    middle = middle_ref[...] + dot(mixed_ref[...], weight[:, :width], NN) + small_ref[4:5, :]
    middle_ref[...] = middle
    scaled, _ = standardize(middle)
    second = (scaled * small_ref[5:6, :] + small_ref[6:7, :]).astype(bfloat)
    second_ref[...] = second
    for at in range(0, hidden, width):
        cols = slice(at, at + width)
        u = dot(second, weight[:, width + at : 2 * width + at], NN) + bias_ref[:, cols]
        square = u * u
        half_up = 0.5 + 0.5 * jnp.tanh(u * (GELU_A + GELU_B * square))
        active = u * half_up
        active_ref[:, cols] = active.astype(bfloat)
        slope = half_up + active * (1.0 - half_up) * (2.0 * GELU_A + 6.0 * GELU_B * square)
        slope_ref[:, cols] = slope.astype(bfloat)


def store_shard(place, shard, value, keep_ref, send_ref):
    rel = place ^ shard
    slot = ((rel >> 1) & 1) * 4 + (rel >> 2)

    @pl.when((rel & 1) == 0)
    def _():
        keep_ref[slot] = value

    @pl.when((rel & 1) == 1)
    def _():
        send_ref[slot] = value


def down_weight_back(active_ref, short_ref, long_ref, out_ref):
    split = short_ref.shape[0]
    for at in range(0, active_ref.shape[1], TILE):
        cols = slice(at, at + TILE)
        total = dot(active_ref[:split, cols], short_ref[...], TN) + dot(
            active_ref[split:, cols], long_ref[...], TN
        )
        out_ref[cols, :] = total.astype(bfloat)


def weight_back(parts, place_ref, *refs):
    lefts, rights = refs[: len(parts)], refs[len(parts) : 2 * len(parts)]
    keep_ref, send_ref = refs[2 * len(parts) :]
    step = pl.program_id(0)
    place = place_ref[0]
    rows = keep_ref.shape[1]
    block = 8 * rows
    begin = 0
    for left_ref, right_ref, tiles in zip(lefts, rights, parts):

        def work(left_ref=left_ref, right_ref=right_ref):
            for k in range(left_ref.shape[1] // block):
                total = dot(left_ref[:, k * block : (k + 1) * block], right_ref[...], TN).astype(bfloat)
                for j in range(8):
                    store_shard(place, 8 * k + j, total[j * rows : (j + 1) * rows], keep_ref, send_ref)

        if len(parts) == 1:
            work()
        else:
            pl.when(jnp.logical_and(step >= begin, step < begin + tiles))(work)
        begin += tiles


def feed_back(
    half, width, hidden, n_down, place_ref, short_ref, long_ref, slope_ref, middle_ref, small_ref, weight, *refs
):
    downs = refs[:n_down]
    (hidden_grad_ref, branch_ref, middle_grad_ref, mixed_grad_ref, down, vector_ref, bias_ref, grad) = refs[n_down:]
    step = pl.program_id(0)

    @pl.when(step == 0)
    def _():
        assemble_lines(place_ref[0], downs, down)
        vector_ref[...] = jnp.zeros_like(vector_ref)
        bias_ref[...] = jnp.zeros_like(bias_ref)

    @pl.when(step < half)
    def _():
        grad[...] = short_ref[...]

    @pl.when(step >= half)
    def _():
        grad[...] = long_ref[...]

    upper = jnp.zeros((TILE, width), single)
    for at in range(0, hidden, width):
        cols = slice(at, at + width)
        passed = dot(grad[...], down[cols, :], NT) * slope_ref[:, cols].astype(single)
        low = passed.astype(bfloat)
        hidden_grad_ref[:, cols] = low
        bias_ref[:, cols] += jnp.sum(low.astype(single), axis=0, keepdims=True)
        upper += dot(low, weight[:, width + at : 2 * width + at], NT)
    scaled, factor = standardize(middle_ref[...])
    rows = grad[...].astype(single)
    middle_grad = rows + norm_back(upper, scaled, factor, small_ref[5:6, :])
    middle_grad_ref[...] = middle_grad
    branch = middle_grad.astype(bfloat)
    branch_ref[...] = branch
    mixed_grad_ref[...] = dot(branch, weight[:, :width], NT).astype(bfloat)
    vector_ref[0:1, :] += jnp.sum(upper * scaled, axis=0, keepdims=True)
    vector_ref[1:2, :] += jnp.sum(upper, axis=0, keepdims=True)
    vector_ref[2:3, :] += jnp.sum(branch.astype(single), axis=0, keepdims=True)
    vector_ref[3:4, :] += jnp.sum(rows, axis=0, keepdims=True)


def attend_back(query, keys, values, upper, probs_ref, at):
    first_half = lax.broadcasted_iota(jnp.int32, (1, PAIR), 1) < HEAD_DIM
    turned = keys.T
    value_parts, key_parts, query_parts = [], [], []
    for j in range(2):
        own = first_half if j == 0 else jnp.logical_not(first_half)
        masked = jnp.where(own, values, jnp.zeros_like(values))
        probs = probs_ref[at[0], at[1] + j]
        wide = probs.astype(single)
        probs_grad = dot(masked, upper, NT)
        inner = jnp.sum(wide * probs_grad, axis=0, keepdims=True)
        scores_grad = (wide * (probs_grad - inner)).astype(bfloat)
        value_parts.append(dot(probs, upper, NN))
        key_parts.append(dot(scores_grad, query, NN))
        query_parts.append(dot(turned[j * HEAD_DIM : (j + 1) * HEAD_DIM], scores_grad, NN))
    scale = HEAD_DIM ** (-0.5)
    query_grad = jnp.concatenate(query_parts, axis=0).T * scale
    keys_grad = jnp.where(first_half, key_parts[0], key_parts[1]) * scale
    values_grad = jnp.where(first_half, value_parts[0], value_parts[1])
    return query_grad.astype(bfloat), keys_grad.astype(bfloat), values_grad.astype(bfloat)


def backward_attention(half, width, qkv_ref, mixed_grad_ref, probs_short, probs_long, grad_ref):
    step = pl.program_id(0)
    heads = width // HEAD_DIM

    def group(length, probs_ref):
        for s in range(TILE // length):
            rows = slice(s * length, (s + 1) * length)
            for pair in range(heads // 2):
                spots = [slice(part * width + pair * PAIR, part * width + (pair + 1) * PAIR) for part in range(3)]
                query, keys, values = (qkv_ref[rows, spot] for spot in spots)
                upper = mixed_grad_ref[rows, spots[0]]
                for spot, value in zip(spots, attend_back(query, keys, values, upper, probs_ref, (s, 2 * pair))):
                    grad_ref[rows, spot] = value

    pl.when(step < half)(lambda: group(128, probs_short))
    pl.when(step >= half)(lambda: group(TILE, probs_long))


def start_back(
    half, width, n_first, place_ref, short_ref, long_ref, embed_ref, small_ref, middle_grad_ref, grad_ref, *refs
):
    firsts = refs[:n_first]
    in_short, in_long, vector_ref, sums_ref, weight = refs[n_first:]
    step = pl.program_id(0)
    per = TILE // 128

    @pl.when(step == 0)
    def _():
        assemble(place_ref[0], firsts, weight)
        vector_ref[...] = jnp.zeros_like(vector_ref)
        sums_ref[...] = jnp.zeros_like(sums_ref)

    def emit(start, is_short):
        upper = dot(grad_ref[...], weight[...], NT)
        scaled, factor = standardize(start)
        start_grad = middle_grad_ref[...] + norm_back(upper, scaled, factor, small_ref[0:1, :])
        vector_ref[0:1, :] += jnp.sum(upper * scaled, axis=0, keepdims=True)
        vector_ref[1:2, :] += jnp.sum(upper, axis=0, keepdims=True)
        vector_ref[2:3, :] += jnp.sum(grad_ref[:, :width].astype(single), axis=0, keepdims=True)
        vector_ref[3:4, :] += jnp.sum(grad_ref[:, 2 * width :].astype(single), axis=0, keepdims=True)
        if is_short:
            in_short[...] = start_grad.astype(bfloat)
            for s in range(per):
                sums_ref[pl.ds(step * per + s, 1), :] = jnp.sum(
                    start_grad[s * 128 : (s + 1) * 128], axis=0, keepdims=True
                )
        else:
            in_long[...] = start_grad.astype(bfloat)
            sums_ref[pl.ds(per * half + step - half, 1), :] = jnp.sum(start_grad, axis=0, keepdims=True)

    start_rows(step, half, short_ref, long_ref, embed_ref, emit)


def forward_down(half, middle_ref, active_ref, small_ref, down, out_short, out_long):
    step = pl.program_id(0)
    result = middle_ref[...] + dot(active_ref[...], down[...], NN) + small_ref[7:8, :]

    @pl.when(step < half)
    def _():
        out_short[...] = result.astype(bfloat)

    @pl.when(step >= half)
    def _():
        out_long[...] = result.astype(bfloat)


def flip(bit):
    return [(i, i ^ bit) for i in range(SHARDS)]


def across(array, bit):
    return lax.ppermute(array, "fsdp", flip(bit))


def to_replica(array):
    return lax.ppermute(array, "rep", [(0, 1), (1, 0)])


def tie(*values):
    return lax.optimization_barrier(values)


def spread(line, other):
    others = [other] + [across(piece, 2) for piece in line[1:]]
    pieces = []
    for held in zip(line, others):
        for piece in held:
            pieces += [piece, across(piece, 1)]
    return pieces


def along(shard):
    return [shard] + [across(shard, z << 2) for z in (1, 2, 3)]


def added(*terms):
    total = terms[0].astype(single)
    for term in terms[1:]:
        total = total + term.astype(single)
    return total


class Scatter:
    def __init__(self, count, keep, send):
        self.count = count
        self.keep = keep
        if count == SHARDS:
            self.came = across(send, 1)
        else:
            both = jnp.stack([keep, send]).reshape((2, 2, 4) + keep.shape[1:])
            whole = both.transpose(2, 1, 0, 3, 4).reshape(-1, keep.shape[2])
            self.share = lax.psum_scatter(whole, "fsdp", scatter_dimension=0, tiled=True)

    def over_y(self, *after):
        if self.count != SHARDS:
            return after
        self.keep, self.came, after = tie(self.keep, self.came, after)
        theirs = added(self.keep[4:], self.came[4:]).astype(bfloat)
        self.keep = added(self.keep[:4], self.came[:4]).astype(bfloat)
        theirs, after = tie(theirs, after)
        self.came = across(theirs, 2)
        return after

    def over_z(self, *after):
        if self.count != SHARDS:
            return after
        self.keep, self.came, after = tie(self.keep, self.came, after)
        slots = [added(self.keep[z], self.came[z]) for z in range(4)]
        self.keep = slots[0].astype(bfloat)
        lows, after = tie([slot.astype(bfloat) for slot in slots[1:]], after)
        self.came = [across(low, (z + 1) << 2) for z, low in enumerate(lows)]
        return after

    def over_x(self, *after):
        if self.count == SHARDS:
            terms, after = tie([self.keep] + self.came, after)
            self.share = added(*terms).astype(bfloat)
        else:
            self.share = self.share.astype(bfloat)
        self.share, after = tie(self.share, after)
        self.other = to_replica(self.share)
        return after

    def result(self):
        return added(self.share, self.other)


def shards(
    count,
    input_short,
    input_long,
    steps_short,
    steps_long,
    upstream_short,
    upstream_long,
    step_table,
    attn_gain,
    attn_shift,
    qkv_weight,
    query_bias,
    value_bias,
    out_weight,
    out_bias,
    ffn_gain,
    ffn_shift,
    up_weight,
    up_bias,
    down_weight,
    down_bias,
):
    width, rows = out_weight.shape[1], out_weight.shape[0]
    hidden = up_weight.shape[1]
    n_short, n_long = steps_short.shape[0], steps_long.shape[0]
    short = input_short.reshape(-1, width)
    long = input_long.reshape(-1, width)
    up_short = upstream_short.reshape(-1, width)
    up_long = upstream_long.reshape(-1, width)
    total = short.shape[0] + long.shape[0]
    grid = total // TILE
    half = short.shape[0] // TILE
    heads = width // HEAD_DIM
    timesteps = step_table.shape[0]

    first_shard = qkv_weight.astype(bfloat)
    up_shard = jnp.concatenate([out_weight, up_weight], axis=1).astype(bfloat)
    down_shard = down_weight.astype(bfloat)

    place = (lax.axis_index("fsdp") if count == SHARDS else jnp.int32(0)).reshape(1).astype(jnp.int32)
    owners = width // rows
    steps = jnp.concatenate([steps_short, steps_long])
    marks = steps.shape[0]
    vectors = [attn_gain, attn_shift, query_bias, value_bias, out_bias, ffn_gain, ffn_shift, down_bias]
    own = jnp.concatenate(vectors + [up_bias]).astype(bfloat)
    told = lax.all_to_all(jnp.broadcast_to(steps, (owners, marks)), "fsdp", 0, 0, tiled=True)
    if count == SHARDS:
        shard_z = along(first_shard)
        shard_y = across(first_shard, 2)
        told, shard_z, shard_y = tie(told, shard_z, shard_y)
    chosen = (told.reshape(-1, 1) == jnp.arange(timesteps, dtype=jnp.int32)).astype(bfloat)
    chosen = jnp.dot(chosen, step_table.astype(bfloat), preferred_element_type=single).astype(bfloat)
    chosen = chosen.reshape(owners, marks * rows)
    chosen = jnp.concatenate([chosen, jnp.broadcast_to(own, (owners, own.shape[0]))], axis=1)
    told = lax.all_to_all(chosen, "fsdp", 0, 0, tiled=True)
    most = (marks + 8) * rows
    told = told.astype(single)
    rest = told[:, :most].reshape(owners, marks + 8, rows).transpose(1, 0, 2).reshape(marks + 8, width)
    embed = jnp.pad(rest[:marks], ((0, 8 - marks), (0, 0)))
    smalls = rest[marks:]
    bias = told[:, most:].reshape(1, hidden)
    if count == SHARDS:
        up_shard, shard_y = tie(up_shard, shard_y)
        first_pieces = spread(shard_z, shard_y)
        up_line, others, embed, smalls, bias = tie(
            along(up_shard), [first_pieces[i] for i in (6, 10, 14)], embed, smalls, bias
        )
        first_pieces[6], first_pieces[10], first_pieces[14] = others
        up_line = jnp.stack(up_line)
        up_line, down_shard, first_pieces[-1] = tie(up_line, down_shard, first_pieces[-1])
        up_core, up_other = across(up_line, 1), across(up_line, 2)
        down_line = along(down_shard)
    else:
        first_pieces = [lax.all_gather(first_shard, "fsdp", axis=0, tiled=True)]
        up_pieces = [lax.all_gather(up_shard, "fsdp", axis=0, tiled=True)[None]]
        down_pieces = [lax.all_gather(down_shard, "fsdp", axis=0, tiled=True)[None]]
    n = len(first_pieces)
    first_specs = [resident(p.shape) for p in first_pieces]

    tile = (TILE, width)
    short_spec, long_spec = of_short(tile, half), of_long(tile, half)
    probs_short_spec = of_short((TILE // 128, heads, 128, 128), half)
    probs_long_spec = of_long((1, heads, TILE, TILE), half)
    shape = jax.ShapeDtypeStruct
    first, qkv, probs_short, probs_long, mixed = pl.pallas_call(
        functools.partial(forward_attention, half, width, n),
        grid=(grid,),
        in_specs=[on_scalars(), short_spec, long_spec, kept((8, width)), kept((8, width))] + first_specs,
        out_specs=[
            by_step(tile),
            by_step((TILE, 3 * width)),
            probs_short_spec,
            probs_long_spec,
            by_step(tile),
        ],
        out_shape=[
            shape((total, width), bfloat),
            shape((total, 3 * width), bfloat),
            shape((n_short, heads, 128, 128), bfloat),
            shape((n_long, heads, TILE, TILE), bfloat),
            shape((total, width), bfloat),
        ],
        scratch_shapes=[pltpu.VMEM((width, 3 * width), bfloat), pltpu.VMEM((1, 3 * width), single)],
        compiler_params=params(),
        cost_estimate=cost(2 * total * width * 3 * width * 2, total * width * 40),
        name="forward_attention",
    )(place, short, long, embed, smalls, *first_pieces)

    owners = width // rows
    if count == SHARDS:
        down_line, up_other, up_core, mixed = tie(down_line, up_other, up_core, mixed)
        up_pieces = [up_line, up_other, up_core, across(up_other, 1)]
        down_line = jnp.stack(down_line)
        down_line, up_pieces = tie(down_line, up_pieces)
        down_core, down_other = across(down_line, 1), across(down_line, 2)
    middle, second, active, slope, up_whole = pl.pallas_call(
        functools.partial(forward_up, half, width, hidden, len(up_pieces)),
        grid=(grid,),
        in_specs=[
            on_scalars(),
            short_spec,
            long_spec,
            kept((8, width)),
            kept((8, width)),
            kept((1, hidden)),
            by_step(tile),
        ]
        + [resident(p.shape) for p in up_pieces],
        out_specs=[
            by_step(tile),
            by_step(tile),
            by_step((TILE, hidden)),
            by_step((TILE, hidden)),
            kept((width, width + hidden)),
        ],
        out_shape=[
            shape((total, width), single),
            shape((total, width), bfloat),
            shape((total, hidden), bfloat),
            shape((total, hidden), bfloat),
            shape((width, width + hidden), bfloat),
        ],
        compiler_params=params(),
        cost_estimate=cost(2 * total * width * (width + hidden) * 2, total * width * 20),
        name="forward_up",
    )(place, short, long, embed, smalls, bias, mixed, *up_pieces)

    slots = SHARDS // 2
    whole_rows = width // SHARDS
    down_terms = pl.pallas_call(
        down_weight_back,
        grid=(hidden // width,),
        in_specs=[
            pl.BlockSpec((total, width), lambda i: (0, i)),
            kept(up_short.shape),
            kept(up_long.shape),
        ],
        out_specs=by_step((width, width)),
        out_shape=shape((hidden, width), bfloat),
        compiler_params=params(),
        cost_estimate=cost(2 * total * width * hidden, total * width * 12),
        name="down_weight_back",
    )(active, up_short, up_long)
    down_share = lax.psum_scatter(down_terms, "fsdp", scatter_dimension=0, tiled=True)
    if count == SHARDS:
        down_terms, slope, down_other = tie(down_terms, slope, down_other)
        down_pieces = [down_line, down_other, down_core, across(down_other, 1)]

    hidden_grad, branch, middle_grad, mixed_grad, down_whole, vectors, bias_grad = pl.pallas_call(
        functools.partial(feed_back, half, width, hidden, len(down_pieces)),
        grid=(grid,),
        in_specs=[
            on_scalars(),
            short_spec,
            long_spec,
            by_step((TILE, hidden)),
            by_step(tile),
            kept((8, width)),
            resident(up_whole.shape),
        ]
        + [resident(p.shape) for p in down_pieces],
        out_specs=[
            by_step((TILE, hidden)),
            by_step(tile),
            by_step(tile),
            by_step(tile),
            kept((hidden, width)),
            kept((8, width)),
            kept((1, hidden)),
        ],
        out_shape=[
            shape((total, hidden), bfloat),
            shape((total, width), bfloat),
            shape((total, width), single),
            shape((total, width), bfloat),
            shape((hidden, width), bfloat),
            shape((8, width), single),
            shape((1, hidden), single),
        ],
        scratch_shapes=[pltpu.VMEM(tile, bfloat)],
        compiler_params=params(),
        cost_estimate=cost(2 * total * width * (width + 2 * hidden), total * width * 30),
        name="feed_back",
    )(place, up_short, up_long, slope, middle, smalls, up_whole, *down_pieces)

    tiles = hidden // width
    column = lambda last: pl.BlockSpec((total, width), lambda i: (0, jnp.minimum(i, last)))
    out_block = pl.BlockSpec((slots, whole_rows, width), lambda i: (0, 0, i))
    up_keep, up_send = pl.pallas_call(
        functools.partial(weight_back, (1, tiles)),
        grid=(tiles + 1,),
        in_specs=[
            on_scalars(),
            kept((total, width)),
            kept((total, width)),
            kept((total, width)),
            pl.BlockSpec((total, width), lambda i: (0, jnp.maximum(i - 1, 0))),
        ],
        out_specs=[out_block] * 2,
        out_shape=[shape((slots, whole_rows, width + hidden), bfloat)] * 2,
        compiler_params=params(),
        cost_estimate=cost(2 * total * width * (width + hidden), total * width * 20),
        name="up_weight_back",
    )(place, mixed, second, branch, hidden_grad)
    up_sum = Scatter(count, up_keep, up_send)
    (qkv,) = up_sum.over_y(qkv)

    projected_grad = pl.pallas_call(
        functools.partial(backward_attention, half, width),
        grid=(grid,),
        in_specs=[by_step((TILE, 3 * width)), by_step(tile), probs_short_spec, probs_long_spec],
        out_specs=by_step((TILE, 3 * width)),
        out_shape=shape((total, 3 * width), bfloat),
        compiler_params=params(),
        cost_estimate=cost(2 * total * width * 3 * width * 2, total * width * 20),
        name="backward_attention",
    )(qkv, mixed_grad, probs_short, probs_long)

    qkv_keep, qkv_send = pl.pallas_call(
        functools.partial(weight_back, (3,)),
        grid=(3,),
        in_specs=[on_scalars(), kept((total, width)), column(2)],
        out_specs=[out_block] * 2,
        out_shape=[shape((slots, whole_rows, 3 * width), bfloat)] * 2,
        compiler_params=params(),
        cost_estimate=cost(2 * total * width * 3 * width, total * width * 16),
        name="qkv_weight_back",
    )(place, first, projected_grad)
    qkv_sum = Scatter(count, qkv_keep, qkv_send)
    middle_grad, qkv_sum.keep, down_share = up_sum.over_z(middle_grad, qkv_sum.keep, down_share)
    (middle_grad,) = qkv_sum.over_y(middle_grad)

    grad_short, grad_long, last_vectors, sums = pl.pallas_call(
        functools.partial(start_back, half, width, n),
        grid=(grid,),
        in_specs=[
            on_scalars(),
            short_spec,
            long_spec,
            kept((8, width)),
            kept((8, width)),
            by_step(tile),
            by_step((TILE, 3 * width)),
        ]
        + first_specs,
        out_specs=[short_spec, long_spec, kept((8, width)), kept((8, width))],
        out_shape=[
            shape(short.shape, bfloat),
            shape(long.shape, bfloat),
            shape((8, width), single),
            shape((8, width), single),
        ],
        scratch_shapes=[pltpu.VMEM((width, 3 * width), bfloat)],
        compiler_params=params(),
        cost_estimate=cost(2 * total * width * 3 * width, total * width * 30),
        name="start_back",
    )(place, short, long, embed, smalls, middle_grad, projected_grad, *first_pieces)
    middle, sums = tie(middle, sums)
    output_short, output_long = pl.pallas_call(
        functools.partial(forward_down, half),
        grid=(grid,),
        in_specs=[by_step(tile), by_step((TILE, hidden)), kept((8, width)), resident(down_whole.shape)],
        out_specs=[short_spec, long_spec],
        out_shape=[shape(short.shape, bfloat), shape(long.shape, bfloat)],
        compiler_params=params(),
        cost_estimate=cost(2 * total * width * hidden, total * width * 30),
        name="forward_down",
    )(middle, active, smalls, down_whole)

    owners = width // rows
    both = jnp.concatenate([vectors[:4], last_vectors[:4], sums[:marks]], axis=0)
    lines = both.shape[0]
    packed = both.reshape(lines, owners, rows).transpose(1, 0, 2).reshape(owners, lines * rows)
    own_steps = jnp.broadcast_to(steps.astype(single), (owners, marks))
    packed = jnp.concatenate([packed, bias_grad.reshape(owners, -1), own_steps], axis=1)
    packed = jnp.concatenate([packed, packed], axis=0)
    came = lax.all_to_all(packed, ("rep", "fsdp"), 0, 0, tiled=True)
    output_short, came, up_sum.keep = qkv_sum.over_z(output_short, came, up_sum.keep)
    vector_sums = jnp.sum(came[:, : 8 * rows], axis=0).reshape(8, rows)
    ends = lines * rows + hidden // owners
    up_bias_grad = jnp.sum(came[:, lines * rows : ends], axis=0)
    sequence_sums = came[:, 8 * rows : lines * rows].reshape(-1, rows)
    all_steps = came[:, ends:].astype(jnp.int32).reshape(-1)
    selector = (all_steps[:, None] == jnp.arange(timesteps, dtype=jnp.int32)[None, :]).astype(single)
    table_grad = lax.dot_general(
        selector,
        sequence_sums,
        TN,
        precision=lax.Precision.HIGHEST,
        preferred_element_type=single,
    )
    up_sum.over_x()
    qkv_sum.over_x()
    up_grads, qkv_weight_grad = up_sum.result(), qkv_sum.result()
    down_weight_grad = added(down_share, to_replica(down_share))
    return (
        output_short.reshape(input_short.shape),
        output_long.reshape(input_long.shape),
        grad_short.reshape(input_short.shape),
        grad_long.reshape(input_long.shape),
        table_grad,
        vector_sums[4],
        vector_sums[5],
        qkv_weight_grad,
        vector_sums[6],
        vector_sums[7],
        up_grads[:, :width],
        vector_sums[2],
        vector_sums[0],
        vector_sums[1],
        up_grads[:, width:],
        up_bias_grad,
        down_weight_grad,
        vector_sums[3],
    )


def solution(mesh):
    rows = P(("rep", "fsdp"), None, None)
    steps = P(("rep", "fsdp"))
    vector, matrix, table = P("fsdp"), P("fsdp", None), P(None, "fsdp")
    weights = (
        table,
        vector,
        vector,
        matrix,
        vector,
        vector,
        matrix,
        vector,
        vector,
        vector,
        matrix,
        vector,
        matrix,
        vector,
    )
    return jax.shard_map(
        functools.partial(shards, mesh.shape["fsdp"]),
        mesh=mesh,
        in_specs=(rows, rows, steps, steps, rows, rows) + weights,
        out_specs=(rows,) * 4 + weights,
        check_vma=False,
    )
```

profile of v0, /device:TPU:16, one launch (start us, length us, event | category | flops | bytes accessed | tf_op | source)
XLA Modules:
  0.0 331.5 jit_solution(8422544460619600222)
XLA Ops:
  7.3 1.1 convert_element_type.226.refs_0_
  8.4 1.6 collective-permute-start.3
  10.5 3.5 %collective-permute-start.1 = (bf16[48,2304]{1,0:T(8,128)(2,1)S(1)}, bf16[48,2304]{1,0:T(8,128)(2,1)S(1)}, u32[]{:S(2)}, u32[]{:S(2)}) collective-permute-start(bf16[48,2304]{1,0:T(8,128)(2,1)S(1)} %convert_element_type.226.refs_0_), channel_id=1, source_target_pairs={{0,8},{1,9},{2,10},{3,11},{4,12},{5,13},{6,14},{7,15},{8,0},{9,1},... | collective-permute-start | bytes 663560 | tf_op jit(solution)/shard_map/ppermute | solution.py:384
  15.3 5.7 %all-to-all-start = ((s32[16,1,6]{2,1,0:T(1,128)}), s32[16,1,6]{2,1,0:T(1,128)S(1)}, u32[]{:S(2)}, u32[]{:S(2)}) async-start(s32[16,1,6]{2,1,0:T(1,128)} %broadcast_in_dim.11), calls=%async_computation | async-start | bytes 16384 | tf_op jit(solution)/shard_map/all_to_all | solution.py:506
  21.9 1.1 convert.35
  23.4 7.8 %all-to-all-done = s32[16,1,6]{2,1,0:T(1,128)S(1)} async-done(((s32[16,1,6]{2,1,0:T(1,128)}), s32[16,1,6]{2,1,0:T(1,128)S(1)}, u32[]{:S(2)}, u32[]{:S(2)}) %all-to-all-start) | async-done | bytes 416 | tf_op jit(solution)/shard_map/all_to_all | solution.py:506
  31.9 3.5 %collective-permute-start.5 = (bf16[48,3840]{1,0:T(8,128)(2,1)S(1)}, bf16[48,3840]{1,0:T(8,128)(2,1)}, u32[]{:S(2)}, u32[]{:S(2)}) collective-permute-start(bf16[48,3840]{1,0:T(8,128)(2,1)S(1)} %pad_maximum_fusion.2), channel_id=1, source_target_pairs={{0,8},{1,9},{2,10},{3,11},{4,12},{5,13},{6,14},{7,15},{8,0},{9,1},... | collective-permute-start | bytes 1105928 | tf_op jit(solution)/shard_map/ppermute | solution.py:384
  35.5 1.4 collective-permute-start.7
  38.1 5.8 %collective-permute-done.7.refs_6_ = bf16[48,2304]{1,0:T(8,128)(2,1)S(1)} collective-permute-done((bf16[48,2304]{1,0:T(8,128)(2,1)S(1)}, bf16[48,2304]{1,0:T(8,128)(2,1)S(1)}, u32[]{:S(2)}, u32[]{:S(2)}) %collective-permute-start.7) | collective-permute-done | bytes 221216 | tf_op jit(solution)/shard_map/ppermute | solution.py:384
  44.0 1.4 collective-permute-start.9
  47.3 5.8 %all-to-all-start.1 = ((bf16[16,2,432]{2,1,0:T(2,128)(2,1)}), bf16[16,2,432]{2,1,0:T(2,128)(2,1)S(1)}, u32[]{:S(2)}, u32[]{:S(2)}) async-start(bf16[16,2,432]{2,1,0:T(2,128)(2,1)} %reshape.176), calls=%async_computation.1 | async-start | bytes 65536 | tf_op jit(solution)/shard_map/all_to_all | solution.py:515
  53.1 14.0 %all-to-all-done.1 = bf16[16,2,432]{2,1,0:T(2,128)(2,1)S(1)} async-done(((bf16[16,2,432]{2,1,0:T(2,128)(2,1)}), bf16[16,2,432]{2,1,0:T(2,128)(2,1)S(1)}, u32[]{:S(2)}, u32[]{:S(2)}) %all-to-all-start.1) | async-done | bytes 27680 | tf_op jit(solution)/shard_map/all_to_all | solution.py:515
  69.7 1.5 pad_maximum_fusion.refs_0_
  72.8 2.5 collective-permute-done.16.refs_1_
  77.7 3.3 %collective-permute-start.12 = (bf16[192,768]{1,0:T(8,128)(2,1)S(1)}, bf16[192,768]{1,0:T(8,128)(2,1)}, u32[]{:S(2)}, u32[]{:S(2)}) collective-permute-start(bf16[192,768]{1,0:T(8,128)(2,1)S(1)} %convert_element_type.231), channel_id=1, source_target_pairs={{0,8},{1,9},{2,10},{3,11},{4,12},{5,13},{6,14},{7,15},{8,0},{9,1},... | collective-permute-start | bytes 884744 | tf_op jit(solution)/shard_map/ppermute | solution.py:384
  81.8 28.7 %forward_attention.1 = (bf16[1024,768]{1,0:T(8,128)(2,1)}, bf16[1024,2304]{1,0:T(8,128)(2,1)}, bf16[4,12,128,128]{3,2,1,0:T(8,128)(2,1)}, bf16[2,12,256,256]{3,2,1,0:T(8,128)(2,1)}, bf16[1024,768]{1,0:T(8,128)(2,1)}) custom-call(s32[1]{0:T(128)} %bitcast.place_ref, bf16[512,768]{1,0:T(8,128)(2,1)} %bitcast.50, bf16[512,768]{1,0:T(8,128)(2,1)} %bitcast.53, ...), custom_call_target="tpu_custom_call" | custom-call | flops 1024 | bytes 1024 | tf_op jit(solution)/shard_map/forward_attention/pallas_call | solution.py:545
  110.7 1.7 pad_maximum_fusion.1.refs_0_
  112.4 1.7 collective-permute-done.23.refs_3_
  115.2 17.9 %forward_up.1 = (f32[1024,768]{1,0:T(8,128)}, bf16[1024,768]{1,0:T(8,128)(2,1)}, bf16[1024,3072]{1,0:T(8,128)(2,1)}, bf16[1024,3072]{1,0:T(8,128)(2,1)}, bf16[768,3840]{1,0:T(8,128)(2,1)}) custom-call(s32[1]{0:T(128)} %bitcast.place_ref, bf16[512,768]{1,0:T(8,128)(2,1)} %bitcast.51, bf16[512,768]{1,0:T(8,128)(2,1)} %bitcast.54, f32[8,768]{1,0:T(8,128)} %pad.4.embed_ref, ...), custom_call_target="tpu_custom_call" | custom-call | flops 1024 | bytes 1024 | tf_op jit(solution)/shard_map/forward_up/pallas_call | solution.py:576
  133.1 9.1 %down_weight_back.1 = bf16[3072,768]{1,0:T(8,128)(2,1)} custom-call(bf16[1024,3072]{1,0:T(8,128)(2,1)} %get-tuple-element.156.active_ref, bf16[512,768]{1,0:T(8,128)(2,1)} %bitcast.56, bf16[512,768]{1,0:T(8,128)(2,1)} %bitcast.58), custom_call_target="tpu_custom_call" | custom-call | flops 1024 | bytes 1024 | tf_op jit(solution)/shard_map/down_weight_back/pallas_call | solution.py:610
  142.9 2.7 collective-permute-done.25.refs_2_
  145.6 1.5 collective-permute-done.26.refs_3_
  148.1 23.5 %feed_back.1 = (bf16[1024,3072]{1,0:T(8,128)(2,1)}, bf16[1024,768]{1,0:T(8,128)(2,1)}, f32[1024,768]{1,0:T(8,128)}, bf16[1024,768]{1,0:T(8,128)(2,1)}, bf16[3072...) custom-call(s32[1]{0:T(128)} %bitcast.place_ref, bf16[512,768]{1,0:T(8,128)(2,1)} %bitcast.57, ...), custom_call_target="tpu_custom_call" | custom-call | flops 1024 | bytes 1024 | tf_op jit(solution)/shard_map/feed_back/pallas_call | solution.py:629
  171.6 16.1 %up_weight_back.1 = (bf16[8,48,3840]{2,1,0:T(8,128)(2,1)}, bf16[8,48,3840]{2,1,0:T(8,128)(2,1)}) custom-call(s32[1]{0:T(128)} %bitcast.place_ref, bf16[1024,768]{1,0:T(8,128)(2,1)} %get-tuple-element.143.mixed_ref.refs_0_, bf16[1024,768]{1,0:T(8,128)(2,1)} %get-tuple-element.155.refs_1_, bf16[1024,768]{1,0:T(8,128)(2,1)} %get-tuple-element.163.refs_2_, ...), custom_call_target="tpu_custom_call" | custom-call | flops 1024 | bytes 1024 | tf_op jit(solution)/shard_map/up_weight_back/pallas_call | solution.py:669
  187.8 5.5 %collective-permute-done.27 = bf16[8,48,3840]{2,1,0:T(8,128)(2,1)S(1)} collective-permute-done((bf16[8,48,3840]{2,1,0:T(8,128)(2,1)}, bf16[8,48,3840]{2,1,0:T(8,128)(2,1)S(1)}, u32[]{:S(2)}, u32[]{:S(2)}) %collective-permute-start.27) | collective-permute-done | bytes 2949152 | tf_op jit(solution)/shard_map/ppermute | solution.py:384
  193.3 2.5 add_convert_fusion
  196.8 19.8 %backward_attention.1.refs_1_.grad_ref = bf16[1024,2304]{1,0:T(8,128)(2,1)} custom-call(bf16[1024,2304]{1,0:T(8,128)(2,1)} %get-tuple-element.174.qkv_ref, bf16[1024,768]{1,0:T(8,128)(2,1)} %get-tuple-element.175.mixed_grad_ref, bf16[4,12,128,128]{3,2,1,0:T(8,128)(2,1)} %get-tuple-element.176.probs_short, bf16[2,12,256,256]{3,2,1,0:T(8,128)(2,1)} %get-tuple-element.177.probs_long), custom_call_target="tpu_custom_call" | custom-call | flops 1024 | bytes 1024 | tf_op jit(solution)/shard_map/backward_attention/pallas_call | solution.py:688
  216.6 9.8 %qkv_weight_back.1 = (bf16[8,48,2304]{2,1,0:T(8,128)(2,1)}, bf16[8,48,2304]{2,1,0:T(8,128)(2,1)}) custom-call(s32[1]{0:T(128)} %bitcast.place_ref, bf16[1024,768]{1,0:T(8,128)(2,1)} %get-tuple-element.173.refs_0_, bf16[1024,2304]{1,0:T(8,128)(2,1)} %backward_attention.1.refs_1_.grad_ref), custom_call_target="tpu_custom_call" | custom-call | flops 1024 | bytes 1024 | tf_op jit(solution)/shard_map/qkv_weight_back/pallas_call | solution.py:699
  226.4 7.1 %collective-permute-done.28 = bf16[4,48,3840]{2,1,0:T(8,128)(2,1)} collective-permute-done((bf16[4,48,3840]{2,1,0:T(8,128)(2,1)S(1)}, bf16[4,48,3840]{2,1,0:T(8,128)(2,1)}, u32[]{:S(2)}, u32[]{:S(2)}) %collective-permute-start.28) | collective-permute-done | bytes 1474592 | tf_op jit(solution)/shard_map/ppermute | solution.py:384
  233.5 2.8 fusion.5
  236.2 1.4 add_convert_fusion.2
  239.9 1.5 collective-permute-start.39
  241.4 10.5 %start_back.1 = (bf16[512,768]{1,0:T(8,128)(2,1)}, bf16[512,768]{1,0:T(8,128)(2,1)}, f32[8,768]{1,0:T(8,128)}, f32[8,768]{1,0:T(8,128)}) custom-call(s32[1]{0:T(128)} %bitcast.place_ref, bf16[512,768]{1,0:T(8,128)(2,1)} %bitcast.52, bf16[512,768]{1,0:T(8,128)(2,1)} %bitcast.55, f32[8,768]{1,0:T(8,128)} %pad.4.embed_ref, f32[8,768]{1,0:T(8,128)} %slice.153.small_ref, ...), custom_call_target="tpu_custom_call" | custom-call | flops 1024 | bytes 1024 | tf_op jit(solution)/shard_map/start_back/pallas_call | solution.py:713
  254.5 4.9 %all-to-all-start.2 = ((f32[32,1,870]{2,1,0:T(1,128)}), f32[32,1,870]{2,1,0:T(1,128)S(1)}, u32[]{:S(2)}, u32[]{:S(2)}) async-start(f32[32,1,870]{2,1,0:T(1,128)} %copy.58), calls=%async_computation.3 | async-start | bytes 229376 | tf_op jit(solution)/shard_map/all_to_all | solution.py:757
  259.4 1.6 collective-permute-start.35
  261.5 1.5 collective-permute-start.37
  263.0 10.1 %forward_down.1 = (bf16[512,768]{1,0:T(8,128)(2,1)}, bf16[512,768]{1,0:T(8,128)(2,1)}) custom-call(f32[1024,768]{1,0:T(8,128)} %get-tuple-element.193.middle_ref, bf16[1024,3072]{1,0:T(8,128)(2,1)} %get-tuple-element.156.active_ref, f32[8,768]{1,0:T(8,128)} %slice.153.small_ref, bf16[3072,768]{1,0:T(8,128)(2,1)} %get-tuple-element.194.down), custom_call_target="tpu_custom_call" | custom-call | flops 1024 | bytes 1024 | tf_op jit(solution)/shard_map/forward_down/pallas_call | solution.py:739
  273.1 1.9 convert_add_fusion.1
  276.7 2.4 collective-permute-done.36
  279.1 16.1 %collective-permute-done.37 = bf16[48,3840]{1,0:T(8,128)(2,1)S(1)} collective-permute-done((bf16[48,3840]{1,0:T(8,128)(2,1)S(1)}, bf16[48,3840]{1,0:T(8,128)(2,1)S(1)}, u32[]{:S(2)}, u32[]{:S(2)}) %collective-permute-start.37) | collective-permute-done | bytes 368672 | tf_op jit(solution)/shard_map/ppermute | solution.py:384
  295.7 2.7 collective-permute-start.32
  299.2 1.5 collective-permute-start.38
  300.7 1.2 fusion
  302.4 1.6 collective-permute-done.31
  304.1 9.5 %collective-permute-done.32 = bf16[48,2304]{1,0:T(8,128)(2,1)S(1)} collective-permute-done((bf16[48,2304]{1,0:T(8,128)(2,1)S(1)}, bf16[48,2304]{1,0:T(8,128)(2,1)S(1)}, u32[]{:S(2)}, u32[]{:S(2)}) %collective-permute-start.32) | collective-permute-done | bytes 221216 | tf_op jit(solution)/shard_map/ppermute | solution.py:384
  313.5 3.9 %collective-permute-done.33 = bf16[48,2304]{1,0:T(8,128)(2,1)S(1)} collective-permute-done((bf16[48,2304]{1,0:T(8,128)(2,1)S(1)}, bf16[48,2304]{1,0:T(8,128)(2,1)S(1)}, u32[]{:S(2)}, u32[]{:S(2)}) %collective-permute-start.33) | collective-permute-done | bytes 221216 | tf_op jit(solution)/shard_map/ppermute | solution.py:384
  317.6 1.5 collective-permute-start.34
  320.7 2.9 collective-permute-done.34
  (211 shorter events, 29.3 us)
Async XLA Ops:
  7.3 45.8 %copy-start.26 = (f32[192,768]{1,0:T(8,128)S(1)}, f32[192,768]{1,0:T(8,128)}, u32[]{:S(2)}) copy-start(f32[192,768]{1,0:T(8,128)} %param.38) | copy-start | bytes 1769476
  8.4 63.8 %copy-start.2 = (bf16[48,2304]{1,0:T(8,128)(2,1)}, bf16[48,2304]{1,0:T(8,128)(2,1)S(1)}, u32[]{:S(2)}) copy-start(bf16[48,2304]{1,0:T(8,128)(2,1)S(1)} %convert_element_type.226.refs_0_) | copy-start | bytes 663556
  8.4 22.9 %collective-permute-start.3 = (bf16[48,2304]{1,0:T(8,128)(2,1)S(1)}, bf16[48,2304]{1,0:T(8,128)(2,1)S(1)}, u32[]{:S(2)}, u32[]{:S(2)}) collective-permute-start(bf16[48,2304]{1,0:T(8,128)(2,1)S(1)} %convert_element_type.226.refs_0_), channel_id=1, source_target_pairs={{0,2},{1,3},{2,0},{3,1},{4,6},{5,7},{6,4},{7,5},{8,10},{9,11},{10,... | collective-permute-start | bytes 663560 | tf_op jit(solution)/shard_map/ppermute | solution.py:384
  10.0 21.3 %collective-permute-start.2 = (bf16[48,2304]{1,0:T(8,128)(2,1)S(1)}, bf16[48,2304]{1,0:T(8,128)(2,1)S(1)}, u32[]{:S(2)}, u32[]{:S(2)}) collective-permute-start(bf16[48,2304]{1,0:T(8,128)(2,1)S(1)} %convert_element_type.226.refs_0_), channel_id=1, source_target_pairs={{0,12},{1,13},{2,14},{3,15},{4,8},{5,9},{6,10},{7,11},{8,4},{9,5},... | collective-permute-start | bytes 663560 | tf_op jit(solution)/shard_map/ppermute | solution.py:384
  10.5 20.9 %collective-permute-start.1 = (bf16[48,2304]{1,0:T(8,128)(2,1)S(1)}, bf16[48,2304]{1,0:T(8,128)(2,1)S(1)}, u32[]{:S(2)}, u32[]{:S(2)}) collective-permute-start(bf16[48,2304]{1,0:T(8,128)(2,1)S(1)} %convert_element_type.226.refs_0_), channel_id=1, source_target_pairs={{0,8},{1,9},{2,10},{3,11},{4,12},{5,13},{6,14},{7,15},{8,0},{9,1},... | collective-permute-start | bytes 663560 | tf_op jit(solution)/shard_map/ppermute | solution.py:384
  14.0 17.4 %collective-permute-start = (bf16[48,2304]{1,0:T(8,128)(2,1)S(1)}, bf16[48,2304]{1,0:T(8,128)(2,1)S(1)}, u32[]{:S(2)}, u32[]{:S(2)}) collective-permute-start(bf16[48,2304]{1,0:T(8,128)(2,1)S(1)} %convert_element_type.226.refs_0_), channel_id=1, source_target_pairs={{0,4},{1,5},{2,6},{3,7},{4,0},{5,1},{6,2},{7,3},{8,12},{9,13},{10,... | collective-permute-start | bytes 663560 | tf_op jit(solution)/shard_map/ppermute | solution.py:384
  15.3 15.9 %all-to-all-start = ((s32[16,1,6]{2,1,0:T(1,128)}), s32[16,1,6]{2,1,0:T(1,128)S(1)}, u32[]{:S(2)}, u32[]{:S(2)}) async-start(s32[16,1,6]{2,1,0:T(1,128)} %broadcast_in_dim.11), calls=%async_computation | async-start | bytes 16384 | tf_op jit(solution)/shard_map/all_to_all | solution.py:506
  31.3 39.9 %copy-start.11 = (bf16[48,2304]{1,0:T(8,128)(2,1)}, bf16[48,2304]{1,0:T(8,128)(2,1)S(1)}, u32[]{:S(2)}) copy-start(bf16[48,2304]{1,0:T(8,128)(2,1)S(1)} %collective-permute-done.2.refs_12_) | copy-start | bytes 663556
  31.3 39.9 %copy-start.12 = (bf16[48,2304]{1,0:T(8,128)(2,1)}, bf16[48,2304]{1,0:T(8,128)(2,1)S(1)}, u32[]{:S(2)}) copy-start(bf16[48,2304]{1,0:T(8,128)(2,1)S(1)} %collective-permute-done.1.refs_8_) | copy-start | bytes 663556
  31.4 38.2 %collective-permute-start.6 = (bf16[48,3840]{1,0:T(8,128)(2,1)S(1)}, bf16[48,3840]{1,0:T(8,128)(2,1)}, u32[]{:S(2)}, u32[]{:S(2)}) collective-permute-start(bf16[48,3840]{1,0:T(8,128)(2,1)S(1)} %pad_maximum_fusion.2), channel_id=1, source_target_pairs={{0,12},{1,13},{2,14},{3,15},{4,8},{5,9},{6,10},{7,11},{8,4},{9,5},... | collective-permute-start | bytes 1105928 | tf_op jit(solution)/shard_map/ppermute | solution.py:384
  31.9 37.7 %collective-permute-start.5 = (bf16[48,3840]{1,0:T(8,128)(2,1)S(1)}, bf16[48,3840]{1,0:T(8,128)(2,1)}, u32[]{:S(2)}, u32[]{:S(2)}) collective-permute-start(bf16[48,3840]{1,0:T(8,128)(2,1)S(1)} %pad_maximum_fusion.2), channel_id=1, source_target_pairs={{0,8},{1,9},{2,10},{3,11},{4,12},{5,13},{6,14},{7,15},{8,0},{9,1},... | collective-permute-start | bytes 1105928 | tf_op jit(solution)/shard_map/ppermute | solution.py:384
  35.4 34.2 %collective-permute-start.4 = (bf16[48,3840]{1,0:T(8,128)(2,1)S(1)}, bf16[48,3840]{1,0:T(8,128)(2,1)}, u32[]{:S(2)}, u32[]{:S(2)}) collective-permute-start(bf16[48,3840]{1,0:T(8,128)(2,1)S(1)} %pad_maximum_fusion.2), channel_id=1, source_target_pairs={{0,4},{1,5},{2,6},{3,7},{4,0},{5,1},{6,2},{7,3},{8,12},{9,13},{10,... | collective-permute-start | bytes 1105928 | tf_op jit(solution)/shard_map/ppermute | solution.py:384
  35.5 8.4 %collective-permute-start.7 = (bf16[48,2304]{1,0:T(8,128)(2,1)S(1)}, bf16[48,2304]{1,0:T(8,128)(2,1)S(1)}, u32[]{:S(2)}, u32[]{:S(2)}) collective-permute-start(bf16[48,2304]{1,0:T(8,128)(2,1)S(1)} %collective-permute-done.refs_4_), channel_id=1, source_target_pairs={{0,2},{1,3},{2,0},{3,1},{4,6},{5,7},{6,4},{7,5},{8,10},{9,11},{10,... | collective-permute-start | bytes 663560 | tf_op jit(solution)/shard_map/ppermute | solution.py:384
  37.5 32.1 %collective-permute-start.8 = (bf16[48,2304]{1,0:T(8,128)(2,1)S(1)}, bf16[48,2304]{1,0:T(8,128)(2,1)S(1)}, u32[]{:S(2)}, u32[]{:S(2)}) collective-permute-start(bf16[48,2304]{1,0:T(8,128)(2,1)S(1)} %collective-permute-done.1.refs_8_), channel_id=1, source_target_pairs={{0,2},{1,3},{2,0},{3,1},{4,6},{5,7},{6,4},{7,5},{8,10},{9,11},{10,... | collective-permute-start | bytes 663560 | tf_op jit(solution)/shard_map/ppermute | solution.py:384
  44.0 25.6 %collective-permute-start.9 = (bf16[48,2304]{1,0:T(8,128)(2,1)S(1)}, bf16[48,2304]{1,0:T(8,128)(2,1)S(1)}, u32[]{:S(2)}, u32[]{:S(2)}) collective-permute-start(bf16[48,2304]{1,0:T(8,128)(2,1)S(1)} %collective-permute-done.2.refs_12_), channel_id=1, source_target_pairs={{0,2},{1,3},{2,0},{3,1},{4,6},{5,7},{6,4},{7,5},{8,10},{9,11},{10,... | collective-permute-start | bytes 663560 | tf_op jit(solution)/shard_map/ppermute | solution.py:384
  47.3 19.8 %all-to-all-start.1 = ((bf16[16,2,432]{2,1,0:T(2,128)(2,1)}), bf16[16,2,432]{2,1,0:T(2,128)(2,1)S(1)}, u32[]{:S(2)}, u32[]{:S(2)}) async-start(bf16[16,2,432]{2,1,0:T(2,128)(2,1)} %reshape.176), calls=%async_computation.1 | async-start | bytes 65536 | tf_op jit(solution)/shard_map/all_to_all | solution.py:515
  53.0 180.4 %reduce-scatter.2.cloned.1.call-start = ((), (), s32[]{:S(2)}) async-start(), calls=%async_computation.4 | async-start | bytes 5013504 | tf_op jit(solution)/shard_map/reduce_scatter | solution.py:624
  69.6 1.7 collective-permute-start.10
  71.3 39.3 %collective-permute-start.15 = (bf16[4,48,3840]{2,1,0:T(8,128)(2,1)S(1)}, bf16[4,48,3840]{2,1,0:T(8,128)(2,1)S(1)}, u32[]{:S(2)}, u32[]{:S(2)}) collective-permute-start(bf16[4,48,3840]{2,1,0:T(8,128)(2,1)S(1)} %pad_maximum_fusion.refs_0_), channel_id=1, source_target_pairs={{0,1},{1,0},{2,3},{3,2},{4,5},{5,4},{6,7},{7,6},{8,9},{9,8},{10,11... | collective-permute-start | bytes 4423688 | tf_op jit(solution)/shard_map/ppermute | solution.py:384
  71.8 38.8 %collective-permute-start.14 = (bf16[4,48,3840]{2,1,0:T(8,128)(2,1)S(1)}, bf16[4,48,3840]{2,1,0:T(8,128)(2,1)}, u32[]{:S(2)}, u32[]{:S(2)}) collective-permute-start(bf16[4,48,3840]{2,1,0:T(8,128)(2,1)S(1)} %pad_maximum_fusion.refs_0_), channel_id=1, source_target_pairs={{0,2},{1,3},{2,0},{3,1},{4,6},{5,7},{6,4},{7,5},{8,10},{9,11},{10,... | collective-permute-start | bytes 4423688 | tf_op jit(solution)/shard_map/ppermute | solution.py:384
  72.2 3.1 collective-permute-start.16
  72.2 3.5 %collective-permute-start.18 = (bf16[48,2304]{1,0:T(8,128)(2,1)S(1)}, bf16[48,2304]{1,0:T(8,128)(2,1)S(1)}, u32[]{:S(2)}, u32[]{:S(2)}) collective-permute-start(bf16[48,2304]{1,0:T(8,128)(2,1)S(1)} %copy-done.14), channel_id=1, source_target_pairs={{0,1},{1,0},{2,3},{3,2},{4,5},{5,4},{6,7},{7,6},{8,9},{9,8},{10,11... | collective-permute-start | bytes 663560 | tf_op jit(solution)/shard_map/ppermute | solution.py:384
  72.7 3.3 collective-permute-start.20
  75.3 1.7 collective-permute-start.22
  75.7 1.7 collective-permute-start.17
  76.0 1.7 collective-permute-start.19
  77.0 4.1 %collective-permute-start.21 = (bf16[48,2304]{1,0:T(8,128)(2,1)}, bf16[48,2304]{1,0:T(8,128)(2,1)S(1)}, u32[]{:S(2)}, u32[]{:S(2)}) collective-permute-start(bf16[48,2304]{1,0:T(8,128)(2,1)} %copy-done.17), channel_id=1, source_target_pairs={{0,1},{1,0},{2,3},{3,2},{4,5},{5,4},{6,7},{7,6},{8,9},{9,8},{10,11... | collective-permute-start | bytes 663560 | tf_op jit(solution)/shard_map/ppermute | solution.py:384
  77.4 33.1 %collective-permute-start.13 = (bf16[192,768]{1,0:T(8,128)(2,1)S(1)}, bf16[192,768]{1,0:T(8,128)(2,1)}, u32[]{:S(2)}, u32[]{:S(2)}) collective-permute-start(bf16[192,768]{1,0:T(8,128)(2,1)S(1)} %convert_element_type.231), channel_id=1, source_target_pairs={{0,12},{1,13},{2,14},{3,15},{4,8},{5,9},{6,10},{7,11},{8,4},{9,5},... | collective-permute-start | bytes 884744 | tf_op jit(solution)/shard_map/ppermute | solution.py:384
  77.7 32.8 %collective-permute-start.12 = (bf16[192,768]{1,0:T(8,128)(2,1)S(1)}, bf16[192,768]{1,0:T(8,128)(2,1)}, u32[]{:S(2)}, u32[]{:S(2)}) collective-permute-start(bf16[192,768]{1,0:T(8,128)(2,1)S(1)} %convert_element_type.231), channel_id=1, source_target_pairs={{0,8},{1,9},{2,10},{3,11},{4,12},{5,13},{6,14},{7,15},{8,0},{9,1},... | collective-permute-start | bytes 884744 | tf_op jit(solution)/shard_map/ppermute | solution.py:384
  81.1 29.4 %collective-permute-start.11 = (bf16[192,768]{1,0:T(8,128)(2,1)S(1)}, bf16[192,768]{1,0:T(8,128)(2,1)}, u32[]{:S(2)}, u32[]{:S(2)}) collective-permute-start(bf16[192,768]{1,0:T(8,128)(2,1)S(1)} %convert_element_type.231), channel_id=1, source_target_pairs={{0,4},{1,5},{2,6},{3,7},{4,0},{5,1},{6,2},{7,3},{8,12},{9,13},{10,... | collective-permute-start | bytes 884744 | tf_op jit(solution)/shard_map/ppermute | solution.py:384
  110.6 3.5 %collective-permute-start.23 = (bf16[4,48,3840]{2,1,0:T(8,128)(2,1)}, bf16[4,48,3840]{2,1,0:T(8,128)(2,1)S(1)}, u32[]{:S(2)}, u32[]{:S(2)}) collective-permute-start(bf16[4,48,3840]{2,1,0:T(8,128)(2,1)} %collective-permute-done.14.refs_1_), channel_id=1, source_target_pairs={{0,1},{1,0},{2,3},{3,2},{4,5},{5,4},{6,7},{7,6},{8,9},{9,8},{10,11... | collective-permute-start | bytes 4423688 | tf_op jit(solution)/shard_map/ppermute | solution.py:384
  114.1 28.4 %collective-permute-start.24 = (bf16[4,192,768]{2,1,0:T(8,128)(2,1)S(1)}, bf16[4,192,768]{2,1,0:T(8,128)(2,1)}, u32[]{:S(2)}, u32[]{:S(2)}) collective-permute-start(bf16[4,192,768]{2,1,0:T(8,128)(2,1)S(1)} %pad_maximum_fusion.1.refs_0_), channel_id=1, source_target_pairs={{0,2},{1,3},{2,0},{3,1},{4,6},{5,7},{6,4},{7,5},{8,10},{9,11},{10,... | collective-permute-start | bytes 3538952 | tf_op jit(solution)/shard_map/ppermute | solution.py:384
  142.3 3.3 collective-permute-start.25
  142.5 4.6 %collective-permute-start.26 = (bf16[4,192,768]{2,1,0:T(8,128)(2,1)}, bf16[4,192,768]{2,1,0:T(8,128)(2,1)S(1)}, u32[]{:S(2)}, u32[]{:S(2)}) collective-permute-start(bf16[4,192,768]{2,1,0:T(8,128)(2,1)} %collective-permute-done.24.refs_1_), channel_id=1, source_target_pairs={{0,1},{1,0},{2,3},{3,2},{4,5},{5,4},{6,7},{7,6},{8,9},{9,8},{10,11... | collective-permute-start | bytes 3538952 | tf_op jit(solution)/shard_map/ppermute | solution.py:384
  187.7 5.6 %collective-permute-start.27 = (bf16[8,48,3840]{2,1,0:T(8,128)(2,1)}, bf16[8,48,3840]{2,1,0:T(8,128)(2,1)S(1)}, u32[]{:S(2)}, u32[]{:S(2)}) collective-permute-start(bf16[8,48,3840]{2,1,0:T(8,128)(2,1)} %get-tuple-element.166), channel_id=1, source_target_pairs={{0,1},{1,0},{2,3},{3,2},{4,5},{5,4},{6,7},{7,6},{8,9},{9,8},{10,11... | collective-permute-start | bytes 8847368 | tf_op jit(solution)/shard_map/ppermute | solution.py:384
  195.8 37.7 %collective-permute-start.28 = (bf16[4,48,3840]{2,1,0:T(8,128)(2,1)S(1)}, bf16[4,48,3840]{2,1,0:T(8,128)(2,1)}, u32[]{:S(2)}, u32[]{:S(2)}) collective-permute-start(bf16[4,48,3840]{2,1,0:T(8,128)(2,1)S(1)} %get-tuple-element.171), channel_id=1, source_target_pairs={{0,2},{1,3},{2,0},{3,1},{4,6},{5,7},{6,4},{7,5},{8,10},{9,11},{10,... | collective-permute-start | bytes 4423688 | tf_op jit(solution)/shard_map/ppermute | solution.py:384
  226.4 9.9 %collective-permute-start.29 = (bf16[8,48,2304]{2,1,0:T(8,128)(2,1)}, bf16[8,48,2304]{2,1,0:T(8,128)(2,1)S(1)}, u32[]{:S(2)}, u32[]{:S(2)}) collective-permute-start(bf16[8,48,2304]{2,1,0:T(8,128)(2,1)} %get-tuple-element.185), channel_id=1, source_target_pairs={{0,1},{1,0},{2,3},{3,2},{4,5},{5,4},{6,7},{7,6},{8,9},{9,8},{10,11... | collective-permute-start | bytes 5308424 | tf_op jit(solution)/shard_map/ppermute | solution.py:384
  237.6 37.4 %collective-permute-start.30 = (bf16[4,48,2304]{2,1,0:T(8,128)(2,1)}, bf16[4,48,2304]{2,1,0:T(8,128)(2,1)S(1)}, u32[]{:S(2)}, u32[]{:S(2)}) collective-permute-start(bf16[4,48,2304]{2,1,0:T(8,128)(2,1)} %get-tuple-element.190), channel_id=1, source_target_pairs={{0,2},{1,3},{2,0},{3,1},{4,6},{5,7},{6,4},{7,5},{8,10},{9,11},{10,... | collective-permute-start | bytes 2654216 | tf_op jit(solution)/shard_map/ppermute | solution.py:384
  239.9 33.2 %collective-permute-start.39 = (bf16[192,768]{1,0:T(8,128)(2,1)}, bf16[192,768]{1,0:T(8,128)(2,1)}, u32[]{:S(2)}, u32[]{:S(2)}) collective-permute-start(bf16[192,768]{1,0:T(8,128)(2,1)} %reduce-scatter.2.cloned.1.call-done), channel_id=1, source_target_pairs={{0,16},{16,0},{1,17},{17,1},{2,18},{18,2},{3,19},{19,3},{4,20},{20... | collective-permute-start | bytes 884744 | tf_op jit(solution)/shard_map/ppermute | solution.py:388
  254.5 18.5 %all-to-all-start.2 = ((f32[32,1,870]{2,1,0:T(1,128)}), f32[32,1,870]{2,1,0:T(1,128)S(1)}, u32[]{:S(2)}, u32[]{:S(2)}) async-start(f32[32,1,870]{2,1,0:T(1,128)} %copy.58), calls=%async_computation.3 | async-start | bytes 229376 | tf_op jit(solution)/shard_map/all_to_all | solution.py:757
  259.4 17.3 %collective-permute-start.35 = (bf16[48,3840]{1,0:T(8,128)(2,1)}, bf16[48,3840]{1,0:T(8,128)(2,1)S(1)}, u32[]{:S(2)}, u32[]{:S(2)}) collective-permute-start(bf16[48,3840]{1,0:T(8,128)(2,1)} %get-tuple-element.218), channel_id=1, source_target_pairs={{0,4},{1,5},{2,6},{3,7},{4,0},{5,1},{6,2},{7,3},{8,12},{9,13},{10,... | collective-permute-start | bytes 1105928 | tf_op jit(solution)/shard_map/ppermute | solution.py:384
  261.0 18.1 %collective-permute-start.36 = (bf16[48,3840]{1,0:T(8,128)(2,1)}, bf16[48,3840]{1,0:T(8,128)(2,1)S(1)}, u32[]{:S(2)}, u32[]{:S(2)}) collective-permute-start(bf16[48,3840]{1,0:T(8,128)(2,1)} %get-tuple-element.219), channel_id=1, source_target_pairs={{0,8},{1,9},{2,10},{3,11},{4,12},{5,13},{6,14},{7,15},{8,0},{9,1},... | collective-permute-start | bytes 1105928 | tf_op jit(solution)/shard_map/ppermute | solution.py:384
  261.5 33.7 %collective-permute-start.37 = (bf16[48,3840]{1,0:T(8,128)(2,1)S(1)}, bf16[48,3840]{1,0:T(8,128)(2,1)S(1)}, u32[]{:S(2)}, u32[]{:S(2)}) collective-permute-start(bf16[48,3840]{1,0:T(8,128)(2,1)S(1)} %copy-done.27), channel_id=1, source_target_pairs={{0,12},{1,13},{2,14},{3,15},{4,8},{5,9},{6,10},{7,11},{8,4},{9,5},... | collective-permute-start | bytes 1105928 | tf_op jit(solution)/shard_map/ppermute | solution.py:384
  295.6 8.4 %collective-permute-start.31 = (bf16[48,2304]{1,0:T(8,128)(2,1)S(1)}, bf16[48,2304]{1,0:T(8,128)(2,1)S(1)}, u32[]{:S(2)}, u32[]{:S(2)}) collective-permute-start(bf16[48,2304]{1,0:T(8,128)(2,1)S(1)} %copy-done.30), channel_id=1, source_target_pairs={{0,4},{1,5},{2,6},{3,7},{4,0},{5,1},{6,2},{7,3},{8,12},{9,13},{10,... | collective-permute-start | bytes 663560 | tf_op jit(solution)/shard_map/ppermute | solution.py:384
  295.7 17.8 %collective-permute-start.32 = (bf16[48,2304]{1,0:T(8,128)(2,1)S(1)}, bf16[48,2304]{1,0:T(8,128)(2,1)S(1)}, u32[]{:S(2)}, u32[]{:S(2)}) collective-permute-start(bf16[48,2304]{1,0:T(8,128)(2,1)S(1)} %copy-done.29), channel_id=1, source_target_pairs={{0,8},{1,9},{2,10},{3,11},{4,12},{5,13},{6,14},{7,15},{8,0},{9,1},... | collective-permute-start | bytes 663560 | tf_op jit(solution)/shard_map/ppermute | solution.py:384
  298.5 19.0 %collective-permute-start.33 = (bf16[48,2304]{1,0:T(8,128)(2,1)S(1)}, bf16[48,2304]{1,0:T(8,128)(2,1)S(1)}, u32[]{:S(2)}, u32[]{:S(2)}) collective-permute-start(bf16[48,2304]{1,0:T(8,128)(2,1)S(1)} %copy-done.28), channel_id=1, source_target_pairs={{0,12},{1,13},{2,14},{3,15},{4,8},{5,9},{6,10},{7,11},{8,4},{9,5},... | collective-permute-start | bytes 663560 | tf_op jit(solution)/shard_map/ppermute | solution.py:384
  299.2 20.0 %collective-permute-start.38 = (bf16[48,3840]{1,0:T(8,128)(2,1)S(1)}, bf16[48,3840]{1,0:T(8,128)(2,1)S(1)}, u32[]{:S(2)}, u32[]{:S(2)}) collective-permute-start(bf16[48,3840]{1,0:T(8,128)(2,1)S(1)} %add_convert_fusion.4), channel_id=1, source_target_pairs={{0,16},{16,0},{1,17},{17,1},{2,18},{18,2},{3,19},{19,3},{4,20},{20... | collective-permute-start | bytes 1105928 | tf_op jit(solution)/shard_map/ppermute | solution.py:388
  317.6 6.0 %collective-permute-start.34 = (bf16[48,2304]{1,0:T(8,128)(2,1)S(1)}, bf16[48,2304]{1,0:T(8,128)(2,1)S(1)}, u32[]{:S(2)}, u32[]{:S(2)}) collective-permute-start(bf16[48,2304]{1,0:T(8,128)(2,1)S(1)} %add_convert_fusion.9), channel_id=1, source_target_pairs={{0,16},{16,0},{1,17},{17,1},{2,18},{18,2},{3,19},{19,3},{4,20},{20... | collective-permute-start | bytes 663560 | tf_op jit(solution)/shard_map/ppermute | solution.py:388
  (39 other events, 512.3 us)
Sparse Core Ops, SparseCore 0:
  142.4 77.4 reduce-scatter.1
where the time goes:
time: 337 us; the launch traced here: 332 us
  Pallas kernels  145 us (43%)
  waiting for transfers between devices  85.8 us (25%)
  starting transfers between devices  51 us (15%)
  other arithmetic  20.9 us (6%)
  between operations  15.2 us (5%)
  local copies, waits for them, and re-layouts  11.8 us (4%)
    ppermute x37, waiting for transfers between devices, across(): return lax.ppermute(array, 'fsdp', flip(bit))  61.1 us
    ppermute x37, starting transfers between devices, across(): return lax.ppermute(array, 'fsdp', flip(bit))  30.1 us
    pallas_call x1, Pallas kernels, shards(): pl.pallas_call(functools.partial(forward_attention, half, width, n), grid...  28.7 us
    pallas_call x1, Pallas kernels, shards(): pl.pallas_call(functools.partial(feed_back, half, width, hidden, len(down...  23.5 us
    pallas_call x1, Pallas kernels, shards(): pl.pallas_call(functools.partial(backward_attention, half, width), grid=(...  19.8 us
    pallas_call x1, Pallas kernels, shards(): pl.pallas_call(functools.partial(forward_up, half, width, hidden, len(up_...  17.9 us
    pallas_call x1, Pallas kernels, shards(): pl.pallas_call(functools.partial(weight_back, (1, tiles)), grid=(tiles +...  16.1 us
    all_to_all x1, waiting for transfers between devices, shards(): told = lax.all_to_all(chosen, 'fsdp', 0, 0, tiled=True)  14 us
  transfers between devices with their start and end apart: 44, of which 16 were waited for; matrix products, arithmetic and copies ran while one was open for 9% of the time, Pallas kernels for 44%

commit v1 on v0

--- a/solution.py
+++ b/solution.py
@@ -13,6 +13,9 @@
 HEAD_DIM = 64
 PAIR = 2 * HEAD_DIM
 TILE = 256
+BAND = 256
+SHORT = 128
+LONG = 256
 SHARDS = 16
 LOG2E = 1.4426950408889634
 GELU_A = 0.7978845608028654
@@ -95,22 +98,22 @@
     )
 
 
-def start_rows(step, half, short_ref, long_ref, embed_ref, emit):
-    per = TILE // 128
+def start_rows(step, half, size, short_ref, long_ref, embed_ref, emit):
+    def group(rows_ref, length, number, is_short):
+        rows = rows_ref[...].astype(single)
+        parts = []
+        for s in range(size // length):
+            embed = embed_ref[pl.ds(number + s, 1), :]
+            parts.append(rows[s * length : (s + 1) * length] + embed)
+        emit(parts[0] if len(parts) == 1 else jnp.concatenate(parts, axis=0), is_short)
 
     @pl.when(step < half)
     def _():
-        rows = short_ref[...].astype(single)
-        parts = []
-        for s in range(per):
-            embed = embed_ref[pl.ds(step * per + s, 1), :]
-            parts.append(rows[s * 128 : (s + 1) * 128] + embed)
-        emit(jnp.concatenate(parts, axis=0), True)
+        group(short_ref, SHORT, step * (size // SHORT), True)
 
     @pl.when(step >= half)
     def _():
-        embed = embed_ref[pl.ds(per * half + step - half, 1), :]
-        emit(long_ref[...].astype(single) + embed, False)
+        group(long_ref, LONG, half * (size // SHORT) + (step - half) * (size // LONG), False)
 
 
 def attend(query, keys, values, probs_ref, at):
@@ -166,7 +169,7 @@
                     bfloat
                 )
 
-    start_rows(step, half, short_ref, long_ref, embed_ref, emit)
+    start_rows(step, half, short_ref.shape[0], short_ref, long_ref, embed_ref, emit)
 
 
 def forward_up(
@@ -183,7 +186,7 @@
     def emit(start, _):
         middle_ref[...] = start
 
-    start_rows(step, half, short_ref, long_ref, embed_ref, emit)
+    start_rows(step, half, short_ref.shape[0], short_ref, long_ref, embed_ref, emit)
     middle = middle_ref[...] + dot(mixed_ref[...], weight[:, :width], NN) + small_ref[4:5, :]
     middle_ref[...] = middle
     scaled, _ = standardize(middle)
@@ -213,31 +216,33 @@
         send_ref[slot] = value
 
 
-def down_weight_back(active_ref, short_ref, long_ref, out_ref):
-    split = short_ref.shape[0]
-    for at in range(0, active_ref.shape[1], TILE):
-        cols = slice(at, at + TILE)
-        total = dot(active_ref[:split, cols], short_ref[...], TN) + dot(
-            active_ref[split:, cols], long_ref[...], TN
-        )
-        out_ref[cols, :] = total.astype(bfloat)
+def down_weight_back(active_ref, short_ref, long_ref, out_ref, grad):
+    @pl.when(pl.program_id(0) == 0)
+    def _():
+        split = short_ref.shape[0]
+        grad[:split, :] = short_ref[...]
+        grad[split:, :] = long_ref[...]
+
+    out_ref[...] = dot(active_ref[...], grad[...], TN).astype(bfloat)
 
 
 def weight_back(parts, place_ref, *refs):
     lefts, rights = refs[: len(parts)], refs[len(parts) : 2 * len(parts)]
-    keep_ref, send_ref = refs[2 * len(parts) :]
+    keep_ref, send_ref, turned = refs[2 * len(parts) :]
     step = pl.program_id(0)
     place = place_ref[0]
     rows = keep_ref.shape[1]
-    block = 8 * rows
     begin = 0
     for left_ref, right_ref, tiles in zip(lefts, rights, parts):
 
-        def work(left_ref=left_ref, right_ref=right_ref):
-            for k in range(left_ref.shape[1] // block):
-                total = dot(left_ref[:, k * block : (k + 1) * block], right_ref[...], TN).astype(bfloat)
-                for j in range(8):
-                    store_shard(place, 8 * k + j, total[j * rows : (j + 1) * rows], keep_ref, send_ref)
+        @pl.when(step == begin)
+        def _(left_ref=left_ref):
+            turned[...] = left_ref[...].T
+
+        def work(right_ref=right_ref):
+            total = dot(turned[...], right_ref[...], NN).astype(bfloat)
+            for k in range(SHARDS):
+                store_shard(place, k, total[k * rows : (k + 1) * rows], keep_ref, send_ref)
 
         if len(parts) == 1:
             work()
@@ -247,14 +252,17 @@
 
 
 def feed_back(
-    half, width, hidden, n_down, place_ref, short_ref, long_ref, slope_ref, middle_ref, small_ref, weight, *refs
+    half, width, hidden, n, place_ref, short_ref, long_ref, slope_ref, middle_ref, small_ref, *refs
 ):
-    downs = refs[:n_down]
-    (hidden_grad_ref, branch_ref, middle_grad_ref, mixed_grad_ref, down, vector_ref, bias_ref, grad) = refs[n_down:]
+    ups, downs = refs[:n], refs[n : 2 * n]
+    (hidden_grad_ref, branch_ref, middle_grad_ref, mixed_grad_ref, vector_ref, bias_ref, weight, down, grad) = refs[
+        2 * n :
+    ]
     step = pl.program_id(0)
 
     @pl.when(step == 0)
     def _():
+        assemble_lines(place_ref[0], ups, weight)
         assemble_lines(place_ref[0], downs, down)
         vector_ref[...] = jnp.zeros_like(vector_ref)
         bias_ref[...] = jnp.zeros_like(bias_ref)
@@ -267,7 +275,7 @@
     def _():
         grad[...] = long_ref[...]
 
-    upper = jnp.zeros((TILE, width), single)
+    upper = jnp.zeros((grad.shape[0], width), single)
     for at in range(0, hidden, width):
         cols = slice(at, at + width)
         passed = dot(grad[...], down[cols, :], NT) * slope_ref[:, cols].astype(single)
@@ -334,7 +342,7 @@
     firsts = refs[:n_first]
     in_short, in_long, vector_ref, sums_ref, weight = refs[n_first:]
     step = pl.program_id(0)
-    per = TILE // 128
+    size = short_ref.shape[0]
 
     @pl.when(step == 0)
     def _():
@@ -350,21 +358,25 @@
         vector_ref[1:2, :] += jnp.sum(upper, axis=0, keepdims=True)
         vector_ref[2:3, :] += jnp.sum(grad_ref[:, :width].astype(single), axis=0, keepdims=True)
         vector_ref[3:4, :] += jnp.sum(grad_ref[:, 2 * width :].astype(single), axis=0, keepdims=True)
-        if is_short:
-            in_short[...] = start_grad.astype(bfloat)
-            for s in range(per):
-                sums_ref[pl.ds(step * per + s, 1), :] = jnp.sum(
-                    start_grad[s * 128 : (s + 1) * 128], axis=0, keepdims=True
-                )
-        else:
-            in_long[...] = start_grad.astype(bfloat)
-            sums_ref[pl.ds(per * half + step - half, 1), :] = jnp.sum(start_grad, axis=0, keepdims=True)
-
-    start_rows(step, half, short_ref, long_ref, embed_ref, emit)
-
-
-def forward_down(half, middle_ref, active_ref, small_ref, down, out_short, out_long):
+        out, length = (in_short, SHORT) if is_short else (in_long, LONG)
+        out[...] = start_grad.astype(bfloat)
+        number = step * (size // SHORT) if is_short else half * (size // SHORT) + (step - half) * (size // LONG)
+        for s in range(size // length):
+            sums_ref[pl.ds(number + s, 1), :] = jnp.sum(
+                start_grad[s * length : (s + 1) * length], axis=0, keepdims=True
+            )
+
+    start_rows(step, half, short_ref.shape[0], short_ref, long_ref, embed_ref, emit)
+
+
+def forward_down(half, n, place_ref, middle_ref, active_ref, small_ref, *refs):
+    downs, (out_short, out_long, down) = refs[:n], refs[n:]
     step = pl.program_id(0)
+
+    @pl.when(step == 0)
+    def _():
+        assemble_lines(place_ref[0], downs, down)
+
     result = middle_ref[...] + dot(active_ref[...], down[...], NN) + small_ref[7:8, :]
 
     @pl.when(step < half)
@@ -539,6 +551,8 @@
 
     tile = (TILE, width)
     short_spec, long_spec = of_short(tile, half), of_long(tile, half)
+    band, half_band = (BAND, width), short.shape[0] // BAND
+    short_band, long_band = of_short(band, half_band), of_long(band, half_band)
     probs_short_spec = of_short((TILE // 128, heads, 128, 128), half)
     probs_long_spec = of_long((1, heads, TILE, TILE), half)
     shape = jax.ShapeDtypeStruct
@@ -573,33 +587,32 @@
         down_line = jnp.stack(down_line)
         down_line, up_pieces = tie(down_line, up_pieces)
         down_core, down_other = across(down_line, 1), across(down_line, 2)
-    middle, second, active, slope, up_whole = pl.pallas_call(
-        functools.partial(forward_up, half, width, hidden, len(up_pieces)),
-        grid=(grid,),
+    middle, second, active, slope = pl.pallas_call(
+        functools.partial(forward_up, half_band, width, hidden, len(up_pieces)),
+        grid=(total // BAND,),
         in_specs=[
             on_scalars(),
-            short_spec,
-            long_spec,
+            short_band,
+            long_band,
             kept((8, width)),
             kept((8, width)),
             kept((1, hidden)),
-            by_step(tile),
+            by_step(band),
         ]
         + [resident(p.shape) for p in up_pieces],
         out_specs=[
-            by_step(tile),
-            by_step(tile),
-            by_step((TILE, hidden)),
-            by_step((TILE, hidden)),
-            kept((width, width + hidden)),
+            by_step(band),
+            by_step(band),
+            by_step((BAND, hidden)),
+            by_step((BAND, hidden)),
         ],
         out_shape=[
             shape((total, width), single),
             shape((total, width), bfloat),
             shape((total, hidden), bfloat),
             shape((total, hidden), bfloat),
-            shape((width, width + hidden), bfloat),
-        ],
+        ],
+        scratch_shapes=[pltpu.VMEM((width, width + hidden), bfloat)],
         compiler_params=params(),
         cost_estimate=cost(2 * total * width * (width + hidden) * 2, total * width * 20),
         name="forward_up",
@@ -617,6 +630,7 @@
         ],
         out_specs=by_step((width, width)),
         out_shape=shape((hidden, width), bfloat),
+        scratch_shapes=[pltpu.VMEM((total, width), bfloat)],
         compiler_params=params(),
         cost_estimate=cost(2 * total * width * hidden, total * width * 12),
         name="down_weight_back",
@@ -626,25 +640,23 @@
         down_terms, slope, down_other = tie(down_terms, slope, down_other)
         down_pieces = [down_line, down_other, down_core, across(down_other, 1)]
 
-    hidden_grad, branch, middle_grad, mixed_grad, down_whole, vectors, bias_grad = pl.pallas_call(
-        functools.partial(feed_back, half, width, hidden, len(down_pieces)),
-        grid=(grid,),
+    hidden_grad, branch, middle_grad, mixed_grad, vectors, bias_grad = pl.pallas_call(
+        functools.partial(feed_back, half_band, width, hidden, len(down_pieces)),
+        grid=(total // BAND,),
         in_specs=[
             on_scalars(),
-            short_spec,
-            long_spec,
-            by_step((TILE, hidden)),
-            by_step(tile),
+            short_band,
+            long_band,
+            by_step((BAND, hidden)),
+            by_step(band),
             kept((8, width)),
-            resident(up_whole.shape),
         ]
-        + [resident(p.shape) for p in down_pieces],
+        + [resident(p.shape) for p in [*up_pieces, *down_pieces]],
         out_specs=[
-            by_step((TILE, hidden)),
-            by_step(tile),
-            by_step(tile),
-            by_step(tile),
-            kept((hidden, width)),
+            by_step((BAND, hidden)),
+            by_step(band),
+            by_step(band),
+            by_step(band),
             kept((8, width)),
             kept((1, hidden)),
         ],
@@ -653,15 +665,18 @@
             shape((total, width), bfloat),
             shape((total, width), single),
             shape((total, width), bfloat),
-            shape((hidden, width), bfloat),
             shape((8, width), single),
             shape((1, hidden), single),
         ],
-        scratch_shapes=[pltpu.VMEM(tile, bfloat)],
+        scratch_shapes=[
+            pltpu.VMEM((width, width + hidden), bfloat),
+            pltpu.VMEM((hidden, width), bfloat),
+            pltpu.VMEM(band, bfloat),
+        ],
         compiler_params=params(),
         cost_estimate=cost(2 * total * width * (width + 2 * hidden), total * width * 30),
         name="feed_back",
-    )(place, up_short, up_long, slope, middle, smalls, up_whole, *down_pieces)
+    )(place, up_short, up_long, slope, middle, smalls, *up_pieces, *down_pieces)
 
     tiles = hidden // width
     column = lambda last: pl.BlockSpec((total, width), lambda i: (0, jnp.minimum(i, last)))
@@ -678,6 +693,7 @@
         ],
         out_specs=[out_block] * 2,
         out_shape=[shape((slots, whole_rows, width + hidden), bfloat)] * 2,
+        scratch_shapes=[pltpu.VMEM((width, total), bfloat)],
         compiler_params=params(),
         cost_estimate=cost(2 * total * width * (width + hidden), total * width * 20),
         name="up_weight_back",
@@ -702,6 +718,7 @@
         in_specs=[on_scalars(), kept((total, width)), column(2)],
         out_specs=[out_block] * 2,
         out_shape=[shape((slots, whole_rows, 3 * width), bfloat)] * 2,
+        scratch_shapes=[pltpu.VMEM((width, total), bfloat)],
         compiler_params=params(),
         cost_estimate=cost(2 * total * width * 3 * width, total * width * 16),
         name="qkv_weight_back",
@@ -711,19 +728,19 @@
     (middle_grad,) = qkv_sum.over_y(middle_grad)
 
     grad_short, grad_long, last_vectors, sums = pl.pallas_call(
-        functools.partial(start_back, half, width, n),
-        grid=(grid,),
+        functools.partial(start_back, half_band, width, n),
+        grid=(total // BAND,),
         in_specs=[
             on_scalars(),
-            short_spec,
-            long_spec,
+            short_band,
+            long_band,
             kept((8, width)),
             kept((8, width)),
-            by_step(tile),
-            by_step((TILE, 3 * width)),
+            by_step(band),
+            by_step((BAND, 3 * width)),
         ]
         + first_specs,
-        out_specs=[short_spec, long_spec, kept((8, width)), kept((8, width))],
+        out_specs=[short_band, long_band, kept((8, width)), kept((8, width))],
         out_shape=[
             shape(short.shape, bfloat),
             shape(long.shape, bfloat),
@@ -735,18 +752,6 @@
         cost_estimate=cost(2 * total * width * 3 * width, total * width * 30),
         name="start_back",
     )(place, short, long, embed, smalls, middle_grad, projected_grad, *first_pieces)
-    middle, sums = tie(middle, sums)
-    output_short, output_long = pl.pallas_call(
-        functools.partial(forward_down, half),
-        grid=(grid,),
-        in_specs=[by_step(tile), by_step((TILE, hidden)), kept((8, width)), resident(down_whole.shape)],
-        out_specs=[short_spec, long_spec],
-        out_shape=[shape(short.shape, bfloat), shape(long.shape, bfloat)],
-        compiler_params=params(),
-        cost_estimate=cost(2 * total * width * hidden, total * width * 30),
-        name="forward_down",
-    )(middle, active, smalls, down_whole)
-
     owners = width // rows
     both = jnp.concatenate([vectors[:4], last_vectors[:4], sums[:marks]], axis=0)
     lines = both.shape[0]
@@ -755,7 +760,24 @@
     packed = jnp.concatenate([packed, bias_grad.reshape(owners, -1), own_steps], axis=1)
     packed = jnp.concatenate([packed, packed], axis=0)
     came = lax.all_to_all(packed, ("rep", "fsdp"), 0, 0, tiled=True)
-    output_short, came, up_sum.keep = qkv_sum.over_z(output_short, came, up_sum.keep)
+    if count == SHARDS:
+        up_sum.came, qkv_sum.came, middle, came = tie(up_sum.came, qkv_sum.came, middle, came)
+    middle, down_share = up_sum.over_x(middle, down_share)
+    down_other = to_replica(down_share)
+    (middle,) = qkv_sum.over_z(middle)
+    output_short, output_long = pl.pallas_call(
+        functools.partial(forward_down, half_band, len(down_pieces)),
+        grid=(total // BAND,),
+        in_specs=[on_scalars(), by_step(band), by_step((BAND, hidden)), kept((8, width))]
+        + [resident(p.shape) for p in down_pieces],
+        out_specs=[short_band, long_band],
+        out_shape=[shape(short.shape, bfloat), shape(long.shape, bfloat)],
+        scratch_shapes=[pltpu.VMEM((hidden, width), bfloat)],
+        compiler_params=params(),
+        cost_estimate=cost(2 * total * width * hidden, total * width * 30),
+        name="forward_down",
+    )(place, middle, active, smalls, *down_pieces)
+
     vector_sums = jnp.sum(came[:, : 8 * rows], axis=0).reshape(8, rows)
     ends = lines * rows + hidden // owners
     up_bias_grad = jnp.sum(came[:, lines * rows : ends], axis=0)
@@ -769,10 +791,9 @@
         precision=lax.Precision.HIGHEST,
         preferred_element_type=single,
     )
-    up_sum.over_x()
-    qkv_sum.over_x()
+    down_other, up_sum.other = qkv_sum.over_x(down_other, up_sum.other)
     up_grads, qkv_weight_grad = up_sum.result(), qkv_sum.result()
-    down_weight_grad = added(down_share, to_replica(down_share))
+    down_weight_grad = added(down_share, down_other)
     return (
         output_short.reshape(input_short.shape),
         output_long.reshape(input_long.shape),

time: 337 us -> 322 us (0.955)
  waiting for transfers between devices: 85.8 us -> 61.5 us
  blocking collectives: 0 us -> 23.1 us
  starting transfers between devices: 51 us -> 43.3 us
  Pallas kernels: 145 us -> 141 us
    ppermute x37, waiting for transfers between devices: 61.1 us -> 35.5 us  [across(): return lax.ppermute(array, 'fsdp', flip(bit))]
    all_to_all x0 -> x1, blocking collectives: none -> 23.1 us  [shards(): came = lax.all_to_all(packed, ('rep', 'fsdp'), 0, 0, tiled=True)]
    all_to_all x1 -> x0, starting transfers between devices: 4.87 us -> none  [shards(): came = lax.all_to_all(packed, ('rep', 'fsdp'), 0, 0, tiled=True)]
  transfers between devices with their start and end apart: 44 -> 43, of which waited for: 16 -> 13; matrix products, arithmetic and copies ran while one was open for 9% -> 8% of each run, Pallas kernels for 44% -> 44%
where the time goes in v1:
time: 322 us; the launch traced here: 318 us
  Pallas kernels  141 us (44%)
  waiting for transfers between devices  61.5 us (19%)
  starting transfers between devices  43.3 us (13%)
  blocking collectives  23.1 us (7%)
  other arithmetic  20 us (6%)
  between operations  15.4 us (5%)
  local copies, waits for them, and re-layouts  12 us (4%)
    ppermute x37, waiting for transfers between devices, across(): return lax.ppermute(array, 'fsdp', flip(bit))  35.5 us
    ppermute x37, starting transfers between devices, across(): return lax.ppermute(array, 'fsdp', flip(bit))  28.8 us
    pallas_call x1, Pallas kernels, shards(): pl.pallas_call(functools.partial(forward_attention, half, width, n), grid...  28.4 us
    all_to_all x1, blocking collectives, shards(): came = lax.all_to_all(packed, ('rep', 'fsdp'), 0, 0, tiled=True)  23.1 us
    pallas_call x1, Pallas kernels, shards(): pl.pallas_call(functools.partial(feed_back, half_band, width, hidden, len...  22.4 us
    pallas_call x1, Pallas kernels, shards(): pl.pallas_call(functools.partial(backward_attention, half, width), grid=(...  19.8 us
    pallas_call x1, Pallas kernels, shards(): pl.pallas_call(functools.partial(forward_up, half_band, width, hidden, le...  17.8 us
    pallas_call x1, Pallas kernels, shards(): pl.pallas_call(functools.partial(weight_back, (1, tiles)), grid=(tiles +...  14 us
  transfers between devices with their start and end apart: 43, of which 13 were waited for; matrix products, arithmetic and copies ran while one was open for 8% of the time, Pallas kernels for 44%

profile of v1, /device:TPU:16, one launch (start us, length us, event | category | flops | bytes accessed | tf_op | source)
XLA Modules:
  0.0 318.0 jit_solution(7701189017971394644)
XLA Ops:
  7.3 1.1 convert_element_type.226.refs_0_
  8.4 1.6 collective-permute-start.3
  10.5 3.5 %collective-permute-start.1 = (bf16[48,2304]{1,0:T(8,128)(2,1)S(1)}, bf16[48,2304]{1,0:T(8,128)(2,1)S(1)}, u32[]{:S(2)}, u32[]{:S(2)}) collective-permute-start(bf16[48,2304]{1,0:T(8,128)(2,1)S(1)} %convert_element_type.226.refs_0_), channel_id=1, source_target_pairs={{0,8},{1,9},{2,10},{3,11},{4,12},{5,13},{6,14},{7,15},{8,0},{9,1},... | collective-permute-start | bytes 663560 | tf_op jit(solution)/shard_map/ppermute | solution.py:396
  15.3 5.7 %all-to-all-start = ((s32[16,1,6]{2,1,0:T(1,128)}), s32[16,1,6]{2,1,0:T(1,128)S(1)}, u32[]{:S(2)}, u32[]{:S(2)}) async-start(s32[16,1,6]{2,1,0:T(1,128)} %broadcast_in_dim.11), calls=%async_computation | async-start | bytes 16384 | tf_op jit(solution)/shard_map/all_to_all | solution.py:518
  21.0 0.9 convert.34
  21.9 1.1 convert.35
  23.4 7.8 %all-to-all-done = s32[16,1,6]{2,1,0:T(1,128)S(1)} async-done(((s32[16,1,6]{2,1,0:T(1,128)}), s32[16,1,6]{2,1,0:T(1,128)S(1)}, u32[]{:S(2)}, u32[]{:S(2)}) %all-to-all-start) | async-done | bytes 416 | tf_op jit(solution)/shard_map/all_to_all | solution.py:518
  31.9 3.5 %collective-permute-start.5 = (bf16[48,3840]{1,0:T(8,128)(2,1)S(1)}, bf16[48,3840]{1,0:T(8,128)(2,1)}, u32[]{:S(2)}, u32[]{:S(2)}) collective-permute-start(bf16[48,3840]{1,0:T(8,128)(2,1)S(1)} %pad_maximum_fusion.2), channel_id=1, source_target_pairs={{0,8},{1,9},{2,10},{3,11},{4,12},{5,13},{6,14},{7,15},{8,0},{9,1},... | collective-permute-start | bytes 1105928 | tf_op jit(solution)/shard_map/ppermute | solution.py:396
  35.5 1.4 collective-permute-start.7
  38.1 5.8 %collective-permute-done.7.refs_6_ = bf16[48,2304]{1,0:T(8,128)(2,1)S(1)} collective-permute-done((bf16[48,2304]{1,0:T(8,128)(2,1)S(1)}, bf16[48,2304]{1,0:T(8,128)(2,1)S(1)}, u32[]{:S(2)}, u32[]{:S(2)}) %collective-permute-start.7) | collective-permute-done | bytes 221216 | tf_op jit(solution)/shard_map/ppermute | solution.py:396
  44.0 1.4 collective-permute-start.9
  47.3 5.8 %all-to-all-start.1 = ((bf16[16,2,432]{2,1,0:T(2,128)(2,1)}), bf16[16,2,432]{2,1,0:T(2,128)(2,1)S(1)}, u32[]{:S(2)}, u32[]{:S(2)}) async-start(bf16[16,2,432]{2,1,0:T(2,128)(2,1)} %reshape.176), calls=%async_computation.1 | async-start | bytes 65536 | tf_op jit(solution)/shard_map/all_to_all | solution.py:527
  53.1 14.0 %all-to-all-done.1 = bf16[16,2,432]{2,1,0:T(2,128)(2,1)S(1)} async-done(((bf16[16,2,432]{2,1,0:T(2,128)(2,1)}), bf16[16,2,432]{2,1,0:T(2,128)(2,1)S(1)}, u32[]{:S(2)}, u32[]{:S(2)}) %all-to-all-start.1) | async-done | bytes 27680 | tf_op jit(solution)/shard_map/all_to_all | solution.py:527
  70.4 1.4 pad_maximum_fusion.refs_0_
  73.5 2.5 collective-permute-done.16.refs_1_
  78.4 3.3 %collective-permute-start.12 = (bf16[192,768]{1,0:T(8,128)(2,1)S(1)}, bf16[192,768]{1,0:T(8,128)(2,1)}, u32[]{:S(2)}, u32[]{:S(2)}) collective-permute-start(bf16[192,768]{1,0:T(8,128)(2,1)S(1)} %convert_element_type.231), channel_id=1, source_target_pairs={{0,8},{1,9},{2,10},{3,11},{4,12},{5,13},{6,14},{7,15},{8,0},{9,1},... | collective-permute-start | bytes 884744 | tf_op jit(solution)/shard_map/ppermute | solution.py:396
  82.5 28.4 %forward_attention.1 = (bf16[1024,768]{1,0:T(8,128)(2,1)}, bf16[1024,2304]{1,0:T(8,128)(2,1)}, bf16[4,12,128,128]{3,2,1,0:T(8,128)(2,1)}, bf16[2,12,256,256]{3,2,1,0:T(8,128)(2,1)}, bf16[1024,768]{1,0:T(8,128)(2,1)}) custom-call(s32[1]{0:T(128)} %bitcast.place_ref, bf16[512,768]{1,0:T(8,128)(2,1)} %bitcast.50, bf16[512,768]{1,0:T(8,128)(2,1)} %bitcast.53, ...), custom_call_target="tpu_custom_call" | custom-call | flops 1024 | bytes 1024 | tf_op jit(solution)/shard_map/forward_attention/pallas_call | solution.py:559
  111.0 1.7 pad_maximum_fusion.1.refs_4_.refs_0_
  112.8 1.7 collective-permute-done.23.refs_3_
  115.6 17.8 %forward_up.1 = (f32[1024,768]{1,0:T(8,128)}, bf16[1024,768]{1,0:T(8,128)(2,1)}, bf16[1024,3072]{1,0:T(8,128)(2,1)}, bf16[1024,3072]{1,0:T(8,128)(2,1)}) custom-call(s32[1]{0:T(128)} %bitcast.place_ref, bf16[512,768]{1,0:T(8,128)(2,1)} %bitcast.51, bf16[512,768]{1,0:T(8,128)(2,1)} %bitcast.54, f32[8,768]{1,0:T(8,128)} %pad.4.embed_ref, ...), custom_call_target="tpu_custom_call" | custom-call | flops 1024 | bytes 1024 | tf_op jit(solution)/shard_map/forward_up/pallas_call | solution.py:590
  133.4 9.3 %down_weight_back.1 = bf16[3072,768]{1,0:T(8,128)(2,1)} custom-call(bf16[1024,3072]{1,0:T(8,128)(2,1)} %get-tuple-element.164.active_ref, bf16[512,768]{1,0:T(8,128)(2,1)} %bitcast.56, bf16[512,768]{1,0:T(8,128)(2,1)} %bitcast.58), custom_call_target="tpu_custom_call" | custom-call | flops 1024 | bytes 1024 | tf_op jit(solution)/shard_map/down_weight_back/pallas_call | solution.py:623
  143.3 2.7 collective-permute-done.25.refs_6_.refs_2_
  146.0 1.6 collective-permute-done.26.refs_7_.refs_3_
  147.6 1.1 copy-done.5
  148.7 22.4 %feed_back.1 = (bf16[1024,3072]{1,0:T(8,128)(2,1)}, bf16[1024,768]{1,0:T(8,128)(2,1)}, f32[1024,768]{1,0:T(8,128)}, bf16[1024,768]{1,0:T(8,128)(2,1)}, f32[8,768]{1,0:T(8,128)}, /*index=5*/f32[1,3072]{1,0:T(1,128)}) custom-call(s32[1]{0:T(128)} %bitcast.place_ref, bf16[512,768]{1,0:T(8,128)(2,1)} %bitcast.57, bf16[512,768]{1,0:T(8,128)(2,1)} %bitcast.59, ...), custom_call_target="tpu_custom_call" | custom-call | flops 1024 | bytes 1024 | tf_op jit(solution)/shard_map/feed_back/pallas_call | solution.py:643
  171.1 14.0 %up_weight_back.1 = (bf16[8,48,3840]{2,1,0:T(8,128)(2,1)}, bf16[8,48,3840]{2,1,0:T(8,128)(2,1)}) custom-call(s32[1]{0:T(128)} %bitcast.place_ref, bf16[1024,768]{1,0:T(8,128)(2,1)} %get-tuple-element.151.mixed_ref.refs_0_, bf16[1024,768]{1,0:T(8,128)(2,1)} %get-tuple-element.163.refs_1_, bf16[1024,768]{1,0:T(8,128)(2,1)} %get-tuple-element.170.refs_2_, ...), custom_call_target="tpu_custom_call" | custom-call | flops 1024 | bytes 1024 | tf_op jit(solution)/shard_map/up_weight_back/pallas_call | solution.py:684
  185.2 5.5 %collective-permute-done.27 = bf16[8,48,3840]{2,1,0:T(8,128)(2,1)S(1)} collective-permute-done((bf16[8,48,3840]{2,1,0:T(8,128)(2,1)}, bf16[8,48,3840]{2,1,0:T(8,128)(2,1)S(1)}, u32[]{:S(2)}, u32[]{:S(2)}) %collective-permute-start.27) | collective-permute-done | bytes 2949152 | tf_op jit(solution)/shard_map/ppermute | solution.py:396
  190.7 2.5 add_convert_fusion
  193.7 19.8 %backward_attention.1.refs_1_.grad_ref = bf16[1024,2304]{1,0:T(8,128)(2,1)} custom-call(bf16[1024,2304]{1,0:T(8,128)(2,1)} %get-tuple-element.181.qkv_ref, bf16[1024,768]{1,0:T(8,128)(2,1)} %get-tuple-element.182.mixed_grad_ref, bf16[4,12,128,128]{3,2,1,0:T(8,128)(2,1)} %get-tuple-element.183.probs_short, bf16[2,12,256,256]{3,2,1,0:T(8,128)(2,1)} %get-tuple-element.184.probs_long), custom_call_target="tpu_custom_call" | custom-call | flops 1024 | bytes 1024 | tf_op jit(solution)/shard_map/backward_attention/pallas_call | solution.py:704
  213.5 8.6 %qkv_weight_back.1 = (bf16[8,48,2304]{2,1,0:T(8,128)(2,1)}, bf16[8,48,2304]{2,1,0:T(8,128)(2,1)}) custom-call(s32[1]{0:T(128)} %bitcast.place_ref, bf16[1024,768]{1,0:T(8,128)(2,1)} %get-tuple-element.180.refs_0_, bf16[1024,2304]{1,0:T(8,128)(2,1)} %backward_attention.1.refs_1_.grad_ref), custom_call_target="tpu_custom_call" | custom-call | flops 1024 | bytes 1024 | tf_op jit(solution)/shard_map/qkv_weight_back/pallas_call | solution.py:715
  222.1 8.8 %collective-permute-done.28 = bf16[4,48,3840]{2,1,0:T(8,128)(2,1)} collective-permute-done((bf16[4,48,3840]{2,1,0:T(8,128)(2,1)S(1)}, bf16[4,48,3840]{2,1,0:T(8,128)(2,1)}, u32[]{:S(2)}, u32[]{:S(2)}) %collective-permute-start.28) | collective-permute-done | bytes 1474592 | tf_op jit(solution)/shard_map/ppermute | solution.py:396
  230.9 2.8 fusion.5
  233.7 1.4 add_convert_fusion.2
  236.8 1.5 collective-permute-start.30
  238.9 1.4 collective-permute-start.32
  240.3 10.5 %start_back.1 = (bf16[512,768]{1,0:T(8,128)(2,1)}, bf16[512,768]{1,0:T(8,128)(2,1)}, f32[8,768]{1,0:T(8,128)}, f32[8,768]{1,0:T(8,128)}) custom-call(s32[1]{0:T(128)} %bitcast.place_ref, bf16[512,768]{1,0:T(8,128)(2,1)} %bitcast.52, bf16[512,768]{1,0:T(8,128)(2,1)} %bitcast.55, f32[8,768]{1,0:T(8,128)} %pad.4.embed_ref, f32[8,768]{1,0:T(8,128)} %slice.153.small_ref, ...), custom_call_target="tpu_custom_call" | custom-call | flops 1024 | bytes 1024 | tf_op jit(solution)/shard_map/start_back/pallas_call | solution.py:730
  252.8 23.1 %all_to_all.30 = f32[32,1,870]{2,1,0:T(1,128)S(1)} all-to-all(f32[32,1,870]{2,1,0:T(1,128)S(1)} %copy.58), channel_id=1, replica_groups=mesh['rep'=2,'fsdp'=16] {'rep','fsdp'}, dimensions={0} | all-to-all | bytes 222720 | tf_op jit(solution)/shard_map/all_to_all | solution.py:762
  276.0 1.2 add_convert_fusion.4
  278.2 1.2 fusion
  279.4 1.2 collective-permute-start.34
  280.6 0.9 collective-permute-start.35
  281.6 1.4 collective-permute-start.36
  283.0 1.5 collective-permute-start.37
  284.4 10.4 %forward_down.1 = (bf16[512,768]{1,0:T(8,128)(2,1)}, bf16[512,768]{1,0:T(8,128)(2,1)}) custom-call(s32[1]{0:T(128)} %bitcast.place_ref, f32[1024,768]{1,0:T(8,128)} %get-tuple-element.222.middle_ref, bf16[1024,3072]{1,0:T(8,128)(2,1)} %get-tuple-element.164.active_ref, f32[8,768]{1,0:T(8,128)} %slice.153.small_ref, bf16[4,192,768]{2,1,0:T(8,128)(2,1)} %copy-done.1, ...), custom_call_target="tpu_custom_call" | custom-call | flops 1024 | bytes 1024 | tf_op jit(solution)/shard_map/forward_down/pallas_call | solution.py:768
  296.9 5.2 %collective-permute-done.36 = bf16[48,2304]{1,0:T(8,128)(2,1)S(1)} collective-permute-done((bf16[48,2304]{1,0:T(8,128)(2,1)S(1)}, bf16[48,2304]{1,0:T(8,128)(2,1)S(1)}, u32[]{:S(2)}, u32[]{:S(2)}) %collective-permute-start.36) | collective-permute-done | bytes 221216 | tf_op jit(solution)/shard_map/ppermute | solution.py:396
  303.8 1.0 collective-permute-start.39
  304.8 0.9 convert_add_fusion.1
  305.7 4.2 %collective-permute-done.39 = bf16[48,2304]{1,0:T(8,128)(2,1)S(1)} collective-permute-done((bf16[48,2304]{1,0:T(8,128)(2,1)S(1)}, bf16[48,2304]{1,0:T(8,128)(2,1)S(1)}, u32[]{:S(2)}, u32[]{:S(2)}) %collective-permute-start.39) | collective-permute-done | bytes 221216 | tf_op jit(solution)/shard_map/ppermute | solution.py:400
  (204 shorter events, 26.1 us)
Async XLA Ops:
  7.3 45.8 %copy-start.25 = (f32[192,768]{1,0:T(8,128)S(1)}, f32[192,768]{1,0:T(8,128)}, u32[]{:S(2)}) copy-start(f32[192,768]{1,0:T(8,128)} %param.38) | copy-start | bytes 1769476
  8.4 64.5 %copy-start.6 = (bf16[48,2304]{1,0:T(8,128)(2,1)}, bf16[48,2304]{1,0:T(8,128)(2,1)S(1)}, u32[]{:S(2)}) copy-start(bf16[48,2304]{1,0:T(8,128)(2,1)S(1)} %convert_element_type.226.refs_0_) | copy-start | bytes 663556
  8.4 22.9 %collective-permute-start.3 = (bf16[48,2304]{1,0:T(8,128)(2,1)S(1)}, bf16[48,2304]{1,0:T(8,128)(2,1)S(1)}, u32[]{:S(2)}, u32[]{:S(2)}) collective-permute-start(bf16[48,2304]{1,0:T(8,128)(2,1)S(1)} %convert_element_type.226.refs_0_), channel_id=1, source_target_pairs={{0,2},{1,3},{2,0},{3,1},{4,6},{5,7},{6,4},{7,5},{8,10},{9,11},{10,... | collective-permute-start | bytes 663560 | tf_op jit(solution)/shard_map/ppermute | solution.py:396
  10.0 21.3 %collective-permute-start.2 = (bf16[48,2304]{1,0:T(8,128)(2,1)S(1)}, bf16[48,2304]{1,0:T(8,128)(2,1)S(1)}, u32[]{:S(2)}, u32[]{:S(2)}) collective-permute-start(bf16[48,2304]{1,0:T(8,128)(2,1)S(1)} %convert_element_type.226.refs_0_), channel_id=1, source_target_pairs={{0,12},{1,13},{2,14},{3,15},{4,8},{5,9},{6,10},{7,11},{8,4},{9,5},... | collective-permute-start | bytes 663560 | tf_op jit(solution)/shard_map/ppermute | solution.py:396
  10.5 20.9 %collective-permute-start.1 = (bf16[48,2304]{1,0:T(8,128)(2,1)S(1)}, bf16[48,2304]{1,0:T(8,128)(2,1)S(1)}, u32[]{:S(2)}, u32[]{:S(2)}) collective-permute-start(bf16[48,2304]{1,0:T(8,128)(2,1)S(1)} %convert_element_type.226.refs_0_), channel_id=1, source_target_pairs={{0,8},{1,9},{2,10},{3,11},{4,12},{5,13},{6,14},{7,15},{8,0},{9,1},... | collective-permute-start | bytes 663560 | tf_op jit(solution)/shard_map/ppermute | solution.py:396
  14.0 17.4 %collective-permute-start = (bf16[48,2304]{1,0:T(8,128)(2,1)S(1)}, bf16[48,2304]{1,0:T(8,128)(2,1)S(1)}, u32[]{:S(2)}, u32[]{:S(2)}) collective-permute-start(bf16[48,2304]{1,0:T(8,128)(2,1)S(1)} %convert_element_type.226.refs_0_), channel_id=1, source_target_pairs={{0,4},{1,5},{2,6},{3,7},{4,0},{5,1},{6,2},{7,3},{8,12},{9,13},{10,... | collective-permute-start | bytes 663560 | tf_op jit(solution)/shard_map/ppermute | solution.py:396
  15.3 15.9 %all-to-all-start = ((s32[16,1,6]{2,1,0:T(1,128)}), s32[16,1,6]{2,1,0:T(1,128)S(1)}, u32[]{:S(2)}, u32[]{:S(2)}) async-start(s32[16,1,6]{2,1,0:T(1,128)} %broadcast_in_dim.11), calls=%async_computation | async-start | bytes 16384 | tf_op jit(solution)/shard_map/all_to_all | solution.py:518
  31.3 40.5 %copy-start.9 = (bf16[48,2304]{1,0:T(8,128)(2,1)}, bf16[48,2304]{1,0:T(8,128)(2,1)S(1)}, u32[]{:S(2)}) copy-start(bf16[48,2304]{1,0:T(8,128)(2,1)S(1)} %collective-permute-done.3.refs_2_) | copy-start | bytes 663556
  31.3 40.5 %copy-start.10 = (bf16[48,2304]{1,0:T(8,128)(2,1)}, bf16[48,2304]{1,0:T(8,128)(2,1)S(1)}, u32[]{:S(2)}) copy-start(bf16[48,2304]{1,0:T(8,128)(2,1)S(1)} %collective-permute-done.2.refs_12_) | copy-start | bytes 663556
  31.3 40.5 %copy-start.11 = (bf16[48,2304]{1,0:T(8,128)(2,1)}, bf16[48,2304]{1,0:T(8,128)(2,1)S(1)}, u32[]{:S(2)}) copy-start(bf16[48,2304]{1,0:T(8,128)(2,1)S(1)} %collective-permute-done.1.refs_8_) | copy-start | bytes 663556
  31.4 38.2 %collective-permute-start.6 = (bf16[48,3840]{1,0:T(8,128)(2,1)S(1)}, bf16[48,3840]{1,0:T(8,128)(2,1)S(1)}, u32[]{:S(2)}, u32[]{:S(2)}) collective-permute-start(bf16[48,3840]{1,0:T(8,128)(2,1)S(1)} %pad_maximum_fusion.2), channel_id=1, source_target_pairs={{0,12},{1,13},{2,14},{3,15},{4,8},{5,9},{6,10},{7,11},{8,4},{9,5},... | collective-permute-start | bytes 1105928 | tf_op jit(solution)/shard_map/ppermute | solution.py:396
  31.9 37.7 %collective-permute-start.5 = (bf16[48,3840]{1,0:T(8,128)(2,1)S(1)}, bf16[48,3840]{1,0:T(8,128)(2,1)}, u32[]{:S(2)}, u32[]{:S(2)}) collective-permute-start(bf16[48,3840]{1,0:T(8,128)(2,1)S(1)} %pad_maximum_fusion.2), channel_id=1, source_target_pairs={{0,8},{1,9},{2,10},{3,11},{4,12},{5,13},{6,14},{7,15},{8,0},{9,1},... | collective-permute-start | bytes 1105928 | tf_op jit(solution)/shard_map/ppermute | solution.py:396
  35.4 34.3 %collective-permute-start.4 = (bf16[48,3840]{1,0:T(8,128)(2,1)S(1)}, bf16[48,3840]{1,0:T(8,128)(2,1)}, u32[]{:S(2)}, u32[]{:S(2)}) collective-permute-start(bf16[48,3840]{1,0:T(8,128)(2,1)S(1)} %pad_maximum_fusion.2), channel_id=1, source_target_pairs={{0,4},{1,5},{2,6},{3,7},{4,0},{5,1},{6,2},{7,3},{8,12},{9,13},{10,... | collective-permute-start | bytes 1105928 | tf_op jit(solution)/shard_map/ppermute | solution.py:396
  35.5 8.4 %collective-permute-start.7 = (bf16[48,2304]{1,0:T(8,128)(2,1)S(1)}, bf16[48,2304]{1,0:T(8,128)(2,1)S(1)}, u32[]{:S(2)}, u32[]{:S(2)}) collective-permute-start(bf16[48,2304]{1,0:T(8,128)(2,1)S(1)} %collective-permute-done.refs_4_), channel_id=1, source_target_pairs={{0,2},{1,3},{2,0},{3,1},{4,6},{5,7},{6,4},{7,5},{8,10},{9,11},{10,... | collective-permute-start | bytes 663560 | tf_op jit(solution)/shard_map/ppermute | solution.py:396
  37.5 32.1 %collective-permute-start.8 = (bf16[48,2304]{1,0:T(8,128)(2,1)S(1)}, bf16[48,2304]{1,0:T(8,128)(2,1)S(1)}, u32[]{:S(2)}, u32[]{:S(2)}) collective-permute-start(bf16[48,2304]{1,0:T(8,128)(2,1)S(1)} %collective-permute-done.1.refs_8_), channel_id=1, source_target_pairs={{0,2},{1,3},{2,0},{3,1},{4,6},{5,7},{6,4},{7,5},{8,10},{9,11},{10,... | collective-permute-start | bytes 663560 | tf_op jit(solution)/shard_map/ppermute | solution.py:396
  44.0 25.6 %collective-permute-start.9 = (bf16[48,2304]{1,0:T(8,128)(2,1)S(1)}, bf16[48,2304]{1,0:T(8,128)(2,1)}, u32[]{:S(2)}, u32[]{:S(2)}) collective-permute-start(bf16[48,2304]{1,0:T(8,128)(2,1)S(1)} %collective-permute-done.2.refs_12_), channel_id=1, source_target_pairs={{0,2},{1,3},{2,0},{3,1},{4,6},{5,7},{6,4},{7,5},{8,10},{9,11},{10,... | collective-permute-start | bytes 663560 | tf_op jit(solution)/shard_map/ppermute | solution.py:396
  47.3 19.8 %all-to-all-start.1 = ((bf16[16,2,432]{2,1,0:T(2,128)(2,1)}), bf16[16,2,432]{2,1,0:T(2,128)(2,1)S(1)}, u32[]{:S(2)}, u32[]{:S(2)}) async-start(bf16[16,2,432]{2,1,0:T(2,128)(2,1)} %reshape.176), calls=%async_computation.1 | async-start | bytes 65536 | tf_op jit(solution)/shard_map/all_to_all | solution.py:527
  53.0 177.9 %reduce-scatter.2.cloned.1.call-start = ((), (), s32[]{:S(2)}) async-start(), calls=%async_computation.4 | async-start | bytes 5013504 | tf_op jit(solution)/shard_map/reduce_scatter | solution.py:638
  69.6 2.3 collective-permute-start.10
  71.9 39.0 %collective-permute-start.15 = (bf16[4,48,3840]{2,1,0:T(8,128)(2,1)S(1)}, bf16[4,48,3840]{2,1,0:T(8,128)(2,1)S(1)}, u32[]{:S(2)}, u32[]{:S(2)}) collective-permute-start(bf16[4,48,3840]{2,1,0:T(8,128)(2,1)S(1)} %pad_maximum_fusion.refs_0_), channel_id=1, source_target_pairs={{0,1},{1,0},{2,3},{3,2},{4,5},{5,4},{6,7},{7,6},{8,9},{9,8},{10,11... | collective-permute-start | bytes 4423688 | tf_op jit(solution)/shard_map/ppermute | solution.py:396
  72.5 38.4 %collective-permute-start.14 = (bf16[4,48,3840]{2,1,0:T(8,128)(2,1)S(1)}, bf16[4,48,3840]{2,1,0:T(8,128)(2,1)}, u32[]{:S(2)}, u32[]{:S(2)}) collective-permute-start(bf16[4,48,3840]{2,1,0:T(8,128)(2,1)S(1)} %pad_maximum_fusion.refs_0_), channel_id=1, source_target_pairs={{0,2},{1,3},{2,0},{3,1},{4,6},{5,7},{6,4},{7,5},{8,10},{9,11},{10,... | collective-permute-start | bytes 4423688 | tf_op jit(solution)/shard_map/ppermute | solution.py:396
  72.9 3.1 collective-permute-start.16
  72.9 3.5 %collective-permute-start.18 = (bf16[48,2304]{1,0:T(8,128)(2,1)S(1)}, bf16[48,2304]{1,0:T(8,128)(2,1)S(1)}, u32[]{:S(2)}, u32[]{:S(2)}) collective-permute-start(bf16[48,2304]{1,0:T(8,128)(2,1)S(1)} %copy-done.13), channel_id=1, source_target_pairs={{0,1},{1,0},{2,3},{3,2},{4,5},{5,4},{6,7},{7,6},{8,9},{9,8},{10,11... | collective-permute-start | bytes 663560 | tf_op jit(solution)/shard_map/ppermute | solution.py:396
  73.4 3.3 %collective-permute-start.20 = (bf16[48,2304]{1,0:T(8,128)(2,1)}, bf16[48,2304]{1,0:T(8,128)(2,1)S(1)}, u32[]{:S(2)}, u32[]{:S(2)}) collective-permute-start(bf16[48,2304]{1,0:T(8,128)(2,1)} %copy-done.11), channel_id=1, source_target_pairs={{0,1},{1,0},{2,3},{3,2},{4,5},{5,4},{6,7},{7,6},{8,9},{9,8},{10,11... | collective-permute-start | bytes 663560 | tf_op jit(solution)/shard_map/ppermute | solution.py:396
  76.0 1.7 collective-permute-start.22
  76.4 1.7 collective-permute-start.17
  76.7 1.7 collective-permute-start.19
  77.7 4.1 %collective-permute-start.21 = (bf16[48,2304]{1,0:T(8,128)(2,1)S(1)}, bf16[48,2304]{1,0:T(8,128)(2,1)S(1)}, u32[]{:S(2)}, u32[]{:S(2)}) collective-permute-start(bf16[48,2304]{1,0:T(8,128)(2,1)S(1)} %copy-done.16), channel_id=1, source_target_pairs={{0,1},{1,0},{2,3},{3,2},{4,5},{5,4},{6,7},{7,6},{8,9},{9,8},{10,11... | collective-permute-start | bytes 663560 | tf_op jit(solution)/shard_map/ppermute | solution.py:396
  78.1 32.8 %collective-permute-start.13 = (bf16[192,768]{1,0:T(8,128)(2,1)S(1)}, bf16[192,768]{1,0:T(8,128)(2,1)}, u32[]{:S(2)}, u32[]{:S(2)}) collective-permute-start(bf16[192,768]{1,0:T(8,128)(2,1)S(1)} %convert_element_type.231), channel_id=1, source_target_pairs={{0,12},{1,13},{2,14},{3,15},{4,8},{5,9},{6,10},{7,11},{8,4},{9,5},... | collective-permute-start | bytes 884744 | tf_op jit(solution)/shard_map/ppermute | solution.py:396
  78.4 32.4 %collective-permute-start.12 = (bf16[192,768]{1,0:T(8,128)(2,1)S(1)}, bf16[192,768]{1,0:T(8,128)(2,1)}, u32[]{:S(2)}, u32[]{:S(2)}) collective-permute-start(bf16[192,768]{1,0:T(8,128)(2,1)S(1)} %convert_element_type.231), channel_id=1, source_target_pairs={{0,8},{1,9},{2,10},{3,11},{4,12},{5,13},{6,14},{7,15},{8,0},{9,1},... | collective-permute-start | bytes 884744 | tf_op jit(solution)/shard_map/ppermute | solution.py:396
  81.8 29.1 %collective-permute-start.11 = (bf16[192,768]{1,0:T(8,128)(2,1)S(1)}, bf16[192,768]{1,0:T(8,128)(2,1)}, u32[]{:S(2)}, u32[]{:S(2)}) collective-permute-start(bf16[192,768]{1,0:T(8,128)(2,1)S(1)} %convert_element_type.231), channel_id=1, source_target_pairs={{0,4},{1,5},{2,6},{3,7},{4,0},{5,1},{6,2},{7,3},{8,12},{9,13},{10,... | collective-permute-start | bytes 884744 | tf_op jit(solution)/shard_map/ppermute | solution.py:396
  110.9 3.5 %collective-permute-start.23 = (bf16[4,48,3840]{2,1,0:T(8,128)(2,1)}, bf16[4,48,3840]{2,1,0:T(8,128)(2,1)S(1)}, u32[]{:S(2)}, u32[]{:S(2)}) collective-permute-start(bf16[4,48,3840]{2,1,0:T(8,128)(2,1)} %collective-permute-done.14.refs_1_), channel_id=1, source_target_pairs={{0,1},{1,0},{2,3},{3,2},{4,5},{5,4},{6,7},{7,6},{8,9},{9,8},{10,11... | collective-permute-start | bytes 4423688 | tf_op jit(solution)/shard_map/ppermute | solution.py:396
  114.5 28.5 %collective-permute-start.24 = (bf16[4,192,768]{2,1,0:T(8,128)(2,1)S(1)}, bf16[4,192,768]{2,1,0:T(8,128)(2,1)}, u32[]{:S(2)}, u32[]{:S(2)}) collective-permute-start(bf16[4,192,768]{2,1,0:T(8,128)(2,1)S(1)} %pad_maximum_fusion.1.refs_4_.refs_0_), channel_id=1, source_target_pairs={{0,2},{1,3},{2,0},{3,1},{4,6},{5,7},{6,4},{7,5},{8,10},{9,11},{10,... | collective-permute-start | bytes 3538952 | tf_op jit(solution)/shard_map/ppermute | solution.py:396
  142.8 3.3 %collective-permute-start.25 = (bf16[4,192,768]{2,1,0:T(8,128)(2,1)S(1)}, bf16[4,192,768]{2,1,0:T(8,128)(2,1)S(1)}, u32[]{:S(2)}, u32[]{:S(2)}) collective-permute-start(bf16[4,192,768]{2,1,0:T(8,128)(2,1)S(1)} %pad_maximum_fusion.1.refs_4_.refs_0_), channel_id=1, source_target_pairs={{0,1},{1,0},{2,3},{3,2},{4,5},{5,4},{6,7},{7,6},{8,9},{9,8},{10,11... | collective-permute-start | bytes 3538952 | tf_op jit(solution)/shard_map/ppermute | solution.py:396
  143.0 4.6 %collective-permute-start.26 = (bf16[4,192,768]{2,1,0:T(8,128)(2,1)}, bf16[4,192,768]{2,1,0:T(8,128)(2,1)S(1)}, u32[]{:S(2)}, u32[]{:S(2)}) collective-permute-start(bf16[4,192,768]{2,1,0:T(8,128)(2,1)} %collective-permute-done.24.refs_5_.refs_1_), channel_id=1, source_target_pairs={{0,1},{1,0},{2,3},{3,2},{4,5},{5,4},{6,7},{7,6},{8,9},{9,8},{10,11... | collective-permute-start | bytes 3538952 | tf_op jit(solution)/shard_map/ppermute | solution.py:396
  185.1 5.6 %collective-permute-start.27 = (bf16[8,48,3840]{2,1,0:T(8,128)(2,1)}, bf16[8,48,3840]{2,1,0:T(8,128)(2,1)S(1)}, u32[]{:S(2)}, u32[]{:S(2)}) collective-permute-start(bf16[8,48,3840]{2,1,0:T(8,128)(2,1)} %get-tuple-element.173), channel_id=1, source_target_pairs={{0,1},{1,0},{2,3},{3,2},{4,5},{5,4},{6,7},{7,6},{8,9},{9,8},{10,11... | collective-permute-start | bytes 8847368 | tf_op jit(solution)/shard_map/ppermute | solution.py:396
  193.3 37.7 %collective-permute-start.28 = (bf16[4,48,3840]{2,1,0:T(8,128)(2,1)S(1)}, bf16[4,48,3840]{2,1,0:T(8,128)(2,1)}, u32[]{:S(2)}, u32[]{:S(2)}) collective-permute-start(bf16[4,48,3840]{2,1,0:T(8,128)(2,1)S(1)} %get-tuple-element.178), channel_id=1, source_target_pairs={{0,2},{1,3},{2,0},{3,1},{4,6},{5,7},{6,4},{7,5},{8,10},{9,11},{10,... | collective-permute-start | bytes 4423688 | tf_op jit(solution)/shard_map/ppermute | solution.py:396
  222.1 11.6 %collective-permute-start.29 = (bf16[8,48,2304]{2,1,0:T(8,128)(2,1)}, bf16[8,48,2304]{2,1,0:T(8,128)(2,1)S(1)}, u32[]{:S(2)}, u32[]{:S(2)}) collective-permute-start(bf16[8,48,2304]{2,1,0:T(8,128)(2,1)} %get-tuple-element.192), channel_id=1, source_target_pairs={{0,1},{1,0},{2,3},{3,2},{4,5},{5,4},{6,7},{7,6},{8,9},{9,8},{10,11... | collective-permute-start | bytes 5308424 | tf_op jit(solution)/shard_map/ppermute | solution.py:396
  235.1 40.8 %collective-permute-start.33 = (bf16[4,48,2304]{2,1,0:T(8,128)(2,1)}, bf16[4,48,2304]{2,1,0:T(8,128)(2,1)S(1)}, u32[]{:S(2)}, u32[]{:S(2)}) collective-permute-start(bf16[4,48,2304]{2,1,0:T(8,128)(2,1)} %get-tuple-element.200), channel_id=1, source_target_pairs={{0,2},{1,3},{2,0},{3,1},{4,6},{5,7},{6,4},{7,5},{8,10},{9,11},{10,... | collective-permute-start | bytes 2654216 | tf_op jit(solution)/shard_map/ppermute | solution.py:396
  236.8 39.1 %collective-permute-start.30 = (bf16[48,3840]{1,0:T(8,128)(2,1)}, bf16[48,3840]{1,0:T(8,128)(2,1)S(1)}, u32[]{:S(2)}, u32[]{:S(2)}) collective-permute-start(bf16[48,3840]{1,0:T(8,128)(2,1)} %get-tuple-element.196), channel_id=1, source_target_pairs={{0,4},{1,5},{2,6},{3,7},{4,0},{5,1},{6,2},{7,3},{8,12},{9,13},{10,... | collective-permute-start | bytes 1105928 | tf_op jit(solution)/shard_map/ppermute | solution.py:396
  238.3 37.6 %collective-permute-start.31 = (bf16[48,3840]{1,0:T(8,128)(2,1)}, bf16[48,3840]{1,0:T(8,128)(2,1)S(1)}, u32[]{:S(2)}, u32[]{:S(2)}) collective-permute-start(bf16[48,3840]{1,0:T(8,128)(2,1)} %get-tuple-element.197), channel_id=1, source_target_pairs={{0,8},{1,9},{2,10},{3,11},{4,12},{5,13},{6,14},{7,15},{8,0},{9,1},... | collective-permute-start | bytes 1105928 | tf_op jit(solution)/shard_map/ppermute | solution.py:396
  238.9 37.0 %collective-permute-start.32 = (bf16[48,3840]{1,0:T(8,128)(2,1)}, bf16[48,3840]{1,0:T(8,128)(2,1)}, u32[]{:S(2)}, u32[]{:S(2)}) collective-permute-start(bf16[48,3840]{1,0:T(8,128)(2,1)} %get-tuple-element.198), channel_id=1, source_target_pairs={{0,12},{1,13},{2,14},{3,15},{4,8},{5,9},{6,10},{7,11},{8,4},{9,5},... | collective-permute-start | bytes 1105928 | tf_op jit(solution)/shard_map/ppermute | solution.py:396
  277.4 24.7 %collective-permute-start.38 = (bf16[48,3840]{1,0:T(8,128)(2,1)S(1)}, bf16[48,3840]{1,0:T(8,128)(2,1)S(1)}, u32[]{:S(2)}, u32[]{:S(2)}) collective-permute-start(bf16[48,3840]{1,0:T(8,128)(2,1)S(1)} %add_convert_fusion.4), channel_id=1, source_target_pairs={{0,16},{16,0},{1,17},{17,1},{2,18},{18,2},{3,19},{19,3},{4,20},{20... | collective-permute-start | bytes 1105928 | tf_op jit(solution)/shard_map/ppermute | solution.py:400
  279.4 16.7 %collective-permute-start.34 = (bf16[48,2304]{1,0:T(8,128)(2,1)S(1)}, bf16[48,2304]{1,0:T(8,128)(2,1)S(1)}, u32[]{:S(2)}, u32[]{:S(2)}) collective-permute-start(bf16[48,2304]{1,0:T(8,128)(2,1)S(1)} %get-tuple-element.228), channel_id=1, source_target_pairs={{0,4},{1,5},{2,6},{3,7},{4,0},{5,1},{6,2},{7,3},{8,12},{9,13},{10,... | collective-permute-start | bytes 663560 | tf_op jit(solution)/shard_map/ppermute | solution.py:396
  280.6 16.3 %collective-permute-start.35 = (bf16[48,2304]{1,0:T(8,128)(2,1)S(1)}, bf16[48,2304]{1,0:T(8,128)(2,1)S(1)}, u32[]{:S(2)}, u32[]{:S(2)}) collective-permute-start(bf16[48,2304]{1,0:T(8,128)(2,1)S(1)} %get-tuple-element.229), channel_id=1, source_target_pairs={{0,8},{1,9},{2,10},{3,11},{4,12},{5,13},{6,14},{7,15},{8,0},{9,1},... | collective-permute-start | bytes 663560 | tf_op jit(solution)/shard_map/ppermute | solution.py:396
  281.6 20.5 %collective-permute-start.36 = (bf16[48,2304]{1,0:T(8,128)(2,1)S(1)}, bf16[48,2304]{1,0:T(8,128)(2,1)S(1)}, u32[]{:S(2)}, u32[]{:S(2)}) collective-permute-start(bf16[48,2304]{1,0:T(8,128)(2,1)S(1)} %get-tuple-element.230), channel_id=1, source_target_pairs={{0,12},{1,13},{2,14},{3,15},{4,8},{5,9},{6,10},{7,11},{8,4},{9,5},... | collective-permute-start | bytes 663560 | tf_op jit(solution)/shard_map/ppermute | solution.py:396
  283.0 19.1 %collective-permute-start.37 = (bf16[192,768]{1,0:T(8,128)(2,1)S(1)}, bf16[192,768]{1,0:T(8,128)(2,1)S(1)}, u32[]{:S(2)}, u32[]{:S(2)}) collective-permute-start(bf16[192,768]{1,0:T(8,128)(2,1)S(1)} %copy-done.27), channel_id=1, source_target_pairs={{0,16},{16,0},{1,17},{17,1},{2,18},{18,2},{3,19},{19,3},{4,20},{20... | collective-permute-start | bytes 884744 | tf_op jit(solution)/shard_map/ppermute | solution.py:400
  303.8 6.0 %collective-permute-start.39 = (bf16[48,2304]{1,0:T(8,128)(2,1)S(1)}, bf16[48,2304]{1,0:T(8,128)(2,1)S(1)}, u32[]{:S(2)}, u32[]{:S(2)}) collective-permute-start(bf16[48,2304]{1,0:T(8,128)(2,1)S(1)} %add_convert_fusion.9), channel_id=1, source_target_pairs={{0,16},{16,0},{1,17},{17,1},{2,18},{18,2},{3,19},{19,3},{4,20},{20... | collective-permute-start | bytes 663560 | tf_op jit(solution)/shard_map/ppermute | solution.py:400
  (35 other events, 405.5 us)
Sparse Core Ops, SparseCore 0:
  142.9 77.4 reduce-scatter.1

commit v2 on v1

--- a/solution.py
+++ b/solution.py
@@ -116,21 +116,38 @@
         group(long_ref, LONG, half * (size // SHORT) + (step - half) * (size // LONG), False)
 
 
+def apart(pair):
+    first_half = lax.broadcasted_iota(jnp.int32, (1, PAIR), 1) < HEAD_DIM
+    zeros = jnp.zeros_like(pair)
+    return jnp.concatenate([jnp.where(first_half, pair, zeros), jnp.where(first_half, zeros, pair)], axis=0)
+
+
+def apart_turned(pair):
+    turned = pair.T
+    upper = lax.broadcasted_iota(jnp.int32, (PAIR, 1), 0) < HEAD_DIM
+    zeros = jnp.zeros_like(turned)
+    return jnp.concatenate([jnp.where(upper, turned, zeros), jnp.where(upper, zeros, turned)], axis=1)
+
+
+def own_half(both):
+    length = both.shape[0] // 2
+    first_half = lax.broadcasted_iota(jnp.int32, (1, PAIR), 1) < HEAD_DIM
+    return jnp.where(first_half, both[:length], both[length:])
+
+
 def attend(query, keys, values, probs_ref, at):
-    first_half = lax.broadcasted_iota(jnp.int32, (1, PAIR), 1) < HEAD_DIM
-    turned = values.T
+    length = query.shape[0]
+    scores = dot(apart(keys), query, NT)
     parts = []
     for j in range(2):
-        own = first_half if j == 0 else jnp.logical_not(first_half)
-        masked = jnp.where(own, keys, jnp.zeros_like(keys))
-        scores = dot(masked, query, NT)
-        summit = jnp.max(scores, axis=0, keepdims=True)
-        expo = jnp.exp2((scores - summit) * (LOG2E * HEAD_DIM ** (-0.5)))
+        own = scores[j * length : (j + 1) * length]
+        summit = jnp.max(own, axis=0, keepdims=True)
+        expo = jnp.exp2((own - summit) * (LOG2E * HEAD_DIM ** (-0.5)))
         total = jnp.sum(expo, axis=0, keepdims=True)
-        probs = (expo * (1.0 / total)).astype(bfloat)
-        probs_ref[at[0], at[1] + j] = probs
-        parts.append(dot(turned[j * HEAD_DIM : (j + 1) * HEAD_DIM], probs, NN))
-    return jnp.concatenate(parts, axis=0).T
+        parts.append((expo * (1.0 / total)).astype(bfloat))
+    probs = jnp.concatenate(parts, axis=0)
+    probs_ref[at] = probs
+    return dot(apart_turned(values), probs, NN).T
 
 
 def forward_attention(
@@ -165,7 +182,7 @@
                 query = qkv_ref[rows, cols]
                 keys = qkv_ref[rows, width + pair * PAIR : width + (pair + 1) * PAIR]
                 values = qkv_ref[rows, 2 * width + pair * PAIR : 2 * width + (pair + 1) * PAIR]
-                mixed_ref[rows, cols] = attend(query, keys, values, probs_ref, (s, 2 * pair)).astype(
+                mixed_ref[rows, cols] = attend(query, keys, values, probs_ref, (s, pair)).astype(
                     bfloat
                 )
 
@@ -296,25 +313,20 @@
     vector_ref[3:4, :] += jnp.sum(rows, axis=0, keepdims=True)
 
 
-def attend_back(query, keys, values, upper, probs_ref, at):
-    first_half = lax.broadcasted_iota(jnp.int32, (1, PAIR), 1) < HEAD_DIM
-    turned = keys.T
-    value_parts, key_parts, query_parts = [], [], []
+def attend_back(query, keys, values, upper, probs):
+    length = query.shape[0]
+    probs_grad = dot(apart(values), upper, NT)
+    parts = []
     for j in range(2):
-        own = first_half if j == 0 else jnp.logical_not(first_half)
-        masked = jnp.where(own, values, jnp.zeros_like(values))
-        probs = probs_ref[at[0], at[1] + j]
-        wide = probs.astype(single)
-        probs_grad = dot(masked, upper, NT)
-        inner = jnp.sum(wide * probs_grad, axis=0, keepdims=True)
-        scores_grad = (wide * (probs_grad - inner)).astype(bfloat)
-        value_parts.append(dot(probs, upper, NN))
-        key_parts.append(dot(scores_grad, query, NN))
-        query_parts.append(dot(turned[j * HEAD_DIM : (j + 1) * HEAD_DIM], scores_grad, NN))
+        rows = slice(j * length, (j + 1) * length)
+        wide, own = probs[rows].astype(single), probs_grad[rows]
+        inner = jnp.sum(wide * own, axis=0, keepdims=True)
+        parts.append((wide * (own - inner)).astype(bfloat))
+    scores_grad = jnp.concatenate(parts, axis=0)
     scale = HEAD_DIM ** (-0.5)
-    query_grad = jnp.concatenate(query_parts, axis=0).T * scale
-    keys_grad = jnp.where(first_half, key_parts[0], key_parts[1]) * scale
-    values_grad = jnp.where(first_half, value_parts[0], value_parts[1])
+    query_grad = dot(apart_turned(keys), scores_grad, NN).T * scale
+    keys_grad = own_half(dot(scores_grad, query, NN)) * scale
+    values_grad = own_half(dot(probs, upper, NN))
     return query_grad.astype(bfloat), keys_grad.astype(bfloat), values_grad.astype(bfloat)
 
 
@@ -329,7 +341,7 @@
                 spots = [slice(part * width + pair * PAIR, part * width + (pair + 1) * PAIR) for part in range(3)]
                 query, keys, values = (qkv_ref[rows, spot] for spot in spots)
                 upper = mixed_grad_ref[rows, spots[0]]
-                for spot, value in zip(spots, attend_back(query, keys, values, upper, probs_ref, (s, 2 * pair))):
+                for spot, value in zip(spots, attend_back(query, keys, values, upper, probs_ref[s, pair])):
                     grad_ref[rows, spot] = value
 
     pl.when(step < half)(lambda: group(128, probs_short))
@@ -553,8 +565,8 @@
     short_spec, long_spec = of_short(tile, half), of_long(tile, half)
     band, half_band = (BAND, width), short.shape[0] // BAND
     short_band, long_band = of_short(band, half_band), of_long(band, half_band)
-    probs_short_spec = of_short((TILE // 128, heads, 128, 128), half)
-    probs_long_spec = of_long((1, heads, TILE, TILE), half)
+    probs_short_spec = of_short((TILE // SHORT, heads // 2, 2 * SHORT, SHORT), half)
+    probs_long_spec = of_long((1, heads // 2, 2 * LONG, LONG), half)
     shape = jax.ShapeDtypeStruct
     first, qkv, probs_short, probs_long, mixed = pl.pallas_call(
         functools.partial(forward_attention, half, width, n),
@@ -570,8 +582,8 @@
         out_shape=[
             shape((total, width), bfloat),
             shape((total, 3 * width), bfloat),
-            shape((n_short, heads, 128, 128), bfloat),
-            shape((n_long, heads, TILE, TILE), bfloat),
+            shape((n_short, heads // 2, 2 * SHORT, SHORT), bfloat),
+            shape((n_long, heads // 2, 2 * LONG, LONG), bfloat),
             shape((total, width), bfloat),
         ],
         scratch_shapes=[pltpu.VMEM((width, 3 * width), bfloat), pltpu.VMEM((1, 3 * width), single)],

time: 322 us -> 318 us (0.988)
  Pallas kernels: 141 us -> 126 us
  waiting for transfers between devices: 61.5 us -> 73.4 us
    ppermute x37, waiting for transfers between devices: 35.5 us -> 47.5 us  [across(): return lax.ppermute(array, 'fsdp', flip(bit))]
    pallas_call x1, Pallas kernels: 28.4 us -> 17.6 us  [shards(): pl.pallas_call(functools.partial(forward_attention, half, width, n), grid...]
    pallas_call x1, Pallas kernels: 19.8 us -> 15 us  [shards(): pl.pallas_call(functools.partial(backward_attention, half, width), grid=(...]
  transfers between devices with their start and end apart: 43 -> 43, of which waited for: 13 -> 16; matrix products, arithmetic and copies ran while one was open for 8% -> 7% of each run, Pallas kernels for 44% -> 40%
where the time goes in v2:
time: 318 us; the launch traced here: 314 us
  Pallas kernels  126 us (40%)
  waiting for transfers between devices  73.4 us (23%)
  starting transfers between devices  43.2 us (14%)
  blocking collectives  23.1 us (7%)
  other arithmetic  19.6 us (6%)
  between operations  15.1 us (5%)
  local copies, waits for them, and re-layouts  12.2 us (4%)
    ppermute x37, waiting for transfers between devices, across(): return lax.ppermute(array, 'fsdp', flip(bit))  47.5 us
    ppermute x37, starting transfers between devices, across(): return lax.ppermute(array, 'fsdp', flip(bit))  28.6 us
    all_to_all x1, blocking collectives, shards(): came = lax.all_to_all(packed, ('rep', 'fsdp'), 0, 0, tiled=True)  23.1 us
    pallas_call x1, Pallas kernels, shards(): pl.pallas_call(functools.partial(feed_back, half_band, width, hidden, len...  22.4 us
    pallas_call x1, Pallas kernels, shards(): pl.pallas_call(functools.partial(forward_up, half_band, width, hidden, le...  17.8 us
    pallas_call x1, Pallas kernels, shards(): pl.pallas_call(functools.partial(forward_attention, half, width, n), grid...  17.6 us
    pallas_call x1, Pallas kernels, shards(): pl.pallas_call(functools.partial(backward_attention, half, width), grid=(...  15 us
    pallas_call x1, Pallas kernels, shards(): pl.pallas_call(functools.partial(weight_back, (1, tiles)), grid=(tiles +...  14 us
  transfers between devices with their start and end apart: 43, of which 16 were waited for; matrix products, arithmetic and copies ran while one was open for 7% of the time, Pallas kernels for 40%

profile of v2, /device:TPU:16, one launch (start us, length us, event | category | flops | bytes accessed | tf_op | source)
XLA Modules:
  0.0 313.6 jit_solution(5316151685375708186)
XLA Ops:
  7.3 1.1 convert_element_type.226.refs_0_
  8.4 1.6 collective-permute-start.3
  10.5 3.5 %collective-permute-start.1 = (bf16[48,2304]{1,0:T(8,128)(2,1)S(1)}, bf16[48,2304]{1,0:T(8,128)(2,1)S(1)}, u32[]{:S(2)}, u32[]{:S(2)}) collective-permute-start(bf16[48,2304]{1,0:T(8,128)(2,1)S(1)} %convert_element_type.226.refs_0_), channel_id=1, source_target_pairs={{0,8},{1,9},{2,10},{3,11},{4,12},{5,13},{6,14},{7,15},{8,0},{9,1},... | collective-permute-start | bytes 663560 | tf_op jit(solution)/shard_map/ppermute | solution.py:408
  15.3 5.7 %all-to-all-start = ((s32[16,1,6]{2,1,0:T(1,128)}), s32[16,1,6]{2,1,0:T(1,128)S(1)}, u32[]{:S(2)}, u32[]{:S(2)}) async-start(s32[16,1,6]{2,1,0:T(1,128)} %broadcast_in_dim.11), calls=%async_computation | async-start | bytes 16384 | tf_op jit(solution)/shard_map/all_to_all | solution.py:530
  21.0 0.9 convert.34
  21.9 1.1 convert.35
  23.4 7.8 %all-to-all-done = s32[16,1,6]{2,1,0:T(1,128)S(1)} async-done(((s32[16,1,6]{2,1,0:T(1,128)}), s32[16,1,6]{2,1,0:T(1,128)S(1)}, u32[]{:S(2)}, u32[]{:S(2)}) %all-to-all-start) | async-done | bytes 416 | tf_op jit(solution)/shard_map/all_to_all | solution.py:530
  31.9 3.5 %collective-permute-start.5 = (bf16[48,3840]{1,0:T(8,128)(2,1)S(1)}, bf16[48,3840]{1,0:T(8,128)(2,1)}, u32[]{:S(2)}, u32[]{:S(2)}) collective-permute-start(bf16[48,3840]{1,0:T(8,128)(2,1)S(1)} %pad_maximum_fusion.2), channel_id=1, source_target_pairs={{0,8},{1,9},{2,10},{3,11},{4,12},{5,13},{6,14},{7,15},{8,0},{9,1},... | collective-permute-start | bytes 1105928 | tf_op jit(solution)/shard_map/ppermute | solution.py:408
  35.5 1.4 collective-permute-start.7
  38.1 5.8 %collective-permute-done.7.refs_6_ = bf16[48,2304]{1,0:T(8,128)(2,1)S(1)} collective-permute-done((bf16[48,2304]{1,0:T(8,128)(2,1)S(1)}, bf16[48,2304]{1,0:T(8,128)(2,1)S(1)}, u32[]{:S(2)}, u32[]{:S(2)}) %collective-permute-start.7) | collective-permute-done | bytes 221216 | tf_op jit(solution)/shard_map/ppermute | solution.py:408
  44.0 1.4 collective-permute-start.9
  47.3 5.8 %all-to-all-start.1 = ((bf16[16,2,432]{2,1,0:T(2,128)(2,1)}), bf16[16,2,432]{2,1,0:T(2,128)(2,1)S(1)}, u32[]{:S(2)}, u32[]{:S(2)}) async-start(bf16[16,2,432]{2,1,0:T(2,128)(2,1)} %reshape.176), calls=%async_computation.1 | async-start | bytes 65536 | tf_op jit(solution)/shard_map/all_to_all | solution.py:539
  53.1 14.0 %all-to-all-done.1 = bf16[16,2,432]{2,1,0:T(2,128)(2,1)S(1)} async-done(((bf16[16,2,432]{2,1,0:T(2,128)(2,1)}), bf16[16,2,432]{2,1,0:T(2,128)(2,1)S(1)}, u32[]{:S(2)}, u32[]{:S(2)}) %all-to-all-start.1) | async-done | bytes 27680 | tf_op jit(solution)/shard_map/all_to_all | solution.py:539
  70.4 1.4 pad_maximum_fusion.refs_0_
  73.5 2.5 collective-permute-done.16.refs_1_
  78.4 3.3 %collective-permute-start.12 = (bf16[192,768]{1,0:T(8,128)(2,1)S(1)}, bf16[192,768]{1,0:T(8,128)(2,1)}, u32[]{:S(2)}, u32[]{:S(2)}) collective-permute-start(bf16[192,768]{1,0:T(8,128)(2,1)S(1)} %convert_element_type.231), channel_id=1, source_target_pairs={{0,8},{1,9},{2,10},{3,11},{4,12},{5,13},{6,14},{7,15},{8,0},{9,1},... | collective-permute-start | bytes 884744 | tf_op jit(solution)/shard_map/ppermute | solution.py:408
  82.5 17.6 %forward_attention.1 = (bf16[1024,768]{1,0:T(8,128)(2,1)}, bf16[1024,2304]{1,0:T(8,128)(2,1)}, bf16[4,6,256,128]{3,2,1,0:T(8,128)(2,1)}, bf16[2,6,512,256]{3,2,1,0:T(8,128)(2,1)}, bf16[1024,768]{1,0:T(8,128)(2,1)}) custom-call(s32[1]{0:T(128)} %bitcast.place_ref, bf16[512,768]{1,0:T(8,128)(2,1)} %bitcast.50, bf16[512,768]{1,0:T(8,128)(2,1)} %bitcast.53, ...), custom_call_target="tpu_custom_call" | custom-call | flops 1024 | bytes 1024 | tf_op jit(solution)/shard_map/forward_attention/pallas_call | solution.py:571
  100.7 3.5 %collective-permute-done.12 = bf16[192,768]{1,0:T(8,128)(2,1)} collective-permute-done((bf16[192,768]{1,0:T(8,128)(2,1)S(1)}, bf16[192,768]{1,0:T(8,128)(2,1)}, u32[]{:S(2)}, u32[]{:S(2)}) %collective-permute-start.12) | collective-permute-done | bytes 294944 | tf_op jit(solution)/shard_map/ppermute | solution.py:408
  104.1 2.7 collective-permute-done.14.refs_1_
  106.9 1.3 pad_maximum_fusion.1.refs_4_.refs_0_
  108.2 2.2 collective-permute-done.23.refs_3_
  111.5 17.8 %forward_up.1 = (f32[1024,768]{1,0:T(8,128)}, bf16[1024,768]{1,0:T(8,128)(2,1)}, bf16[1024,3072]{1,0:T(8,128)(2,1)}, bf16[1024,3072]{1,0:T(8,128)(2,1)}) custom-call(s32[1]{0:T(128)} %bitcast.place_ref, bf16[512,768]{1,0:T(8,128)(2,1)} %bitcast.51, bf16[512,768]{1,0:T(8,128)(2,1)} %bitcast.54, f32[8,768]{1,0:T(8,128)} %pad.4.embed_ref, ...), custom_call_target="tpu_custom_call" | custom-call | flops 1024 | bytes 1024 | tf_op jit(solution)/shard_map/forward_up/pallas_call | solution.py:602
  129.3 9.3 %down_weight_back.1 = bf16[3072,768]{1,0:T(8,128)(2,1)} custom-call(bf16[1024,3072]{1,0:T(8,128)(2,1)} %get-tuple-element.164.active_ref, bf16[512,768]{1,0:T(8,128)(2,1)} %bitcast.56, bf16[512,768]{1,0:T(8,128)(2,1)} %bitcast.58), custom_call_target="tpu_custom_call" | custom-call | flops 1024 | bytes 1024 | tf_op jit(solution)/shard_map/down_weight_back/pallas_call | solution.py:635
  139.2 2.6 collective-permute-done.25.refs_6_.refs_2_
  141.8 1.6 collective-permute-done.26.refs_7_.refs_3_
  143.4 1.1 copy-done.5
  144.5 22.4 %feed_back.1 = (bf16[1024,3072]{1,0:T(8,128)(2,1)}, bf16[1024,768]{1,0:T(8,128)(2,1)}, f32[1024,768]{1,0:T(8,128)}, bf16[1024,768]{1,0:T(8,128)(2,1)}, f32[8,768]{1,0:T(8,128)}, /*index=5*/f32[1,3072]{1,0:T(1,128)}) custom-call(s32[1]{0:T(128)} %bitcast.place_ref, bf16[512,768]{1,0:T(8,128)(2,1)} %bitcast.57, bf16[512,768]{1,0:T(8,128)(2,1)} %bitcast.59, ...), custom_call_target="tpu_custom_call" | custom-call | flops 1024 | bytes 1024 | tf_op jit(solution)/shard_map/feed_back/pallas_call | solution.py:655
  166.9 14.0 %up_weight_back.1 = (bf16[8,48,3840]{2,1,0:T(8,128)(2,1)}, bf16[8,48,3840]{2,1,0:T(8,128)(2,1)}) custom-call(s32[1]{0:T(128)} %bitcast.place_ref, bf16[1024,768]{1,0:T(8,128)(2,1)} %get-tuple-element.151.mixed_ref.refs_0_, bf16[1024,768]{1,0:T(8,128)(2,1)} %get-tuple-element.163.refs_1_, bf16[1024,768]{1,0:T(8,128)(2,1)} %get-tuple-element.170.refs_2_, ...), custom_call_target="tpu_custom_call" | custom-call | flops 1024 | bytes 1024 | tf_op jit(solution)/shard_map/up_weight_back/pallas_call | solution.py:696
  181.1 5.5 %collective-permute-done.27 = bf16[8,48,3840]{2,1,0:T(8,128)(2,1)S(1)} collective-permute-done((bf16[8,48,3840]{2,1,0:T(8,128)(2,1)}, bf16[8,48,3840]{2,1,0:T(8,128)(2,1)S(1)}, u32[]{:S(2)}, u32[]{:S(2)}) %collective-permute-start.27) | collective-permute-done | bytes 2949152 | tf_op jit(solution)/shard_map/ppermute | solution.py:408
  186.6 2.5 add_convert_fusion
  189.5 15.0 %backward_attention.1.refs_1_.grad_ref = bf16[1024,2304]{1,0:T(8,128)(2,1)} custom-call(bf16[1024,2304]{1,0:T(8,128)(2,1)} %get-tuple-element.181.qkv_ref, bf16[1024,768]{1,0:T(8,128)(2,1)} %get-tuple-element.182.mixed_grad_ref, bf16[4,6,256,128]{3,2,1,0:T(8,128)(2,1)} %get-tuple-element.183.probs_short, bf16[2,6,512,256]{3,2,1,0:T(8,128)(2,1)} %get-tuple-element.184.probs_long), custom_call_target="tpu_custom_call" | custom-call | flops 1024 | bytes 1024 | tf_op jit(solution)/shard_map/backward_attention/pallas_call | solution.py:716
  204.5 8.6 %qkv_weight_back.1 = (bf16[8,48,2304]{2,1,0:T(8,128)(2,1)}, bf16[8,48,2304]{2,1,0:T(8,128)(2,1)}) custom-call(s32[1]{0:T(128)} %bitcast.place_ref, bf16[1024,768]{1,0:T(8,128)(2,1)} %get-tuple-element.180.refs_0_, bf16[1024,2304]{1,0:T(8,128)(2,1)} %backward_attention.1.refs_1_.grad_ref), custom_call_target="tpu_custom_call" | custom-call | flops 1024 | bytes 1024 | tf_op jit(solution)/shard_map/qkv_weight_back/pallas_call | solution.py:727
  213.2 13.6 %collective-permute-done.28 = bf16[4,48,3840]{2,1,0:T(8,128)(2,1)} collective-permute-done((bf16[4,48,3840]{2,1,0:T(8,128)(2,1)S(1)}, bf16[4,48,3840]{2,1,0:T(8,128)(2,1)}, u32[]{:S(2)}, u32[]{:S(2)}) %collective-permute-start.28) | collective-permute-done | bytes 1474592 | tf_op jit(solution)/shard_map/ppermute | solution.py:408
  226.8 2.8 fusion.5
  229.6 1.4 add_convert_fusion.2
  232.6 1.4 collective-permute-start.30
  234.6 1.5 collective-permute-start.32
  236.2 10.5 %start_back.1 = (bf16[512,768]{1,0:T(8,128)(2,1)}, bf16[512,768]{1,0:T(8,128)(2,1)}, f32[8,768]{1,0:T(8,128)}, f32[8,768]{1,0:T(8,128)}) custom-call(s32[1]{0:T(128)} %bitcast.place_ref, bf16[512,768]{1,0:T(8,128)(2,1)} %bitcast.52, bf16[512,768]{1,0:T(8,128)(2,1)} %bitcast.55, f32[8,768]{1,0:T(8,128)} %pad.4.embed_ref, f32[8,768]{1,0:T(8,128)} %slice.153.small_ref, ...), custom_call_target="tpu_custom_call" | custom-call | flops 1024 | bytes 1024 | tf_op jit(solution)/shard_map/start_back/pallas_call | solution.py:742
  248.7 23.1 %all_to_all.30 = f32[32,1,870]{2,1,0:T(1,128)S(1)} all-to-all(f32[32,1,870]{2,1,0:T(1,128)S(1)} %copy.58), channel_id=1, replica_groups=mesh['rep'=2,'fsdp'=16] {'rep','fsdp'}, dimensions={0} | all-to-all | bytes 222720 | tf_op jit(solution)/shard_map/all_to_all | solution.py:774
  271.9 1.2 add_convert_fusion.4
  274.1 1.2 fusion
  275.3 1.2 collective-permute-start.34
  277.3 1.6 collective-permute-start.36
  278.8 1.5 collective-permute-start.37
  280.4 10.4 %forward_down.1 = (bf16[512,768]{1,0:T(8,128)(2,1)}, bf16[512,768]{1,0:T(8,128)(2,1)}) custom-call(s32[1]{0:T(128)} %bitcast.place_ref, f32[1024,768]{1,0:T(8,128)} %get-tuple-element.222.middle_ref, bf16[1024,3072]{1,0:T(8,128)(2,1)} %get-tuple-element.164.active_ref, f32[8,768]{1,0:T(8,128)} %slice.153.small_ref, bf16[4,192,768]{2,1,0:T(8,128)(2,1)} %copy-done.1, ...), custom_call_target="tpu_custom_call" | custom-call | flops 1024 | bytes 1024 | tf_op jit(solution)/shard_map/forward_down/pallas_call | solution.py:780
  292.6 5.3 %collective-permute-done.36 = bf16[48,2304]{1,0:T(8,128)(2,1)S(1)} collective-permute-done((bf16[48,2304]{1,0:T(8,128)(2,1)S(1)}, bf16[48,2304]{1,0:T(8,128)(2,1)S(1)}, u32[]{:S(2)}, u32[]{:S(2)}) %collective-permute-start.36) | collective-permute-done | bytes 221216 | tf_op jit(solution)/shard_map/ppermute | solution.py:408
  299.7 1.0 collective-permute-start.39
  301.6 4.1 %collective-permute-done.39 = bf16[48,2304]{1,0:T(8,128)(2,1)S(1)} collective-permute-done((bf16[48,2304]{1,0:T(8,128)(2,1)S(1)}, bf16[48,2304]{1,0:T(8,128)(2,1)S(1)}, u32[]{:S(2)}, u32[]{:S(2)}) %collective-permute-start.39) | collective-permute-done | bytes 221216 | tf_op jit(solution)/shard_map/ppermute | solution.py:412
  (204 shorter events, 28.0 us)
Async XLA Ops:
  7.3 45.8 %copy-start.25 = (f32[192,768]{1,0:T(8,128)S(1)}, f32[192,768]{1,0:T(8,128)}, u32[]{:S(2)}) copy-start(f32[192,768]{1,0:T(8,128)} %param.38) | copy-start | bytes 1769476
  8.4 64.5 %copy-start.6 = (bf16[48,2304]{1,0:T(8,128)(2,1)}, bf16[48,2304]{1,0:T(8,128)(2,1)S(1)}, u32[]{:S(2)}) copy-start(bf16[48,2304]{1,0:T(8,128)(2,1)S(1)} %convert_element_type.226.refs_0_) | copy-start | bytes 663556
  8.4 22.9 %collective-permute-start.3 = (bf16[48,2304]{1,0:T(8,128)(2,1)S(1)}, bf16[48,2304]{1,0:T(8,128)(2,1)S(1)}, u32[]{:S(2)}, u32[]{:S(2)}) collective-permute-start(bf16[48,2304]{1,0:T(8,128)(2,1)S(1)} %convert_element_type.226.refs_0_), channel_id=1, source_target_pairs={{0,2},{1,3},{2,0},{3,1},{4,6},{5,7},{6,4},{7,5},{8,10},{9,11},{10,... | collective-permute-start | bytes 663560 | tf_op jit(solution)/shard_map/ppermute | solution.py:408
  10.0 21.3 %collective-permute-start.2 = (bf16[48,2304]{1,0:T(8,128)(2,1)S(1)}, bf16[48,2304]{1,0:T(8,128)(2,1)S(1)}, u32[]{:S(2)}, u32[]{:S(2)}) collective-permute-start(bf16[48,2304]{1,0:T(8,128)(2,1)S(1)} %convert_element_type.226.refs_0_), channel_id=1, source_target_pairs={{0,12},{1,13},{2,14},{3,15},{4,8},{5,9},{6,10},{7,11},{8,4},{9,5},... | collective-permute-start | bytes 663560 | tf_op jit(solution)/shard_map/ppermute | solution.py:408
  10.5 20.9 %collective-permute-start.1 = (bf16[48,2304]{1,0:T(8,128)(2,1)S(1)}, bf16[48,2304]{1,0:T(8,128)(2,1)S(1)}, u32[]{:S(2)}, u32[]{:S(2)}) collective-permute-start(bf16[48,2304]{1,0:T(8,128)(2,1)S(1)} %convert_element_type.226.refs_0_), channel_id=1, source_target_pairs={{0,8},{1,9},{2,10},{3,11},{4,12},{5,13},{6,14},{7,15},{8,0},{9,1},... | collective-permute-start | bytes 663560 | tf_op jit(solution)/shard_map/ppermute | solution.py:408
  14.0 17.4 %collective-permute-start = (bf16[48,2304]{1,0:T(8,128)(2,1)S(1)}, bf16[48,2304]{1,0:T(8,128)(2,1)S(1)}, u32[]{:S(2)}, u32[]{:S(2)}) collective-permute-start(bf16[48,2304]{1,0:T(8,128)(2,1)S(1)} %convert_element_type.226.refs_0_), channel_id=1, source_target_pairs={{0,4},{1,5},{2,6},{3,7},{4,0},{5,1},{6,2},{7,3},{8,12},{9,13},{10,... | collective-permute-start | bytes 663560 | tf_op jit(solution)/shard_map/ppermute | solution.py:408
  15.3 15.9 %all-to-all-start = ((s32[16,1,6]{2,1,0:T(1,128)}), s32[16,1,6]{2,1,0:T(1,128)S(1)}, u32[]{:S(2)}, u32[]{:S(2)}) async-start(s32[16,1,6]{2,1,0:T(1,128)} %broadcast_in_dim.11), calls=%async_computation | async-start | bytes 16384 | tf_op jit(solution)/shard_map/all_to_all | solution.py:530
  31.3 40.5 %copy-start.9 = (bf16[48,2304]{1,0:T(8,128)(2,1)}, bf16[48,2304]{1,0:T(8,128)(2,1)S(1)}, u32[]{:S(2)}) copy-start(bf16[48,2304]{1,0:T(8,128)(2,1)S(1)} %collective-permute-done.3.refs_2_) | copy-start | bytes 663556
  31.3 40.5 %copy-start.10 = (bf16[48,2304]{1,0:T(8,128)(2,1)}, bf16[48,2304]{1,0:T(8,128)(2,1)S(1)}, u32[]{:S(2)}) copy-start(bf16[48,2304]{1,0:T(8,128)(2,1)S(1)} %collective-permute-done.2.refs_12_) | copy-start | bytes 663556
  31.3 40.5 %copy-start.11 = (bf16[48,2304]{1,0:T(8,128)(2,1)}, bf16[48,2304]{1,0:T(8,128)(2,1)S(1)}, u32[]{:S(2)}) copy-start(bf16[48,2304]{1,0:T(8,128)(2,1)S(1)} %collective-permute-done.1.refs_8_) | copy-start | bytes 663556
  31.4 38.2 %collective-permute-start.6 = (bf16[48,3840]{1,0:T(8,128)(2,1)S(1)}, bf16[48,3840]{1,0:T(8,128)(2,1)S(1)}, u32[]{:S(2)}, u32[]{:S(2)}) collective-permute-start(bf16[48,3840]{1,0:T(8,128)(2,1)S(1)} %pad_maximum_fusion.2), channel_id=1, source_target_pairs={{0,12},{1,13},{2,14},{3,15},{4,8},{5,9},{6,10},{7,11},{8,4},{9,5},... | collective-permute-start | bytes 1105928 | tf_op jit(solution)/shard_map/ppermute | solution.py:408
  31.9 37.7 %collective-permute-start.5 = (bf16[48,3840]{1,0:T(8,128)(2,1)S(1)}, bf16[48,3840]{1,0:T(8,128)(2,1)}, u32[]{:S(2)}, u32[]{:S(2)}) collective-permute-start(bf16[48,3840]{1,0:T(8,128)(2,1)S(1)} %pad_maximum_fusion.2), channel_id=1, source_target_pairs={{0,8},{1,9},{2,10},{3,11},{4,12},{5,13},{6,14},{7,15},{8,0},{9,1},... | collective-permute-start | bytes 1105928 | tf_op jit(solution)/shard_map/ppermute | solution.py:408
  35.4 34.3 %collective-permute-start.4 = (bf16[48,3840]{1,0:T(8,128)(2,1)S(1)}, bf16[48,3840]{1,0:T(8,128)(2,1)}, u32[]{:S(2)}, u32[]{:S(2)}) collective-permute-start(bf16[48,3840]{1,0:T(8,128)(2,1)S(1)} %pad_maximum_fusion.2), channel_id=1, source_target_pairs={{0,4},{1,5},{2,6},{3,7},{4,0},{5,1},{6,2},{7,3},{8,12},{9,13},{10,... | collective-permute-start | bytes 1105928 | tf_op jit(solution)/shard_map/ppermute | solution.py:408
  35.5 8.4 %collective-permute-start.7 = (bf16[48,2304]{1,0:T(8,128)(2,1)S(1)}, bf16[48,2304]{1,0:T(8,128)(2,1)S(1)}, u32[]{:S(2)}, u32[]{:S(2)}) collective-permute-start(bf16[48,2304]{1,0:T(8,128)(2,1)S(1)} %collective-permute-done.refs_4_), channel_id=1, source_target_pairs={{0,2},{1,3},{2,0},{3,1},{4,6},{5,7},{6,4},{7,5},{8,10},{9,11},{10,... | collective-permute-start | bytes 663560 | tf_op jit(solution)/shard_map/ppermute | solution.py:408
  37.5 32.1 %collective-permute-start.8 = (bf16[48,2304]{1,0:T(8,128)(2,1)S(1)}, bf16[48,2304]{1,0:T(8,128)(2,1)S(1)}, u32[]{:S(2)}, u32[]{:S(2)}) collective-permute-start(bf16[48,2304]{1,0:T(8,128)(2,1)S(1)} %collective-permute-done.1.refs_8_), channel_id=1, source_target_pairs={{0,2},{1,3},{2,0},{3,1},{4,6},{5,7},{6,4},{7,5},{8,10},{9,11},{10,... | collective-permute-start | bytes 663560 | tf_op jit(solution)/shard_map/ppermute | solution.py:408
  44.0 25.6 %collective-permute-start.9 = (bf16[48,2304]{1,0:T(8,128)(2,1)S(1)}, bf16[48,2304]{1,0:T(8,128)(2,1)}, u32[]{:S(2)}, u32[]{:S(2)}) collective-permute-start(bf16[48,2304]{1,0:T(8,128)(2,1)S(1)} %collective-permute-done.2.refs_12_), channel_id=1, source_target_pairs={{0,2},{1,3},{2,0},{3,1},{4,6},{5,7},{6,4},{7,5},{8,10},{9,11},{10,... | collective-permute-start | bytes 663560 | tf_op jit(solution)/shard_map/ppermute | solution.py:408
  47.3 19.8 %all-to-all-start.1 = ((bf16[16,2,432]{2,1,0:T(2,128)(2,1)}), bf16[16,2,432]{2,1,0:T(2,128)(2,1)S(1)}, u32[]{:S(2)}, u32[]{:S(2)}) async-start(bf16[16,2,432]{2,1,0:T(2,128)(2,1)} %reshape.176), calls=%async_computation.1 | async-start | bytes 65536 | tf_op jit(solution)/shard_map/all_to_all | solution.py:539
  53.0 173.8 %reduce-scatter.2.cloned.1.call-start = ((), (), s32[]{:S(2)}) async-start(), calls=%async_computation.4 | async-start | bytes 5013504 | tf_op jit(solution)/shard_map/reduce_scatter | solution.py:650
  69.6 2.3 collective-permute-start.10
  71.9 32.2 %collective-permute-start.15 = (bf16[4,48,3840]{2,1,0:T(8,128)(2,1)S(1)}, bf16[4,48,3840]{2,1,0:T(8,128)(2,1)S(1)}, u32[]{:S(2)}, u32[]{:S(2)}) collective-permute-start(bf16[4,48,3840]{2,1,0:T(8,128)(2,1)S(1)} %pad_maximum_fusion.refs_0_), channel_id=1, source_target_pairs={{0,1},{1,0},{2,3},{3,2},{4,5},{5,4},{6,7},{7,6},{8,9},{9,8},{10,11... | collective-permute-start | bytes 4423688 | tf_op jit(solution)/shard_map/ppermute | solution.py:408
  72.5 34.4 %collective-permute-start.14 = (bf16[4,48,3840]{2,1,0:T(8,128)(2,1)S(1)}, bf16[4,48,3840]{2,1,0:T(8,128)(2,1)}, u32[]{:S(2)}, u32[]{:S(2)}) collective-permute-start(bf16[4,48,3840]{2,1,0:T(8,128)(2,1)S(1)} %pad_maximum_fusion.refs_0_), channel_id=1, source_target_pairs={{0,2},{1,3},{2,0},{3,1},{4,6},{5,7},{6,4},{7,5},{8,10},{9,11},{10,... | collective-permute-start | bytes 4423688 | tf_op jit(solution)/shard_map/ppermute | solution.py:408
  72.9 3.1 collective-permute-start.16
  72.9 3.5 %collective-permute-start.18 = (bf16[48,2304]{1,0:T(8,128)(2,1)S(1)}, bf16[48,2304]{1,0:T(8,128)(2,1)S(1)}, u32[]{:S(2)}, u32[]{:S(2)}) collective-permute-start(bf16[48,2304]{1,0:T(8,128)(2,1)S(1)} %copy-done.13), channel_id=1, source_target_pairs={{0,1},{1,0},{2,3},{3,2},{4,5},{5,4},{6,7},{7,6},{8,9},{9,8},{10,11... | collective-permute-start | bytes 663560 | tf_op jit(solution)/shard_map/ppermute | solution.py:408
  73.4 3.3 %collective-permute-start.20 = (bf16[48,2304]{1,0:T(8,128)(2,1)}, bf16[48,2304]{1,0:T(8,128)(2,1)S(1)}, u32[]{:S(2)}, u32[]{:S(2)}) collective-permute-start(bf16[48,2304]{1,0:T(8,128)(2,1)} %copy-done.11), channel_id=1, source_target_pairs={{0,1},{1,0},{2,3},{3,2},{4,5},{5,4},{6,7},{7,6},{8,9},{9,8},{10,11... | collective-permute-start | bytes 663560 | tf_op jit(solution)/shard_map/ppermute | solution.py:408
  76.0 1.7 collective-permute-start.22
  76.4 1.7 collective-permute-start.17
  76.7 1.7 collective-permute-start.19
  77.7 4.1 %collective-permute-start.21 = (bf16[48,2304]{1,0:T(8,128)(2,1)S(1)}, bf16[48,2304]{1,0:T(8,128)(2,1)S(1)}, u32[]{:S(2)}, u32[]{:S(2)}) collective-permute-start(bf16[48,2304]{1,0:T(8,128)(2,1)S(1)} %copy-done.16), channel_id=1, source_target_pairs={{0,1},{1,0},{2,3},{3,2},{4,5},{5,4},{6,7},{7,6},{8,9},{9,8},{10,11... | collective-permute-start | bytes 663560 | tf_op jit(solution)/shard_map/ppermute | solution.py:408
  78.1 22.6 %collective-permute-start.13 = (bf16[192,768]{1,0:T(8,128)(2,1)S(1)}, bf16[192,768]{1,0:T(8,128)(2,1)}, u32[]{:S(2)}, u32[]{:S(2)}) collective-permute-start(bf16[192,768]{1,0:T(8,128)(2,1)S(1)} %convert_element_type.231), channel_id=1, source_target_pairs={{0,12},{1,13},{2,14},{3,15},{4,8},{5,9},{6,10},{7,11},{8,4},{9,5},... | collective-permute-start | bytes 884744 | tf_op jit(solution)/shard_map/ppermute | solution.py:408
  78.4 25.7 %collective-permute-start.12 = (bf16[192,768]{1,0:T(8,128)(2,1)S(1)}, bf16[192,768]{1,0:T(8,128)(2,1)}, u32[]{:S(2)}, u32[]{:S(2)}) collective-permute-start(bf16[192,768]{1,0:T(8,128)(2,1)S(1)} %convert_element_type.231), channel_id=1, source_target_pairs={{0,8},{1,9},{2,10},{3,11},{4,12},{5,13},{6,14},{7,15},{8,0},{9,1},... | collective-permute-start | bytes 884744 | tf_op jit(solution)/shard_map/ppermute | solution.py:408
  81.8 22.3 %collective-permute-start.11 = (bf16[192,768]{1,0:T(8,128)(2,1)S(1)}, bf16[192,768]{1,0:T(8,128)(2,1)}, u32[]{:S(2)}, u32[]{:S(2)}) collective-permute-start(bf16[192,768]{1,0:T(8,128)(2,1)S(1)} %convert_element_type.231), channel_id=1, source_target_pairs={{0,4},{1,5},{2,6},{3,7},{4,0},{5,1},{6,2},{7,3},{8,12},{9,13},{10,... | collective-permute-start | bytes 884744 | tf_op jit(solution)/shard_map/ppermute | solution.py:408
  106.9 3.5 %collective-permute-start.23 = (bf16[4,48,3840]{2,1,0:T(8,128)(2,1)}, bf16[4,48,3840]{2,1,0:T(8,128)(2,1)S(1)}, u32[]{:S(2)}, u32[]{:S(2)}) collective-permute-start(bf16[4,48,3840]{2,1,0:T(8,128)(2,1)} %collective-permute-done.14.refs_1_), channel_id=1, source_target_pairs={{0,1},{1,0},{2,3},{3,2},{4,5},{5,4},{6,7},{7,6},{8,9},{9,8},{10,11... | collective-permute-start | bytes 4423688 | tf_op jit(solution)/shard_map/ppermute | solution.py:408
  110.3 28.5 %collective-permute-start.24 = (bf16[4,192,768]{2,1,0:T(8,128)(2,1)S(1)}, bf16[4,192,768]{2,1,0:T(8,128)(2,1)}, u32[]{:S(2)}, u32[]{:S(2)}) collective-permute-start(bf16[4,192,768]{2,1,0:T(8,128)(2,1)S(1)} %pad_maximum_fusion.1.refs_4_.refs_0_), channel_id=1, source_target_pairs={{0,2},{1,3},{2,0},{3,1},{4,6},{5,7},{6,4},{7,5},{8,10},{9,11},{10,... | collective-permute-start | bytes 3538952 | tf_op jit(solution)/shard_map/ppermute | solution.py:408
  138.6 3.2 %collective-permute-start.25 = (bf16[4,192,768]{2,1,0:T(8,128)(2,1)S(1)}, bf16[4,192,768]{2,1,0:T(8,128)(2,1)S(1)}, u32[]{:S(2)}, u32[]{:S(2)}) collective-permute-start(bf16[4,192,768]{2,1,0:T(8,128)(2,1)S(1)} %pad_maximum_fusion.1.refs_4_.refs_0_), channel_id=1, source_target_pairs={{0,1},{1,0},{2,3},{3,2},{4,5},{5,4},{6,7},{7,6},{8,9},{9,8},{10,11... | collective-permute-start | bytes 3538952 | tf_op jit(solution)/shard_map/ppermute | solution.py:408
  138.8 4.6 %collective-permute-start.26 = (bf16[4,192,768]{2,1,0:T(8,128)(2,1)}, bf16[4,192,768]{2,1,0:T(8,128)(2,1)S(1)}, u32[]{:S(2)}, u32[]{:S(2)}) collective-permute-start(bf16[4,192,768]{2,1,0:T(8,128)(2,1)} %collective-permute-done.24.refs_5_.refs_1_), channel_id=1, source_target_pairs={{0,1},{1,0},{2,3},{3,2},{4,5},{5,4},{6,7},{7,6},{8,9},{9,8},{10,11... | collective-permute-start | bytes 3538952 | tf_op jit(solution)/shard_map/ppermute | solution.py:408
  181.0 5.6 %collective-permute-start.27 = (bf16[8,48,3840]{2,1,0:T(8,128)(2,1)}, bf16[8,48,3840]{2,1,0:T(8,128)(2,1)S(1)}, u32[]{:S(2)}, u32[]{:S(2)}) collective-permute-start(bf16[8,48,3840]{2,1,0:T(8,128)(2,1)} %get-tuple-element.173), channel_id=1, source_target_pairs={{0,1},{1,0},{2,3},{3,2},{4,5},{5,4},{6,7},{7,6},{8,9},{9,8},{10,11... | collective-permute-start | bytes 8847368 | tf_op jit(solution)/shard_map/ppermute | solution.py:408
  189.1 37.7 %collective-permute-start.28 = (bf16[4,48,3840]{2,1,0:T(8,128)(2,1)S(1)}, bf16[4,48,3840]{2,1,0:T(8,128)(2,1)}, u32[]{:S(2)}, u32[]{:S(2)}) collective-permute-start(bf16[4,48,3840]{2,1,0:T(8,128)(2,1)S(1)} %get-tuple-element.178), channel_id=1, source_target_pairs={{0,2},{1,3},{2,0},{3,1},{4,6},{5,7},{6,4},{7,5},{8,10},{9,11},{10,... | collective-permute-start | bytes 4423688 | tf_op jit(solution)/shard_map/ppermute | solution.py:408
  213.2 16.4 %collective-permute-start.29 = (bf16[8,48,2304]{2,1,0:T(8,128)(2,1)}, bf16[8,48,2304]{2,1,0:T(8,128)(2,1)S(1)}, u32[]{:S(2)}, u32[]{:S(2)}) collective-permute-start(bf16[8,48,2304]{2,1,0:T(8,128)(2,1)} %get-tuple-element.192), channel_id=1, source_target_pairs={{0,1},{1,0},{2,3},{3,2},{4,5},{5,4},{6,7},{7,6},{8,9},{9,8},{10,11... | collective-permute-start | bytes 5308424 | tf_op jit(solution)/shard_map/ppermute | solution.py:408
  231.0 40.8 %collective-permute-start.33 = (bf16[4,48,2304]{2,1,0:T(8,128)(2,1)}, bf16[4,48,2304]{2,1,0:T(8,128)(2,1)S(1)}, u32[]{:S(2)}, u32[]{:S(2)}) collective-permute-start(bf16[4,48,2304]{2,1,0:T(8,128)(2,1)} %get-tuple-element.200), channel_id=1, source_target_pairs={{0,2},{1,3},{2,0},{3,1},{4,6},{5,7},{6,4},{7,5},{8,10},{9,11},{10,... | collective-permute-start | bytes 2654216 | tf_op jit(solution)/shard_map/ppermute | solution.py:408
  232.6 39.2 %collective-permute-start.30 = (bf16[48,3840]{1,0:T(8,128)(2,1)}, bf16[48,3840]{1,0:T(8,128)(2,1)S(1)}, u32[]{:S(2)}, u32[]{:S(2)}) collective-permute-start(bf16[48,3840]{1,0:T(8,128)(2,1)} %get-tuple-element.196), channel_id=1, source_target_pairs={{0,4},{1,5},{2,6},{3,7},{4,0},{5,1},{6,2},{7,3},{8,12},{9,13},{10,... | collective-permute-start | bytes 1105928 | tf_op jit(solution)/shard_map/ppermute | solution.py:408
  234.0 37.8 %collective-permute-start.31 = (bf16[48,3840]{1,0:T(8,128)(2,1)}, bf16[48,3840]{1,0:T(8,128)(2,1)S(1)}, u32[]{:S(2)}, u32[]{:S(2)}) collective-permute-start(bf16[48,3840]{1,0:T(8,128)(2,1)} %get-tuple-element.197), channel_id=1, source_target_pairs={{0,8},{1,9},{2,10},{3,11},{4,12},{5,13},{6,14},{7,15},{8,0},{9,1},... | collective-permute-start | bytes 1105928 | tf_op jit(solution)/shard_map/ppermute | solution.py:408
  234.6 37.2 %collective-permute-start.32 = (bf16[48,3840]{1,0:T(8,128)(2,1)}, bf16[48,3840]{1,0:T(8,128)(2,1)}, u32[]{:S(2)}, u32[]{:S(2)}) collective-permute-start(bf16[48,3840]{1,0:T(8,128)(2,1)} %get-tuple-element.198), channel_id=1, source_target_pairs={{0,12},{1,13},{2,14},{3,15},{4,8},{5,9},{6,10},{7,11},{8,4},{9,5},... | collective-permute-start | bytes 1105928 | tf_op jit(solution)/shard_map/ppermute | solution.py:408
  273.3 24.7 %collective-permute-start.38 = (bf16[48,3840]{1,0:T(8,128)(2,1)S(1)}, bf16[48,3840]{1,0:T(8,128)(2,1)S(1)}, u32[]{:S(2)}, u32[]{:S(2)}) collective-permute-start(bf16[48,3840]{1,0:T(8,128)(2,1)S(1)} %add_convert_fusion.4), channel_id=1, source_target_pairs={{0,16},{16,0},{1,17},{17,1},{2,18},{18,2},{3,19},{19,3},{4,20},{20... | collective-permute-start | bytes 1105928 | tf_op jit(solution)/shard_map/ppermute | solution.py:412
  275.3 16.8 %collective-permute-start.34 = (bf16[48,2304]{1,0:T(8,128)(2,1)S(1)}, bf16[48,2304]{1,0:T(8,128)(2,1)S(1)}, u32[]{:S(2)}, u32[]{:S(2)}) collective-permute-start(bf16[48,2304]{1,0:T(8,128)(2,1)S(1)} %get-tuple-element.228), channel_id=1, source_target_pairs={{0,4},{1,5},{2,6},{3,7},{4,0},{5,1},{6,2},{7,3},{8,12},{9,13},{10,... | collective-permute-start | bytes 663560 | tf_op jit(solution)/shard_map/ppermute | solution.py:408
  276.5 16.1 %collective-permute-start.35 = (bf16[48,2304]{1,0:T(8,128)(2,1)S(1)}, bf16[48,2304]{1,0:T(8,128)(2,1)S(1)}, u32[]{:S(2)}, u32[]{:S(2)}) collective-permute-start(bf16[48,2304]{1,0:T(8,128)(2,1)S(1)} %get-tuple-element.229), channel_id=1, source_target_pairs={{0,8},{1,9},{2,10},{3,11},{4,12},{5,13},{6,14},{7,15},{8,0},{9,1},... | collective-permute-start | bytes 663560 | tf_op jit(solution)/shard_map/ppermute | solution.py:408
  277.3 20.7 %collective-permute-start.36 = (bf16[48,2304]{1,0:T(8,128)(2,1)S(1)}, bf16[48,2304]{1,0:T(8,128)(2,1)S(1)}, u32[]{:S(2)}, u32[]{:S(2)}) collective-permute-start(bf16[48,2304]{1,0:T(8,128)(2,1)S(1)} %get-tuple-element.230), channel_id=1, source_target_pairs={{0,12},{1,13},{2,14},{3,15},{4,8},{5,9},{6,10},{7,11},{8,4},{9,5},... | collective-permute-start | bytes 663560 | tf_op jit(solution)/shard_map/ppermute | solution.py:408
  278.8 19.1 %collective-permute-start.37 = (bf16[192,768]{1,0:T(8,128)(2,1)S(1)}, bf16[192,768]{1,0:T(8,128)(2,1)S(1)}, u32[]{:S(2)}, u32[]{:S(2)}) collective-permute-start(bf16[192,768]{1,0:T(8,128)(2,1)S(1)} %copy-done.27), channel_id=1, source_target_pairs={{0,16},{16,0},{1,17},{17,1},{2,18},{18,2},{3,19},{19,3},{4,20},{20... | collective-permute-start | bytes 884744 | tf_op jit(solution)/shard_map/ppermute | solution.py:412
  299.7 6.0 %collective-permute-start.39 = (bf16[48,2304]{1,0:T(8,128)(2,1)S(1)}, bf16[48,2304]{1,0:T(8,128)(2,1)S(1)}, u32[]{:S(2)}, u32[]{:S(2)}) collective-permute-start(bf16[48,2304]{1,0:T(8,128)(2,1)S(1)} %add_convert_fusion.9), channel_id=1, source_target_pairs={{0,16},{16,0},{1,17},{17,1},{2,18},{18,2},{3,19},{19,3},{4,20},{20... | collective-permute-start | bytes 663560 | tf_op jit(solution)/shard_map/ppermute | solution.py:412
  (35 other events, 397.7 us)
Sparse Core Ops, SparseCore 0:
  138.7 77.3 reduce-scatter.1

commit v3 on v2

--- a/solution.py
+++ b/solution.py
@@ -719,7 +719,7 @@
         in_specs=[by_step((TILE, 3 * width)), by_step(tile), probs_short_spec, probs_long_spec],
         out_specs=by_step((TILE, 3 * width)),
         out_shape=shape((total, 3 * width), bfloat),
-        compiler_params=params(),
+        compiler_params=params(24 << 20),
         cost_estimate=cost(2 * total * width * 3 * width * 2, total * width * 20),
         name="backward_attention",
     )(qkv, mixed_grad, probs_short, probs_long)
@@ -731,14 +731,12 @@
         out_specs=[out_block] * 2,
         out_shape=[shape((slots, whole_rows, 3 * width), bfloat)] * 2,
         scratch_shapes=[pltpu.VMEM((width, total), bfloat)],
-        compiler_params=params(),
+        compiler_params=params(36 << 20),
         cost_estimate=cost(2 * total * width * 3 * width, total * width * 16),
         name="qkv_weight_back",
     )(place, first, projected_grad)
     qkv_sum = Scatter(count, qkv_keep, qkv_send)
-    middle_grad, qkv_sum.keep, down_share = up_sum.over_z(middle_grad, qkv_sum.keep, down_share)
-    (middle_grad,) = qkv_sum.over_y(middle_grad)
-
+    qkv_sum.keep, middle_grad = tie(qkv_sum.keep, middle_grad)
     grad_short, grad_long, last_vectors, sums = pl.pallas_call(
         functools.partial(start_back, half_band, width, n),
         grid=(total // BAND,),
@@ -764,6 +762,8 @@
         cost_estimate=cost(2 * total * width * 3 * width, total * width * 30),
         name="start_back",
     )(place, short, long, embed, smalls, middle_grad, projected_grad, *first_pieces)
+    sums, qkv_sum.keep, down_share = up_sum.over_z(sums, qkv_sum.keep, down_share)
+    sums, middle = qkv_sum.over_y(sums, middle)
     owners = width // rows
     both = jnp.concatenate([vectors[:4], last_vectors[:4], sums[:marks]], axis=0)
     lines = both.shape[0]
@@ -772,11 +772,6 @@
     packed = jnp.concatenate([packed, bias_grad.reshape(owners, -1), own_steps], axis=1)
     packed = jnp.concatenate([packed, packed], axis=0)
     came = lax.all_to_all(packed, ("rep", "fsdp"), 0, 0, tiled=True)
-    if count == SHARDS:
-        up_sum.came, qkv_sum.came, middle, came = tie(up_sum.came, qkv_sum.came, middle, came)
-    middle, down_share = up_sum.over_x(middle, down_share)
-    down_other = to_replica(down_share)
-    (middle,) = qkv_sum.over_z(middle)
     output_short, output_long = pl.pallas_call(
         functools.partial(forward_down, half_band, len(down_pieces)),
         grid=(total // BAND,),
@@ -790,6 +785,11 @@
         name="forward_down",
     )(place, middle, active, smalls, *down_pieces)
 
+    if count == SHARDS:
+        up_sum.came, qkv_sum.came, came, output_short = tie(up_sum.came, qkv_sum.came, came, output_short)
+    output_short, down_share = up_sum.over_x(output_short, down_share)
+    down_other = to_replica(down_share)
+    output_short, came = qkv_sum.over_z(output_short, came)
     vector_sums = jnp.sum(came[:, : 8 * rows], axis=0).reshape(8, rows)
     ends = lines * rows + hidden // owners
     up_bias_grad = jnp.sum(came[:, lines * rows : ends], axis=0)

time: 318 us -> 323 us (1.016)
  blocking collectives: 23.1 us -> 0 us
  waiting for transfers between devices: 73.4 us -> 94.5 us
  starting transfers between devices: 43.2 us -> 50.5 us
  Pallas kernels: 126 us -> 120 us
  other arithmetic: 19.6 us -> 23 us
    all_to_all x1 -> x0, blocking collectives: 23.1 us -> none  [shards(): came = lax.all_to_all(packed, ('rep', 'fsdp'), 0, 0, tiled=True)]
    all_to_all x0 -> x1, waiting for transfers between devices: none -> 16.2 us  [shards(): came = lax.all_to_all(packed, ('rep', 'fsdp'), 0, 0, tiled=True)]
    all_to_all x0 -> x1, starting transfers between devices: none -> 6.94 us  [shards(): came = lax.all_to_all(packed, ('rep', 'fsdp'), 0, 0, tiled=True)]
    ppermute x37, waiting for transfers between devices: 47.5 us -> 52.3 us  [across(): return lax.ppermute(array, 'fsdp', flip(bit))]
  transfers between devices with their start and end apart: 43 -> 44, of which waited for: 16 -> 18; matrix products, arithmetic and copies ran while one was open for 7% -> 8% of each run, Pallas kernels for 40% -> 38%
where the time goes in v3:
time: 323 us; the launch traced here: 319 us
  Pallas kernels  120 us (37%)
  waiting for transfers between devices  94.5 us (29%)
  starting transfers between devices  50.5 us (16%)
  other arithmetic  23 us (7%)
  between operations  15.2 us (5%)
  local copies, waits for them, and re-layouts  14.1 us (4%)
    ppermute x37, waiting for transfers between devices, across(): return lax.ppermute(array, 'fsdp', flip(bit))  52.3 us
    ppermute x37, starting transfers between devices, across(): return lax.ppermute(array, 'fsdp', flip(bit))  28.9 us
    pallas_call x1, Pallas kernels, shards(): pl.pallas_call(functools.partial(feed_back, half_band, width, hidden, len...  22.4 us
    pallas_call x1, Pallas kernels, shards(): pl.pallas_call(functools.partial(forward_up, half_band, width, hidden, le...  17.8 us
    pallas_call x1, Pallas kernels, shards(): pl.pallas_call(functools.partial(forward_attention, half, width, n), grid...  17.6 us
    all_to_all x1, waiting for transfers between devices, shards(): came = lax.all_to_all(packed, ('rep', 'fsdp'), 0, 0, tiled=True)  16.2 us
    pallas_call x1, Pallas kernels, shards(): pl.pallas_call(functools.partial(weight_back, (1, tiles)), grid=(tiles +...  14.2 us
    all_to_all x1, waiting for transfers between devices, shards(): told = lax.all_to_all(chosen, 'fsdp', 0, 0, tiled=True)  14 us
  transfers between devices with their start and end apart: 44, of which 18 were waited for; matrix products, arithmetic and copies ran while one was open for 8% of the time, Pallas kernels for 38%

profile of v3, /device:TPU:16, one launch (start us, length us, event | category | flops | bytes accessed | tf_op | source)
XLA Modules:
  0.0 318.8 jit_solution(7004359336781357556)
XLA Ops:
  7.3 1.1 convert_element_type.226.refs_0_
  8.4 1.6 collective-permute-start.3
  10.5 3.5 %collective-permute-start.1 = (bf16[48,2304]{1,0:T(8,128)(2,1)S(1)}, bf16[48,2304]{1,0:T(8,128)(2,1)S(1)}, u32[]{:S(2)}, u32[]{:S(2)}) collective-permute-start(bf16[48,2304]{1,0:T(8,128)(2,1)S(1)} %convert_element_type.226.refs_0_), channel_id=1, source_target_pairs={{0,8},{1,9},{2,10},{3,11},{4,12},{5,13},{6,14},{7,15},{8,0},{9,1},... | collective-permute-start | bytes 663560 | tf_op jit(solution)/shard_map/ppermute | solution.py:408
  15.3 5.7 %all-to-all-start = ((s32[16,1,6]{2,1,0:T(1,128)}), s32[16,1,6]{2,1,0:T(1,128)S(1)}, u32[]{:S(2)}, u32[]{:S(2)}) async-start(s32[16,1,6]{2,1,0:T(1,128)} %broadcast_in_dim.11), calls=%async_computation | async-start | bytes 16384 | tf_op jit(solution)/shard_map/all_to_all | solution.py:530
  21.9 1.1 convert.35
  23.4 7.8 %all-to-all-done = s32[16,1,6]{2,1,0:T(1,128)S(1)} async-done(((s32[16,1,6]{2,1,0:T(1,128)}), s32[16,1,6]{2,1,0:T(1,128)S(1)}, u32[]{:S(2)}, u32[]{:S(2)}) %all-to-all-start) | async-done | bytes 416 | tf_op jit(solution)/shard_map/all_to_all | solution.py:530
  31.9 3.5 %collective-permute-start.5 = (bf16[48,3840]{1,0:T(8,128)(2,1)S(1)}, bf16[48,3840]{1,0:T(8,128)(2,1)}, u32[]{:S(2)}, u32[]{:S(2)}) collective-permute-start(bf16[48,3840]{1,0:T(8,128)(2,1)S(1)} %pad_maximum_fusion.2), channel_id=1, source_target_pairs={{0,8},{1,9},{2,10},{3,11},{4,12},{5,13},{6,14},{7,15},{8,0},{9,1},... | collective-permute-start | bytes 1105928 | tf_op jit(solution)/shard_map/ppermute | solution.py:408
  35.5 1.4 collective-permute-start.7
  38.1 5.8 %collective-permute-done.7.refs_6_ = bf16[48,2304]{1,0:T(8,128)(2,1)S(1)} collective-permute-done((bf16[48,2304]{1,0:T(8,128)(2,1)S(1)}, bf16[48,2304]{1,0:T(8,128)(2,1)S(1)}, u32[]{:S(2)}, u32[]{:S(2)}) %collective-permute-start.7) | collective-permute-done | bytes 221216 | tf_op jit(solution)/shard_map/ppermute | solution.py:408
  44.0 1.4 collective-permute-start.9
  47.3 5.8 %all-to-all-start.1 = ((bf16[16,2,432]{2,1,0:T(2,128)(2,1)}), bf16[16,2,432]{2,1,0:T(2,128)(2,1)S(1)}, u32[]{:S(2)}, u32[]{:S(2)}) async-start(bf16[16,2,432]{2,1,0:T(2,128)(2,1)} %reshape.176), calls=%async_computation.1 | async-start | bytes 65536 | tf_op jit(solution)/shard_map/all_to_all | solution.py:539
  53.1 14.0 %all-to-all-done.1 = bf16[16,2,432]{2,1,0:T(2,128)(2,1)S(1)} async-done(((bf16[16,2,432]{2,1,0:T(2,128)(2,1)}), bf16[16,2,432]{2,1,0:T(2,128)(2,1)S(1)}, u32[]{:S(2)}, u32[]{:S(2)}) %all-to-all-start.1) | async-done | bytes 27680 | tf_op jit(solution)/shard_map/all_to_all | solution.py:539
  70.4 1.4 pad_maximum_fusion.refs_0_
  73.5 2.5 collective-permute-done.16.refs_1_
  78.4 3.3 %collective-permute-start.12 = (bf16[192,768]{1,0:T(8,128)(2,1)S(1)}, bf16[192,768]{1,0:T(8,128)(2,1)}, u32[]{:S(2)}, u32[]{:S(2)}) collective-permute-start(bf16[192,768]{1,0:T(8,128)(2,1)S(1)} %convert_element_type.231), channel_id=1, source_target_pairs={{0,8},{1,9},{2,10},{3,11},{4,12},{5,13},{6,14},{7,15},{8,0},{9,1},... | collective-permute-start | bytes 884744 | tf_op jit(solution)/shard_map/ppermute | solution.py:408
  82.5 17.6 %forward_attention.1 = (bf16[1024,768]{1,0:T(8,128)(2,1)}, bf16[1024,2304]{1,0:T(8,128)(2,1)}, bf16[4,6,256,128]{3,2,1,0:T(8,128)(2,1)}, bf16[2,6,512,256]{3,2,1,0:T(8,128)(2,1)}, bf16[1024,768]{1,0:T(8,128)(2,1)}) custom-call(s32[1]{0:T(128)} %bitcast.place_ref, bf16[512,768]{1,0:T(8,128)(2,1)} %bitcast.52, bf16[512,768]{1,0:T(8,128)(2,1)} %bitcast.55, ...), custom_call_target="tpu_custom_call" | custom-call | flops 1024 | bytes 1024 | tf_op jit(solution)/shard_map/forward_attention/pallas_call | solution.py:571
  100.7 3.5 %collective-permute-done.12 = bf16[192,768]{1,0:T(8,128)(2,1)} collective-permute-done((bf16[192,768]{1,0:T(8,128)(2,1)S(1)}, bf16[192,768]{1,0:T(8,128)(2,1)}, u32[]{:S(2)}, u32[]{:S(2)}) %collective-permute-start.12) | collective-permute-done | bytes 294944 | tf_op jit(solution)/shard_map/ppermute | solution.py:408
  104.1 2.7 collective-permute-done.14.refs_1_
  106.9 1.3 pad_maximum_fusion.1.refs_4_.refs_0_
  108.2 2.2 collective-permute-done.23.refs_3_
  111.5 17.8 %forward_up.1 = (f32[1024,768]{1,0:T(8,128)}, bf16[1024,768]{1,0:T(8,128)(2,1)}, bf16[1024,3072]{1,0:T(8,128)(2,1)}, bf16[1024,3072]{1,0:T(8,128)(2,1)}) custom-call(s32[1]{0:T(128)} %bitcast.place_ref, bf16[512,768]{1,0:T(8,128)(2,1)} %bitcast.53, bf16[512,768]{1,0:T(8,128)(2,1)} %bitcast.56, f32[8,768]{1,0:T(8,128)} %pad.4.embed_ref, ...), custom_call_target="tpu_custom_call" | custom-call | flops 1024 | bytes 1024 | tf_op jit(solution)/shard_map/forward_up/pallas_call | solution.py:602
  129.3 9.3 %down_weight_back.1 = bf16[3072,768]{1,0:T(8,128)(2,1)} custom-call(bf16[1024,3072]{1,0:T(8,128)(2,1)} %get-tuple-element.170.active_ref, bf16[512,768]{1,0:T(8,128)(2,1)} %bitcast.58, bf16[512,768]{1,0:T(8,128)(2,1)} %bitcast.60), custom_call_target="tpu_custom_call" | custom-call | flops 1024 | bytes 1024 | tf_op jit(solution)/shard_map/down_weight_back/pallas_call | solution.py:635
  139.1 2.6 collective-permute-done.25.refs_6_.refs_2_
  141.7 1.7 collective-permute-done.26.refs_7_.refs_3_
  144.5 22.4 %feed_back.1 = (bf16[1024,3072]{1,0:T(8,128)(2,1)}, bf16[1024,768]{1,0:T(8,128)(2,1)}, f32[1024,768]{1,0:T(8,128)}, bf16[1024,768]{1,0:T(8,128)(2,1)}, f32[8,768]{1,0:T(8,128)}, /*index=5*/f32[1,3072]{1,0:T(1,128)}) custom-call(s32[1]{0:T(128)} %bitcast.place_ref, bf16[512,768]{1,0:T(8,128)(2,1)} %bitcast.59, bf16[512,768]{1,0:T(8,128)(2,1)} %bitcast.61, ...), custom_call_target="tpu_custom_call" | custom-call | flops 1024 | bytes 1024 | tf_op jit(solution)/shard_map/feed_back/pallas_call | solution.py:655
  166.9 14.2 %up_weight_back.1 = (bf16[8,48,3840]{2,1,0:T(8,128)(2,1)}, bf16[8,48,3840]{2,1,0:T(8,128)(2,1)}) custom-call(s32[1]{0:T(128)} %bitcast.place_ref, bf16[1024,768]{1,0:T(8,128)(2,1)} %get-tuple-element.157.mixed_ref.refs_0_, bf16[1024,768]{1,0:T(8,128)(2,1)} %get-tuple-element.169.refs_1_, bf16[1024,768]{1,0:T(8,128)(2,1)} %get-tuple-element.176.refs_2_, ...), custom_call_target="tpu_custom_call" | custom-call | flops 1024 | bytes 1024 | tf_op jit(solution)/shard_map/up_weight_back/pallas_call | solution.py:696
  181.2 5.5 %collective-permute-done.27 = bf16[8,48,3840]{2,1,0:T(8,128)(2,1)S(1)} collective-permute-done((bf16[8,48,3840]{2,1,0:T(8,128)(2,1)}, bf16[8,48,3840]{2,1,0:T(8,128)(2,1)S(1)}, u32[]{:S(2)}, u32[]{:S(2)}) %collective-permute-start.27) | collective-permute-done | bytes 2949152 | tf_op jit(solution)/shard_map/ppermute | solution.py:408
  186.7 4.3 %add_convert_fusion = (bf16[4,48,3840]{2,1,0:T(8,128)(2,1)}, bf16[4,48,3840]{2,1,0:T(8,128)(2,1)}) fusion(bf16[8,48,3840]{2,1,0:T(8,128)(2,1)S(1)} %collective-permute-done.27, bf16[8,48,3840]{2,1,0:T(8,128)(2,1)} %get-tuple-element.181), kind=kLoop, calls=%fused_computation | loop fusion | flops 5898240 | bytes 8847360 | tf_op jit(solution)/shard_map/convert_element_type | solution.py:454
  192.0 11.8 %backward_attention.1.refs_1_.grad_ref = bf16[1024,2304]{1,0:T(8,128)(2,1)S(1)} custom-call(bf16[1024,2304]{1,0:T(8,128)(2,1)S(1)} %bitcast.51, bf16[1024,768]{1,0:T(8,128)(2,1)S(1)} %copy-done.4, bf16[4,6,256,128]{3,2,1,0:T(8,128)(2,1)S(1)} %copy-done.3, bf16[2,6,512,256]{3,2,1,0:T(8,128)(2,1)S(1)} %copy-done.1), custom_call_target="tpu_custom_call" | custom-call | flops 1024 | bytes 1024 | tf_op jit(solution)/shard_map/backward_attention/pallas_call | solution.py:716
  203.9 6.0 %qkv_weight_back.1 = (bf16[8,48,2304]{2,1,0:T(8,128)(2,1)S(1)}, bf16[8,48,2304]{2,1,0:T(8,128)(2,1)S(1)}) custom-call(s32[1]{0:T(128)} %bitcast.place_ref, bf16[1024,768]{1,0:T(8,128)(2,1)S(1)} %copy-done.2, bf16[1024,2304]{1,0:T(8,128)(2,1)S(1)} %backward_attention.1.refs_1_.grad_ref), custom_call_target="tpu_custom_call" | custom-call | flops 1024 | bytes 1024 | tf_op jit(solution)/shard_map/qkv_weight_back/pallas_call | solution.py:727
  210.2 10.5 %start_back.1 = (bf16[512,768]{1,0:T(8,128)(2,1)}, bf16[512,768]{1,0:T(8,128)(2,1)}, f32[8,768]{1,0:T(8,128)}, f32[8,768]{1,0:T(8,128)}) custom-call(s32[1]{0:T(128)} %bitcast.place_ref, bf16[512,768]{1,0:T(8,128)(2,1)} %bitcast.54, bf16[512,768]{1,0:T(8,128)(2,1)} %bitcast.57, f32[8,768]{1,0:T(8,128)} %pad.4.embed_ref, f32[8,768]{1,0:T(8,128)} %slice.153.small_ref, ...), custom_call_target="tpu_custom_call" | custom-call | flops 1024 | bytes 1024 | tf_op jit(solution)/shard_map/start_back/pallas_call | solution.py:740
  220.7 8.1 %collective-permute-done.28 = bf16[4,48,3840]{2,1,0:T(8,128)(2,1)} collective-permute-done((bf16[4,48,3840]{2,1,0:T(8,128)(2,1)}, bf16[4,48,3840]{2,1,0:T(8,128)(2,1)}, u32[]{:S(2)}, u32[]{:S(2)}) %collective-permute-start.28) | collective-permute-done | bytes 1474592 | tf_op jit(solution)/shard_map/ppermute | solution.py:408
  228.8 3.1 fusion.5
  231.9 1.8 add_convert_fusion.2
  237.0 1.3 collective-permute-start.30
  238.8 1.7 collective-permute-start.32
  242.4 6.9 %all-to-all-start.2 = ((f32[32,1,870]{2,1,0:T(1,128)}), f32[32,1,870]{2,1,0:T(1,128)S(1)}, u32[]{:S(2)}, u32[]{:S(2)}) async-start(f32[32,1,870]{2,1,0:T(1,128)} %copy.58), calls=%async_computation.3 | async-start | bytes 229376 | tf_op jit(solution)/shard_map/all_to_all | solution.py:774
  249.4 10.5 %forward_down.1 = (bf16[512,768]{1,0:T(8,128)(2,1)}, bf16[512,768]{1,0:T(8,128)(2,1)}) custom-call(s32[1]{0:T(128)} %bitcast.place_ref, f32[1024,768]{1,0:T(8,128)} %get-tuple-element.215.middle_ref, bf16[1024,3072]{1,0:T(8,128)(2,1)} %get-tuple-element.170.active_ref, f32[8,768]{1,0:T(8,128)} %slice.153.small_ref, bf16[4,192,768]{2,1,0:T(8,128)(2,1)} %copy-done.6, ...), custom_call_target="tpu_custom_call" | custom-call | flops 1024 | bytes 1024 | tf_op jit(solution)/shard_map/forward_down/pallas_call | solution.py:775
  259.9 16.2 %all-to-all-done.2 = f32[32,1,870]{2,1,0:T(1,128)S(1)} async-done(((f32[32,1,870]{2,1,0:T(1,128)}), f32[32,1,870]{2,1,0:T(1,128)S(1)}, u32[]{:S(2)}, u32[]{:S(2)}) %all-to-all-start.2) | async-done | bytes 111392 | tf_op jit(solution)/shard_map/all_to_all | solution.py:774
  276.1 1.4 add_convert_fusion.4
  279.3 1.2 fusion
  280.4 1.2 collective-permute-start.34
  282.3 1.6 collective-permute-start.36
  284.0 1.5 collective-permute-start.37
  286.8 3.2 %collective-permute-done.34 = bf16[48,2304]{1,0:T(8,128)(2,1)S(1)} collective-permute-done((bf16[48,2304]{1,0:T(8,128)(2,1)}, bf16[48,2304]{1,0:T(8,128)(2,1)S(1)}, u32[]{:S(2)}, u32[]{:S(2)}) %collective-permute-start.34) | collective-permute-done | bytes 221216 | tf_op jit(solution)/shard_map/ppermute | solution.py:408
  290.0 7.7 %collective-permute-done.35 = bf16[48,2304]{1,0:T(8,128)(2,1)S(1)} collective-permute-done((bf16[48,2304]{1,0:T(8,128)(2,1)S(1)}, bf16[48,2304]{1,0:T(8,128)(2,1)S(1)}, u32[]{:S(2)}, u32[]{:S(2)}) %collective-permute-start.35) | collective-permute-done | bytes 221216 | tf_op jit(solution)/shard_map/ppermute | solution.py:408
  297.7 5.4 %collective-permute-done.36 = bf16[48,2304]{1,0:T(8,128)(2,1)S(1)} collective-permute-done((bf16[48,2304]{1,0:T(8,128)(2,1)S(1)}, bf16[48,2304]{1,0:T(8,128)(2,1)S(1)}, u32[]{:S(2)}, u32[]{:S(2)}) %collective-permute-start.36) | collective-permute-done | bytes 221216 | tf_op jit(solution)/shard_map/ppermute | solution.py:408
  306.8 4.1 %collective-permute-done.39 = bf16[48,2304]{1,0:T(8,128)(2,1)S(1)} collective-permute-done((bf16[48,2304]{1,0:T(8,128)(2,1)S(1)}, bf16[48,2304]{1,0:T(8,128)(2,1)S(1)}, u32[]{:S(2)}, u32[]{:S(2)}) %collective-permute-start.39) | collective-permute-done | bytes 221216 | tf_op jit(solution)/shard_map/ppermute | solution.py:412
  (216 shorter events, 33.3 us)
Async XLA Ops:
  7.3 45.8 %copy-start.29 = (f32[192,768]{1,0:T(8,128)S(1)}, f32[192,768]{1,0:T(8,128)}, u32[]{:S(2)}) copy-start(f32[192,768]{1,0:T(8,128)} %param.38) | copy-start | bytes 1769476
  8.4 64.5 %copy-start.11 = (bf16[48,2304]{1,0:T(8,128)(2,1)}, bf16[48,2304]{1,0:T(8,128)(2,1)S(1)}, u32[]{:S(2)}) copy-start(bf16[48,2304]{1,0:T(8,128)(2,1)S(1)} %convert_element_type.226.refs_0_) | copy-start | bytes 663556
  8.4 22.9 %collective-permute-start.3 = (bf16[48,2304]{1,0:T(8,128)(2,1)S(1)}, bf16[48,2304]{1,0:T(8,128)(2,1)S(1)}, u32[]{:S(2)}, u32[]{:S(2)}) collective-permute-start(bf16[48,2304]{1,0:T(8,128)(2,1)S(1)} %convert_element_type.226.refs_0_), channel_id=1, source_target_pairs={{0,2},{1,3},{2,0},{3,1},{4,6},{5,7},{6,4},{7,5},{8,10},{9,11},{10,... | collective-permute-start | bytes 663560 | tf_op jit(solution)/shard_map/ppermute | solution.py:408
  10.0 21.3 %collective-permute-start.2 = (bf16[48,2304]{1,0:T(8,128)(2,1)S(1)}, bf16[48,2304]{1,0:T(8,128)(2,1)S(1)}, u32[]{:S(2)}, u32[]{:S(2)}) collective-permute-start(bf16[48,2304]{1,0:T(8,128)(2,1)S(1)} %convert_element_type.226.refs_0_), channel_id=1, source_target_pairs={{0,12},{1,13},{2,14},{3,15},{4,8},{5,9},{6,10},{7,11},{8,4},{9,5},... | collective-permute-start | bytes 663560 | tf_op jit(solution)/shard_map/ppermute | solution.py:408
  10.5 20.9 %collective-permute-start.1 = (bf16[48,2304]{1,0:T(8,128)(2,1)S(1)}, bf16[48,2304]{1,0:T(8,128)(2,1)S(1)}, u32[]{:S(2)}, u32[]{:S(2)}) collective-permute-start(bf16[48,2304]{1,0:T(8,128)(2,1)S(1)} %convert_element_type.226.refs_0_), channel_id=1, source_target_pairs={{0,8},{1,9},{2,10},{3,11},{4,12},{5,13},{6,14},{7,15},{8,0},{9,1},... | collective-permute-start | bytes 663560 | tf_op jit(solution)/shard_map/ppermute | solution.py:408
  14.0 17.4 %collective-permute-start = (bf16[48,2304]{1,0:T(8,128)(2,1)S(1)}, bf16[48,2304]{1,0:T(8,128)(2,1)S(1)}, u32[]{:S(2)}, u32[]{:S(2)}) collective-permute-start(bf16[48,2304]{1,0:T(8,128)(2,1)S(1)} %convert_element_type.226.refs_0_), channel_id=1, source_target_pairs={{0,4},{1,5},{2,6},{3,7},{4,0},{5,1},{6,2},{7,3},{8,12},{9,13},{10,... | collective-permute-start | bytes 663560 | tf_op jit(solution)/shard_map/ppermute | solution.py:408
  15.3 15.9 %all-to-all-start = ((s32[16,1,6]{2,1,0:T(1,128)}), s32[16,1,6]{2,1,0:T(1,128)S(1)}, u32[]{:S(2)}, u32[]{:S(2)}) async-start(s32[16,1,6]{2,1,0:T(1,128)} %broadcast_in_dim.11), calls=%async_computation | async-start | bytes 16384 | tf_op jit(solution)/shard_map/all_to_all | solution.py:530
  31.3 40.5 %copy-start.13 = (bf16[48,2304]{1,0:T(8,128)(2,1)}, bf16[48,2304]{1,0:T(8,128)(2,1)S(1)}, u32[]{:S(2)}) copy-start(bf16[48,2304]{1,0:T(8,128)(2,1)S(1)} %collective-permute-done.3.refs_2_) | copy-start | bytes 663556
  31.3 40.5 %copy-start.14 = (bf16[48,2304]{1,0:T(8,128)(2,1)}, bf16[48,2304]{1,0:T(8,128)(2,1)S(1)}, u32[]{:S(2)}) copy-start(bf16[48,2304]{1,0:T(8,128)(2,1)S(1)} %collective-permute-done.2.refs_12_) | copy-start | bytes 663556
  31.4 38.2 %collective-permute-start.6 = (bf16[48,3840]{1,0:T(8,128)(2,1)S(1)}, bf16[48,3840]{1,0:T(8,128)(2,1)S(1)}, u32[]{:S(2)}, u32[]{:S(2)}) collective-permute-start(bf16[48,3840]{1,0:T(8,128)(2,1)S(1)} %pad_maximum_fusion.2), channel_id=1, source_target_pairs={{0,12},{1,13},{2,14},{3,15},{4,8},{5,9},{6,10},{7,11},{8,4},{9,5},... | collective-permute-start | bytes 1105928 | tf_op jit(solution)/shard_map/ppermute | solution.py:408
  31.9 37.7 %collective-permute-start.5 = (bf16[48,3840]{1,0:T(8,128)(2,1)S(1)}, bf16[48,3840]{1,0:T(8,128)(2,1)}, u32[]{:S(2)}, u32[]{:S(2)}) collective-permute-start(bf16[48,3840]{1,0:T(8,128)(2,1)S(1)} %pad_maximum_fusion.2), channel_id=1, source_target_pairs={{0,8},{1,9},{2,10},{3,11},{4,12},{5,13},{6,14},{7,15},{8,0},{9,1},... | collective-permute-start | bytes 1105928 | tf_op jit(solution)/shard_map/ppermute | solution.py:408
  35.4 34.2 %collective-permute-start.4 = (bf16[48,3840]{1,0:T(8,128)(2,1)S(1)}, bf16[48,3840]{1,0:T(8,128)(2,1)}, u32[]{:S(2)}, u32[]{:S(2)}) collective-permute-start(bf16[48,3840]{1,0:T(8,128)(2,1)S(1)} %pad_maximum_fusion.2), channel_id=1, source_target_pairs={{0,4},{1,5},{2,6},{3,7},{4,0},{5,1},{6,2},{7,3},{8,12},{9,13},{10,... | collective-permute-start | bytes 1105928 | tf_op jit(solution)/shard_map/ppermute | solution.py:408
  35.5 8.4 %collective-permute-start.7 = (bf16[48,2304]{1,0:T(8,128)(2,1)S(1)}, bf16[48,2304]{1,0:T(8,128)(2,1)S(1)}, u32[]{:S(2)}, u32[]{:S(2)}) collective-permute-start(bf16[48,2304]{1,0:T(8,128)(2,1)S(1)} %collective-permute-done.refs_4_), channel_id=1, source_target_pairs={{0,2},{1,3},{2,0},{3,1},{4,6},{5,7},{6,4},{7,5},{8,10},{9,11},{10,... | collective-permute-start | bytes 663560 | tf_op jit(solution)/shard_map/ppermute | solution.py:408
  37.5 32.1 %collective-permute-start.8 = (bf16[48,2304]{1,0:T(8,128)(2,1)S(1)}, bf16[48,2304]{1,0:T(8,128)(2,1)S(1)}, u32[]{:S(2)}, u32[]{:S(2)}) collective-permute-start(bf16[48,2304]{1,0:T(8,128)(2,1)S(1)} %collective-permute-done.1.refs_8_), channel_id=1, source_target_pairs={{0,2},{1,3},{2,0},{3,1},{4,6},{5,7},{6,4},{7,5},{8,10},{9,11},{10,... | collective-permute-start | bytes 663560 | tf_op jit(solution)/shard_map/ppermute | solution.py:408
  44.0 25.6 %collective-permute-start.9 = (bf16[48,2304]{1,0:T(8,128)(2,1)S(1)}, bf16[48,2304]{1,0:T(8,128)(2,1)}, u32[]{:S(2)}, u32[]{:S(2)}) collective-permute-start(bf16[48,2304]{1,0:T(8,128)(2,1)S(1)} %collective-permute-done.2.refs_12_), channel_id=1, source_target_pairs={{0,2},{1,3},{2,0},{3,1},{4,6},{5,7},{6,4},{7,5},{8,10},{9,11},{10,... | collective-permute-start | bytes 663560 | tf_op jit(solution)/shard_map/ppermute | solution.py:408
  47.3 19.8 %all-to-all-start.1 = ((bf16[16,2,432]{2,1,0:T(2,128)(2,1)}), bf16[16,2,432]{2,1,0:T(2,128)(2,1)S(1)}, u32[]{:S(2)}, u32[]{:S(2)}) async-start(bf16[16,2,432]{2,1,0:T(2,128)(2,1)} %reshape.176), calls=%async_computation.1 | async-start | bytes 65536 | tf_op jit(solution)/shard_map/all_to_all | solution.py:539
  53.0 175.8 %reduce-scatter.2.cloned.1.call-start = ((), (), s32[]{:S(2)}) async-start(), calls=%async_computation.4 | async-start | bytes 5013504 | tf_op jit(solution)/shard_map/reduce_scatter | solution.py:650
  69.6 2.3 collective-permute-start.10
  71.9 32.2 %collective-permute-start.15 = (bf16[4,48,3840]{2,1,0:T(8,128)(2,1)S(1)}, bf16[4,48,3840]{2,1,0:T(8,128)(2,1)S(1)}, u32[]{:S(2)}, u32[]{:S(2)}) collective-permute-start(bf16[4,48,3840]{2,1,0:T(8,128)(2,1)S(1)} %pad_maximum_fusion.refs_0_), channel_id=1, source_target_pairs={{0,1},{1,0},{2,3},{3,2},{4,5},{5,4},{6,7},{7,6},{8,9},{9,8},{10,11... | collective-permute-start | bytes 4423688 | tf_op jit(solution)/shard_map/ppermute | solution.py:408
  72.5 34.4 %collective-permute-start.14 = (bf16[4,48,3840]{2,1,0:T(8,128)(2,1)S(1)}, bf16[4,48,3840]{2,1,0:T(8,128)(2,1)}, u32[]{:S(2)}, u32[]{:S(2)}) collective-permute-start(bf16[4,48,3840]{2,1,0:T(8,128)(2,1)S(1)} %pad_maximum_fusion.refs_0_), channel_id=1, source_target_pairs={{0,2},{1,3},{2,0},{3,1},{4,6},{5,7},{6,4},{7,5},{8,10},{9,11},{10,... | collective-permute-start | bytes 4423688 | tf_op jit(solution)/shard_map/ppermute | solution.py:408
  72.9 3.1 collective-permute-start.16
  72.9 3.5 %collective-permute-start.18 = (bf16[48,2304]{1,0:T(8,128)(2,1)S(1)}, bf16[48,2304]{1,0:T(8,128)(2,1)S(1)}, u32[]{:S(2)}, u32[]{:S(2)}) collective-permute-start(bf16[48,2304]{1,0:T(8,128)(2,1)S(1)} %copy-done.17), channel_id=1, source_target_pairs={{0,1},{1,0},{2,3},{3,2},{4,5},{5,4},{6,7},{7,6},{8,9},{9,8},{10,11... | collective-permute-start | bytes 663560 | tf_op jit(solution)/shard_map/ppermute | solution.py:408
  73.4 3.3 %collective-permute-start.20 = (bf16[48,2304]{1,0:T(8,128)(2,1)}, bf16[48,2304]{1,0:T(8,128)(2,1)S(1)}, u32[]{:S(2)}, u32[]{:S(2)}) collective-permute-start(bf16[48,2304]{1,0:T(8,128)(2,1)} %copy-done.15), channel_id=1, source_target_pairs={{0,1},{1,0},{2,3},{3,2},{4,5},{5,4},{6,7},{7,6},{8,9},{9,8},{10,11... | collective-permute-start | bytes 663560 | tf_op jit(solution)/shard_map/ppermute | solution.py:408
  76.0 1.7 collective-permute-start.22
  76.4 1.7 collective-permute-start.17
  76.7 1.7 collective-permute-start.19
  77.7 4.1 %collective-permute-start.21 = (bf16[48,2304]{1,0:T(8,128)(2,1)S(1)}, bf16[48,2304]{1,0:T(8,128)(2,1)S(1)}, u32[]{:S(2)}, u32[]{:S(2)}) collective-permute-start(bf16[48,2304]{1,0:T(8,128)(2,1)S(1)} %copy-done.20), channel_id=1, source_target_pairs={{0,1},{1,0},{2,3},{3,2},{4,5},{5,4},{6,7},{7,6},{8,9},{9,8},{10,11... | collective-permute-start | bytes 663560 | tf_op jit(solution)/shard_map/ppermute | solution.py:408
  78.1 22.6 %collective-permute-start.13 = (bf16[192,768]{1,0:T(8,128)(2,1)S(1)}, bf16[192,768]{1,0:T(8,128)(2,1)}, u32[]{:S(2)}, u32[]{:S(2)}) collective-permute-start(bf16[192,768]{1,0:T(8,128)(2,1)S(1)} %convert_element_type.231), channel_id=1, source_target_pairs={{0,12},{1,13},{2,14},{3,15},{4,8},{5,9},{6,10},{7,11},{8,4},{9,5},... | collective-permute-start | bytes 884744 | tf_op jit(solution)/shard_map/ppermute | solution.py:408
  78.4 25.7 %collective-permute-start.12 = (bf16[192,768]{1,0:T(8,128)(2,1)S(1)}, bf16[192,768]{1,0:T(8,128)(2,1)}, u32[]{:S(2)}, u32[]{:S(2)}) collective-permute-start(bf16[192,768]{1,0:T(8,128)(2,1)S(1)} %convert_element_type.231), channel_id=1, source_target_pairs={{0,8},{1,9},{2,10},{3,11},{4,12},{5,13},{6,14},{7,15},{8,0},{9,1},... | collective-permute-start | bytes 884744 | tf_op jit(solution)/shard_map/ppermute | solution.py:408
  81.8 22.3 %collective-permute-start.11 = (bf16[192,768]{1,0:T(8,128)(2,1)S(1)}, bf16[192,768]{1,0:T(8,128)(2,1)}, u32[]{:S(2)}, u32[]{:S(2)}) collective-permute-start(bf16[192,768]{1,0:T(8,128)(2,1)S(1)} %convert_element_type.231), channel_id=1, source_target_pairs={{0,4},{1,5},{2,6},{3,7},{4,0},{5,1},{6,2},{7,3},{8,12},{9,13},{10,... | collective-permute-start | bytes 884744 | tf_op jit(solution)/shard_map/ppermute | solution.py:408
  106.9 3.5 %collective-permute-start.23 = (bf16[4,48,3840]{2,1,0:T(8,128)(2,1)}, bf16[4,48,3840]{2,1,0:T(8,128)(2,1)S(1)}, u32[]{:S(2)}, u32[]{:S(2)}) collective-permute-start(bf16[4,48,3840]{2,1,0:T(8,128)(2,1)} %collective-permute-done.14.refs_1_), channel_id=1, source_target_pairs={{0,1},{1,0},{2,3},{3,2},{4,5},{5,4},{6,7},{7,6},{8,9},{9,8},{10,11... | collective-permute-start | bytes 4423688 | tf_op jit(solution)/shard_map/ppermute | solution.py:408
  110.3 28.4 %collective-permute-start.24 = (bf16[4,192,768]{2,1,0:T(8,128)(2,1)S(1)}, bf16[4,192,768]{2,1,0:T(8,128)(2,1)}, u32[]{:S(2)}, u32[]{:S(2)}) collective-permute-start(bf16[4,192,768]{2,1,0:T(8,128)(2,1)S(1)} %pad_maximum_fusion.1.refs_4_.refs_0_), channel_id=1, source_target_pairs={{0,2},{1,3},{2,0},{3,1},{4,6},{5,7},{6,4},{7,5},{8,10},{9,11},{10,... | collective-permute-start | bytes 3538952 | tf_op jit(solution)/shard_map/ppermute | solution.py:408
  138.6 3.2 collective-permute-start.25
  138.8 4.6 %collective-permute-start.26 = (bf16[4,192,768]{2,1,0:T(8,128)(2,1)}, bf16[4,192,768]{2,1,0:T(8,128)(2,1)S(1)}, u32[]{:S(2)}, u32[]{:S(2)}) collective-permute-start(bf16[4,192,768]{2,1,0:T(8,128)(2,1)} %collective-permute-done.24.refs_5_.refs_1_), channel_id=1, source_target_pairs={{0,1},{1,0},{2,3},{3,2},{4,5},{5,4},{6,7},{7,6},{8,9},{9,8},{10,11... | collective-permute-start | bytes 3538952 | tf_op jit(solution)/shard_map/ppermute | solution.py:408
  181.1 5.6 %collective-permute-start.27 = (bf16[8,48,3840]{2,1,0:T(8,128)(2,1)}, bf16[8,48,3840]{2,1,0:T(8,128)(2,1)S(1)}, u32[]{:S(2)}, u32[]{:S(2)}) collective-permute-start(bf16[8,48,3840]{2,1,0:T(8,128)(2,1)} %get-tuple-element.179), channel_id=1, source_target_pairs={{0,1},{1,0},{2,3},{3,2},{4,5},{5,4},{6,7},{7,6},{8,9},{9,8},{10,11... | collective-permute-start | bytes 8847368 | tf_op jit(solution)/shard_map/ppermute | solution.py:408
  191.0 37.8 %collective-permute-start.28 = (bf16[4,48,3840]{2,1,0:T(8,128)(2,1)}, bf16[4,48,3840]{2,1,0:T(8,128)(2,1)}, u32[]{:S(2)}, u32[]{:S(2)}) collective-permute-start(bf16[4,48,3840]{2,1,0:T(8,128)(2,1)} %get-tuple-element.184), channel_id=1, source_target_pairs={{0,2},{1,3},{2,0},{3,1},{4,6},{5,7},{6,4},{7,5},{8,10},{9,11},{10,... | collective-permute-start | bytes 4423688 | tf_op jit(solution)/shard_map/ppermute | solution.py:408
  209.9 22.0 %collective-permute-start.29 = (bf16[8,48,2304]{2,1,0:T(8,128)(2,1)S(1)}, bf16[8,48,2304]{2,1,0:T(8,128)(2,1)}, u32[]{:S(2)}, u32[]{:S(2)}) collective-permute-start(bf16[8,48,2304]{2,1,0:T(8,128)(2,1)S(1)} %get-tuple-element.201), channel_id=1, source_target_pairs={{0,1},{1,0},{2,3},{3,2},{4,5},{5,4},{6,7},{7,6},{8,9},{9,8},{10,11... | collective-permute-start | bytes 5308424 | tf_op jit(solution)/shard_map/ppermute | solution.py:408
  233.8 42.3 %collective-permute-start.33 = (bf16[4,48,2304]{2,1,0:T(8,128)(2,1)S(1)}, bf16[4,48,2304]{2,1,0:T(8,128)(2,1)S(1)}, u32[]{:S(2)}, u32[]{:S(2)}) collective-permute-start(bf16[4,48,2304]{2,1,0:T(8,128)(2,1)S(1)} %get-tuple-element.210), channel_id=1, source_target_pairs={{0,2},{1,3},{2,0},{3,1},{4,6},{5,7},{6,4},{7,5},{8,10},{9,11},{10,... | collective-permute-start | bytes 2654216 | tf_op jit(solution)/shard_map/ppermute | solution.py:408
  237.0 39.0 %collective-permute-start.30 = (bf16[48,3840]{1,0:T(8,128)(2,1)}, bf16[48,3840]{1,0:T(8,128)(2,1)}, u32[]{:S(2)}, u32[]{:S(2)}) collective-permute-start(bf16[48,3840]{1,0:T(8,128)(2,1)} %get-tuple-element.205), channel_id=1, source_target_pairs={{0,4},{1,5},{2,6},{3,7},{4,0},{5,1},{6,2},{7,3},{8,12},{9,13},{10,... | collective-permute-start | bytes 1105928 | tf_op jit(solution)/shard_map/ppermute | solution.py:408
  238.3 37.8 %collective-permute-start.31 = (bf16[48,3840]{1,0:T(8,128)(2,1)}, bf16[48,3840]{1,0:T(8,128)(2,1)}, u32[]{:S(2)}, u32[]{:S(2)}) collective-permute-start(bf16[48,3840]{1,0:T(8,128)(2,1)} %get-tuple-element.206), channel_id=1, source_target_pairs={{0,8},{1,9},{2,10},{3,11},{4,12},{5,13},{6,14},{7,15},{8,0},{9,1},... | collective-permute-start | bytes 1105928 | tf_op jit(solution)/shard_map/ppermute | solution.py:408
  238.8 37.3 %collective-permute-start.32 = (bf16[48,3840]{1,0:T(8,128)(2,1)}, bf16[48,3840]{1,0:T(8,128)(2,1)}, u32[]{:S(2)}, u32[]{:S(2)}) collective-permute-start(bf16[48,3840]{1,0:T(8,128)(2,1)} %get-tuple-element.207), channel_id=1, source_target_pairs={{0,12},{1,13},{2,14},{3,15},{4,8},{5,9},{6,10},{7,11},{8,4},{9,5},... | collective-permute-start | bytes 1105928 | tf_op jit(solution)/shard_map/ppermute | solution.py:408
  242.4 33.6 %all-to-all-start.2 = ((f32[32,1,870]{2,1,0:T(1,128)}), f32[32,1,870]{2,1,0:T(1,128)S(1)}, u32[]{:S(2)}, u32[]{:S(2)}) async-start(f32[32,1,870]{2,1,0:T(1,128)} %copy.58), calls=%async_computation.3 | async-start | bytes 229376 | tf_op jit(solution)/shard_map/all_to_all | solution.py:774
  278.7 24.4 %collective-permute-start.38 = (bf16[48,3840]{1,0:T(8,128)(2,1)S(1)}, bf16[48,3840]{1,0:T(8,128)(2,1)S(1)}, u32[]{:S(2)}, u32[]{:S(2)}) collective-permute-start(bf16[48,3840]{1,0:T(8,128)(2,1)S(1)} %add_convert_fusion.4), channel_id=1, source_target_pairs={{0,16},{16,0},{1,17},{17,1},{2,18},{18,2},{3,19},{19,3},{4,20},{20... | collective-permute-start | bytes 1105928 | tf_op jit(solution)/shard_map/ppermute | solution.py:412
  280.4 9.6 %collective-permute-start.34 = (bf16[48,2304]{1,0:T(8,128)(2,1)}, bf16[48,2304]{1,0:T(8,128)(2,1)S(1)}, u32[]{:S(2)}, u32[]{:S(2)}) collective-permute-start(bf16[48,2304]{1,0:T(8,128)(2,1)} %get-tuple-element.240), channel_id=1, source_target_pairs={{0,4},{1,5},{2,6},{3,7},{4,0},{5,1},{6,2},{7,3},{8,12},{9,13},{10,... | collective-permute-start | bytes 663560 | tf_op jit(solution)/shard_map/ppermute | solution.py:408
  281.7 16.1 %collective-permute-start.35 = (bf16[48,2304]{1,0:T(8,128)(2,1)S(1)}, bf16[48,2304]{1,0:T(8,128)(2,1)S(1)}, u32[]{:S(2)}, u32[]{:S(2)}) collective-permute-start(bf16[48,2304]{1,0:T(8,128)(2,1)S(1)} %get-tuple-element.241), channel_id=1, source_target_pairs={{0,8},{1,9},{2,10},{3,11},{4,12},{5,13},{6,14},{7,15},{8,0},{9,1},... | collective-permute-start | bytes 663560 | tf_op jit(solution)/shard_map/ppermute | solution.py:408
  282.3 20.8 %collective-permute-start.36 = (bf16[48,2304]{1,0:T(8,128)(2,1)S(1)}, bf16[48,2304]{1,0:T(8,128)(2,1)S(1)}, u32[]{:S(2)}, u32[]{:S(2)}) collective-permute-start(bf16[48,2304]{1,0:T(8,128)(2,1)S(1)} %get-tuple-element.242), channel_id=1, source_target_pairs={{0,12},{1,13},{2,14},{3,15},{4,8},{5,9},{6,10},{7,11},{8,4},{9,5},... | collective-permute-start | bytes 663560 | tf_op jit(solution)/shard_map/ppermute | solution.py:408
  284.0 19.1 %collective-permute-start.37 = (bf16[192,768]{1,0:T(8,128)(2,1)S(1)}, bf16[192,768]{1,0:T(8,128)(2,1)S(1)}, u32[]{:S(2)}, u32[]{:S(2)}) collective-permute-start(bf16[192,768]{1,0:T(8,128)(2,1)S(1)} %copy-done.31), channel_id=1, source_target_pairs={{0,16},{16,0},{1,17},{17,1},{2,18},{18,2},{3,19},{19,3},{4,20},{20... | collective-permute-start | bytes 884744 | tf_op jit(solution)/shard_map/ppermute | solution.py:412
  304.9 6.0 %collective-permute-start.39 = (bf16[48,2304]{1,0:T(8,128)(2,1)S(1)}, bf16[48,2304]{1,0:T(8,128)(2,1)S(1)}, u32[]{:S(2)}, u32[]{:S(2)}) collective-permute-start(bf16[48,2304]{1,0:T(8,128)(2,1)S(1)} %add_convert_fusion.9), channel_id=1, source_target_pairs={{0,16},{16,0},{1,17},{17,1},{2,18},{18,2},{3,19},{19,3},{4,20},{20... | collective-permute-start | bytes 663560 | tf_op jit(solution)/shard_map/ppermute | solution.py:412
  (41 other events, 517.2 us)
Sparse Core Ops, SparseCore 0:
  138.7 77.3 reduce-scatter.1
